TPU v7x, 32 devices: a whole 2x2x4 slice. The times are simulated.
32 devices in a mesh: dp: 16 (over z, y, core), tensor: 2 (over x).
Axes of the slice: x: 2, y: 2, z: 4, core: 2. Of those that a mesh axis runs over, the one named last changes fastest.
Arguments:
- video_in: bfloat16 [32, 256, 1152], P('dp', 'tensor'), may hold values from -15 to 15
- condition: float32 [2, 1152], replicated, may hold values from -5 to 5
- adaln_spatial: bfloat16 [1152, 6, 1152], P('dp'), may hold values from -0.1875 to 0.1875
- qkv_spatial: bfloat16 [1152, 3, 1152], P('dp', None, 'tensor'), may hold values from -0.1875 to 0.1875
- proj_spatial: bfloat16 [1152, 1152], P('tensor', 'dp'), may hold values from -1.5 to 1.5
- up_spatial: bfloat16 [1152, 4608], P('dp', 'tensor'), may hold values from -0.1875 to 0.1875
- down_spatial: bfloat16 [4608, 1152], P('tensor', 'dp'), may hold values from -0.09375 to 0.09375
- adaln_temporal: bfloat16 [1152, 6, 1152], P('dp'), may hold values from -0.1875 to 0.1875
- qkv_temporal: bfloat16 [1152, 3, 1152], P('dp', None, 'tensor'), may hold values from -0.1875 to 0.1875
- proj_temporal: bfloat16 [1152, 1152], P('tensor', 'dp'), may hold values from -0.5 to 0.5
- up_temporal: bfloat16 [1152, 4608], P('dp', 'tensor'), may hold values from -0.1875 to 0.1875
- down_temporal: bfloat16 [4608, 1152], P('tensor', 'dp'), may hold values from -0.09375 to 0.09375
- grad_output: float32 [32, 256, 1152], P('dp', 'tensor'), may hold values from -6 to 6
Outputs:
- video_out: bfloat16 [32, 256, 1152], P('dp', 'tensor')
- video_grad: float32 [32, 256, 1152], P('dp', 'tensor')
- condition_grad: float32 [2, 1152], P(None, 'dp')
- adaln_spatial_grad: float32 [1152, 6, 1152], P('dp')
- qkv_spatial_grad: float32 [1152, 3, 1152], P('dp', None, 'tensor')
- proj_spatial_grad: float32 [1152, 1152], P('tensor', 'dp')
- up_spatial_grad: float32 [1152, 4608], P('dp', 'tensor')
- down_spatial_grad: float32 [4608, 1152], P('tensor', 'dp')
- adaln_temporal_grad: float32 [1152, 6, 1152], P('dp')
- qkv_temporal_grad: float32 [1152, 3, 1152], P('dp', None, 'tensor')
- proj_temporal_grad: float32 [1152, 1152], P('tensor', 'dp')
- up_temporal_grad: float32 [1152, 4608], P('dp', 'tensor')
- down_temporal_grad: float32 [4608, 1152], P('tensor', 'dp')
- frame_rms: float32 [8, 16], replicated
- shift_grad: float32 [4, 2, 1152], replicated
All inputs are finite; a program needn't handle non-finite values.
Results may differ from a plain program's by a relative error of at most 0.024.
Values may be sent and summed in bfloat16 or wider, within the bound.
A program may use at most 256 MiB of HBM per device.

v0:
```python
import jax
import jax.numpy as jnp
from jax import lax
from jax.sharding import PartitionSpec as P

HEAD_DIM = 72
PATCHES = 256
FRAMES = 16


highest = lax.Precision.HIGHEST
epsilon = 1e-06
spatial_forms = ("aqhe,akhe->ahqk", "ahqk,akhe->aqhe", "ahqk,aqhe->akhe")
temporal_forms = ("fshe,gshe->shfg", "shfg,gshe->fshe", "shfg,fshe->gshe")


def layer_norm(stream):
    average = jnp.mean(stream, axis=-1, keepdims=True)
    centered = stream - average
    inverse = lax.rsqrt(jnp.mean(centered * centered, axis=-1, keepdims=True) + epsilon)
    return (centered * inverse, inverse)


def modulated(stream, modrow, offset):
    normed = layer_norm(stream)[0]
    shifted = normed * (1.0 + modrow[:, offset + 1][:, None, :]) + modrow[:, offset][:, None, :]
    return shifted.astype(jnp.bfloat16)


def gelu_tanh(pre_act):
    return jax.nn.gelu(pre_act, approximate=True)


def gather_rows(hidden_local):
    return lax.all_gather(hidden_local, "tensor", axis=1, tiled=True)


def reduce_rows(partial_value):
    return lax.psum_scatter(
        partial_value.astype(jnp.bfloat16), "tensor", scatter_dimension=1, tiled=True
    ).astype(jnp.float32)


def gather_grads(grad_branch):
    return lax.all_gather(grad_branch, "tensor", axis=1, tiled=True)


def reduce_back(partial_value):
    return lax.psum_scatter(
        partial_value.astype(jnp.bfloat16), "tensor", scatter_dimension=1, tiled=True
    ).astype(jnp.float32)


def gather_attention(qkv_shard, proj_shard):
    return (
        lax.all_gather(qkv_shard, "dp", axis=0, tiled=True),
        lax.all_gather(proj_shard, "dp", axis=1, tiled=True),
    )


def gather_mlp(up_shard, down_shard):
    return (
        lax.all_gather(up_shard, "dp", axis=0, tiled=True),
        lax.all_gather(down_shard, "dp", axis=1, tiled=True),
    )


def to_places(stream):
    return lax.all_to_all(
        stream.astype(jnp.bfloat16), "dp", split_axis=1, concat_axis=0, tiled=True
    ).astype(stream.dtype)


def to_frames(stream):
    return lax.all_to_all(
        stream.astype(jnp.bfloat16), "dp", split_axis=0, concat_axis=1, tiled=True
    ).astype(stream.dtype)


def row_tables(row_ids, clip_count):
    clip_table = (
        row_ids[:, None] % clip_count == jnp.arange(clip_count, dtype=jnp.int32)[None, :]
    ).astype(jnp.float32)
    frame_table = (
        row_ids[:, None] // clip_count == jnp.arange(FRAMES, dtype=jnp.int32)[None, :]
    ).astype(jnp.float32)
    return (clip_table, frame_table)


def frame_squares(entries, frame_table):
    per_row = jnp.sum(entries * entries, axis=(1, 2))
    return jnp.dot(per_row, frame_table, precision=highest)


def split_heads(qkv_vals, lead_dim):
    head_count = qkv_vals.shape[-1] // HEAD_DIM
    head_view = qkv_vals.reshape((lead_dim, -1, 3, head_count, HEAD_DIM))
    return (head_view[:, :, 0], head_view[:, :, 1], head_view[:, :, 2])


def attend(qkv_vals, lead_dim, einsum_forms):
    queries, key_rows, values = split_heads(qkv_vals, lead_dim)
    scores = jnp.einsum(
        einsum_forms[0], queries, key_rows, preferred_element_type=jnp.float32
    ) * HEAD_DIM ** (-0.5)
    highest_score = jnp.max(scores, axis=-1, keepdims=True)
    unnormed = jnp.exp(scores - highest_score)
    denominator = jnp.sum(unnormed, axis=-1, keepdims=True)
    attn_probs = (unnormed / denominator).astype(jnp.bfloat16)
    attended = jnp.einsum(einsum_forms[1], attn_probs, values, preferred_element_type=jnp.float32)
    attended = attended.astype(jnp.bfloat16).reshape(qkv_vals.shape[0], qkv_vals.shape[1], -1)
    return (attended, highest_score + jnp.log(denominator))


def attend_back(qkv_vals, log_total, grad_attended, lead_dim, einsum_forms):
    queries, key_rows, values = split_heads(qkv_vals, lead_dim)
    scale_factor = HEAD_DIM ** (-0.5)
    scores = (
        jnp.einsum(einsum_forms[0], queries, key_rows, preferred_element_type=jnp.float32)
        * scale_factor
    )
    attn_probs = jnp.exp(scores - log_total)
    grad_view = grad_attended.reshape(queries.shape)
    grad_probs = jnp.einsum(einsum_forms[0], grad_view, values, preferred_element_type=jnp.float32)
    grad_scores = attn_probs * (
        grad_probs - jnp.sum(attn_probs * grad_probs, axis=-1, keepdims=True)
    )
    grad_scaled = (grad_scores * scale_factor).astype(jnp.bfloat16)
    grad_queries = jnp.einsum(
        einsum_forms[1], grad_scaled, key_rows, preferred_element_type=jnp.float32
    )
    grad_keys = jnp.einsum(
        einsum_forms[2], grad_scaled, queries, preferred_element_type=jnp.float32
    )
    grad_values = jnp.einsum(
        einsum_forms[2],
        attn_probs.astype(jnp.bfloat16),
        grad_view,
        preferred_element_type=jnp.float32,
    )
    stacked = jnp.stack([grad_queries, grad_keys, grad_values], axis=2)
    return stacked.reshape(qkv_vals.shape).astype(jnp.bfloat16)


def attention_forward(stream, modrow, shards, lead_dim, einsum_forms):
    gathered = gather_rows(modulated(stream, modrow, 0))
    weights = gather_attention(shards[0], shards[1])
    qkv_vals = jnp.einsum(
        "abd,dkh->abkh", gathered, weights[0], preferred_element_type=jnp.float32
    ).astype(jnp.bfloat16)
    attended, log_total = attend(qkv_vals, lead_dim, einsum_forms)
    branch = reduce_rows(
        jnp.einsum("abh,hd->abd", attended, weights[1], preferred_element_type=jnp.float32)
    )
    gated_out = modrow[:, 2][:, None, :] * branch
    stored = (stream, branch, attended, log_total, gathered, qkv_vals, weights)
    return (stream + gated_out, gated_out, stored)


def mlp_forward(stream, modrow, shards):
    gathered = gather_rows(modulated(stream, modrow, 3))
    weights = gather_mlp(shards[0], shards[1])
    up_values = jnp.einsum("abd,dh->abh", gathered, weights[0], preferred_element_type=jnp.float32)
    active = gelu_tanh(up_values).astype(jnp.bfloat16)
    branch = reduce_rows(
        jnp.einsum("abh,hd->abd", active, weights[1], preferred_element_type=jnp.float32)
    )
    gated_out = modrow[:, 5][:, None, :] * branch
    stored = (stream, branch, gathered, up_values, active, weights)
    return (stream + gated_out, gated_out, stored)


def branch_back(grad_stream, modrow, offset, branch):
    grad_branch = (grad_stream * modrow[:, offset + 2][:, None, :]).astype(jnp.bfloat16)
    grad_gate = jnp.sum(grad_stream * branch, axis=1)
    return (gather_grads(grad_branch), grad_gate)


def norm_back(grad_stream, grad_hidden, stream, modrow, offset):
    normed, inverse = layer_norm(stream)
    grad_normed = grad_hidden * (1.0 + modrow[:, offset + 1][:, None, :])
    centered_grad = grad_normed - jnp.mean(grad_normed, axis=-1, keepdims=True)
    grad_input = inverse * (
        centered_grad - normed * jnp.mean(grad_normed * normed, axis=-1, keepdims=True)
    )
    grad_shift = jnp.sum(grad_hidden, axis=1)
    grad_scale = jnp.sum(grad_hidden * normed, axis=1)
    return (grad_stream + grad_input, grad_shift, grad_scale)


def attention_back(grad_stream, modrow, stored, lead_dim, einsum_forms):
    stream, branch, attended, log_total = (stored[0], stored[1], stored[2], stored[3])
    gathered, qkv_vals, weights = (stored[4], stored[5], stored[6])
    grad_gathered, grad_gate = branch_back(grad_stream, modrow, 0, branch)
    grad_attended = jnp.einsum(
        "abd,hd->abh", grad_gathered, weights[1], preferred_element_type=jnp.float32
    ).astype(jnp.bfloat16)
    grad_proj = jnp.einsum(
        "abh,abd->hd", attended, grad_gathered, preferred_element_type=jnp.float32
    )
    grad_qkv = attend_back(qkv_vals, log_total, grad_attended, lead_dim, einsum_forms)
    grad_qkv_w = jnp.einsum("abd,abkh->dkh", gathered, grad_qkv, preferred_element_type=jnp.float32)
    grad_hidden = reduce_back(
        jnp.einsum("abkh,dkh->abd", grad_qkv, weights[0], preferred_element_type=jnp.float32)
    )
    weight_grads = (
        lax.psum_scatter(
            grad_qkv_w.astype(jnp.bfloat16), "dp", scatter_dimension=0, tiled=True
        ).astype(jnp.float32),
        lax.psum_scatter(
            grad_proj.astype(jnp.bfloat16), "dp", scatter_dimension=1, tiled=True
        ).astype(jnp.float32),
    )
    grad_stream, grad_shift, grad_scale = norm_back(grad_stream, grad_hidden, stream, modrow, 0)
    return (grad_stream, jnp.stack([grad_shift, grad_scale, grad_gate], axis=1), weight_grads)


def mlp_back(grad_stream, modrow, stored):
    stream, branch = (stored[0], stored[1])
    gathered, up_values, active, weights = (stored[2], stored[3], stored[4], stored[5])
    grad_gathered, grad_gate = branch_back(grad_stream, modrow, 3, branch)
    grad_active = jnp.einsum(
        "abd,hd->abh", grad_gathered, weights[1], preferred_element_type=jnp.float32
    )
    grad_down = jnp.einsum("abh,abd->hd", active, grad_gathered, preferred_element_type=jnp.float32)
    grad_upped = jax.vjp(gelu_tanh, up_values)[1](grad_active)[0].astype(jnp.bfloat16)
    grad_up = jnp.einsum("abd,abh->dh", gathered, grad_upped, preferred_element_type=jnp.float32)
    grad_hidden = reduce_back(
        jnp.einsum("abh,dh->abd", grad_upped, weights[0], preferred_element_type=jnp.float32)
    )
    weight_grads = (
        lax.psum_scatter(
            grad_up.astype(jnp.bfloat16), "dp", scatter_dimension=0, tiled=True
        ).astype(jnp.float32),
        lax.psum_scatter(
            grad_down.astype(jnp.bfloat16), "dp", scatter_dimension=1, tiled=True
        ).astype(jnp.float32),
    )
    grad_stream, grad_shift, grad_scale = norm_back(grad_stream, grad_hidden, stream, modrow, 3)
    return (grad_stream, jnp.stack([grad_shift, grad_scale, grad_gate], axis=1), weight_grads)


def modulations(condition, adaln_spatial, adaln_temporal):
    silu_low = jax.nn.silu(condition).astype(jnp.bfloat16)
    model_width = condition.shape[1]
    full_spatial, full_temporal = (
        lax.all_gather(adaln_spatial, "dp", axis=0, tiled=True),
        lax.all_gather(adaln_temporal, "dp", axis=0, tiled=True),
    )
    mod_spatial = jnp.dot(
        silu_low, full_spatial.reshape(model_width, -1), preferred_element_type=jnp.float32
    )
    mod_temporal = jnp.dot(
        silu_low, full_temporal.reshape(model_width, -1), preferred_element_type=jnp.float32
    )
    return (mod_spatial, mod_temporal)


def body(
    video_in,
    condition,
    adaln_spatial,
    qkv_spatial,
    proj_spatial,
    up_spatial,
    down_spatial,
    adaln_temporal,
    qkv_temporal,
    proj_temporal,
    up_temporal,
    down_temporal,
    grad_output,
):
    local_rows = video_in.shape[0]
    model_width = video_in.shape[2]
    clip_count = condition.shape[0]
    all_rows = local_rows * lax.axis_size("dp")
    spatial_ids = lax.axis_index("dp") * local_rows + jnp.arange(local_rows, dtype=jnp.int32)
    temporal_ids = jnp.arange(all_rows, dtype=jnp.int32)
    clip_spatial, frame_spatial = row_tables(spatial_ids, clip_count)
    clip_temporal, frame_temporal = row_tables(temporal_ids, clip_count)
    mod_spatial, mod_temporal = modulations(condition, adaln_spatial, adaln_temporal)
    rows_spatial = jnp.dot(clip_spatial, mod_spatial, precision=highest).reshape(
        local_rows, 6, model_width
    )
    rows_temporal = jnp.dot(clip_temporal, mod_temporal, precision=highest).reshape(
        all_rows, 6, model_width
    )
    stream = video_in.astype(jnp.float32)
    stream_one, gated_one, stored_one = attention_forward(
        stream, rows_spatial, (qkv_spatial, proj_spatial), local_rows, spatial_forms
    )
    stream_two, gated_two, stored_two = mlp_forward(
        stream_one, rows_spatial, (up_spatial, down_spatial)
    )
    placed = to_places(stream_two)
    stream_three, gated_three, stored_three = attention_forward(
        placed, rows_temporal, (qkv_temporal, proj_temporal), FRAMES, temporal_forms
    )
    stream_four, gated_four, stored_four = mlp_forward(
        stream_three, rows_temporal, (up_temporal, down_temporal)
    )
    video_out = to_frames(stream_four).astype(jnp.bfloat16)
    squares = jnp.stack(
        [
            frame_squares(stream_one, frame_spatial),
            frame_squares(stream_two, frame_spatial),
            frame_squares(stream_three, frame_temporal),
            frame_squares(stream_four, frame_temporal),
            frame_squares(gated_one, frame_spatial),
            frame_squares(gated_two, frame_spatial),
            frame_squares(gated_three, frame_temporal),
            frame_squares(gated_four, frame_temporal),
        ]
    )
    grad_placed = to_places(grad_output)
    grad_placed, mod_four, mlp_grads_two = mlp_back(grad_placed, rows_temporal, stored_four)
    grad_placed, mod_three, attn_grads_two = attention_back(
        grad_placed, rows_temporal, stored_three, FRAMES, temporal_forms
    )
    grad_stream = to_frames(grad_placed)
    grad_stream, mod_two, mlp_grads_one = mlp_back(grad_stream, rows_spatial, stored_two)
    grad_stream, mod_one, attn_grads_one = attention_back(
        grad_stream, rows_spatial, stored_one, local_rows, spatial_forms
    )
    grad_rows_spatial = jnp.concatenate([mod_one, mod_two], axis=1).reshape(local_rows, -1)
    grad_rows_temporal = jnp.concatenate([mod_three, mod_four], axis=1).reshape(all_rows, -1)
    grad_mod_spatial = jnp.dot(clip_spatial.T, grad_rows_spatial, precision=highest)
    grad_mod_temporal = jnp.dot(clip_temporal.T, grad_rows_temporal, precision=highest)
    grad_mod_spatial, grad_mod_temporal, totals = lax.psum(
        (grad_mod_spatial, grad_mod_temporal, squares), ("dp", "tensor")
    )
    frame_rms = jnp.sqrt(totals / (clip_count * PATCHES * model_width))
    groups_spatial = grad_mod_spatial.reshape(clip_count, 6, model_width)
    groups_temporal = grad_mod_temporal.reshape(clip_count, 6, model_width)
    shift_grad = jnp.stack(
        [groups_spatial[:, 0], groups_spatial[:, 3], groups_temporal[:, 0], groups_temporal[:, 3]]
    )
    row_share = adaln_spatial.shape[0]
    cond_rows = lax.dynamic_slice_in_dim(condition, lax.axis_index("dp") * row_share, row_share, 1)
    silu_rows, silu_pull = jax.vjp(jax.nn.silu, cond_rows)
    silu_low = silu_rows.astype(jnp.bfloat16).astype(jnp.float32)
    adaln_spatial_grad = jnp.dot(silu_low.T, grad_mod_spatial, precision=highest).reshape(
        adaln_spatial.shape
    )
    adaln_temporal_grad = jnp.dot(silu_low.T, grad_mod_temporal, precision=highest).reshape(
        adaln_temporal.shape
    )
    back_spatial = jnp.dot(
        grad_mod_spatial,
        adaln_spatial.reshape(row_share, -1).astype(jnp.float32).T,
        precision=highest,
    )
    back_temporal = jnp.dot(
        grad_mod_temporal,
        adaln_temporal.reshape(row_share, -1).astype(jnp.float32).T,
        precision=highest,
    )
    condition_grad = silu_pull(back_spatial + back_temporal)[0]
    return (
        video_out,
        grad_stream,
        condition_grad,
        adaln_spatial_grad,
        attn_grads_one[0],
        attn_grads_one[1],
        mlp_grads_one[0],
        mlp_grads_one[1],
        adaln_temporal_grad,
        attn_grads_two[0],
        attn_grads_two[1],
        mlp_grads_two[0],
        mlp_grads_two[1],
        frame_rms,
        shift_grad,
    )


def solution(mesh):
    return jax.shard_map(
        body,
        mesh=mesh,
        in_specs=(
            P("dp", "tensor", None),
            P(),
            P("dp", None, None),
            P("dp", None, "tensor"),
            P("tensor", "dp"),
            P("dp", "tensor"),
            P("tensor", "dp"),
            P("dp", None, None),
            P("dp", None, "tensor"),
            P("tensor", "dp"),
            P("dp", "tensor"),
            P("tensor", "dp"),
            P("dp", "tensor", None),
        ),
        out_specs=(
            P("dp", "tensor", None),
            P("dp", "tensor", None),
            P(None, "dp"),
            P("dp", None, None),
            P("dp", None, "tensor"),
            P("tensor", "dp"),
            P("dp", "tensor"),
            P("tensor", "dp"),
            P("dp", None, None),
            P("dp", None, "tensor"),
            P("tensor", "dp"),
            P("dp", "tensor"),
            P("tensor", "dp"),
            P(),
            P(),
        ),
        check_vma=False,
    )
```

profile of v0, /device:TPU:0, one launch (start us, length us, event | category | flops | bytes accessed | tf_op | source)
XLA Modules:
  0.0 1975.5 jit_solution(10076505963828110319)
XLA Ops:
  10.3 124.2 %all-gather.19.cloned.1.call-done = bf16[1152,6,1152]{2,0,1:T(8,128)(2,1)} async-done(((bf16[72,6,1152]{2,0,1:T(8,128)(2,1)}), bf16[1152,6,1152]{2,0,1:T(8,128)(2,1)}) %all-gather.19.cloned.1.call-update) | async-done | bytes 15925264 | tf_op jit(solution)/shard_map/all_gather | solution.py:247
  134.5 22.4 %copy.118 = bf16[1152,6,1152]{0,2,1:T(8,128)(2,1)} copy(bf16[1152,6,1152]{2,0,1:T(8,128)(2,1)} %all-gather.19.cloned.1.call-done) | data formatting | bytes 31850496 | tf_op jit(solution)/shard_map/all_gather | solution.py:247
  186.6 23.4 %all-gather.21.cloned.1.call-done = bf16[2,256,1152]{2,1,0:T(8,128)(2,1)} async-done(((bf16[2,128,1152]{2,1,0:T(8,128)(2,1)}), bf16[2,256,1152]{2,1,0:T(8,128)(2,1)}) %all-gather.21.cloned.1.call-update) | async-done | bytes 1179664 | tf_op jit(solution)/shard_map/all_gather | solution.py:35
  219.6 31.9 %all-gather.25.cloned.1.call-done = bf16[576,1152]{0,1:T(8,128)(2,1)} async-done(((bf16[576,72]{0,1:T(8,128)(2,1)}), bf16[576,1152]{0,1:T(8,128)(2,1)}) %all-gather.25.cloned.1.call-update) | async-done | bytes 1327120 | tf_op jit(solution)/shard_map/all_gather | solution.py:57
  281.7 52.8 %all-gather.29.cloned.1.call-done = bf16[1152,2304]{1,0:T(8,128)(2,1)} async-done(((bf16[72,2304]{1,0:T(8,128)(2,1)}), bf16[1152,2304]{1,0:T(8,128)(2,1)}) %all-gather.29.cloned.1.call-update) | async-done | bytes 5308432 | tf_op jit(solution)/shard_map/all_gather | solution.py:63
  334.5 23.6 %all-gather.27.cloned.1.call-done = bf16[2,256,1152]{2,1,0:T(8,128)(2,1)} async-done(((bf16[2,128,1152]{2,1,0:T(8,128)(2,1)}), bf16[2,256,1152]{2,1,0:T(8,128)(2,1)}) %all-gather.27.cloned.1.call-update) | async-done | bytes 1179664 | tf_op jit(solution)/shard_map/all_gather | solution.py:35
  366.4 50.5 %all-gather.31.cloned.1.call-done = bf16[2304,1152]{0,1:T(8,128)(2,1)} async-done(((bf16[2304,72]{0,1:T(8,128)(2,1)}), bf16[2304,1152]{0,1:T(8,128)(2,1)}) %all-gather.31.cloned.1.call-update) | async-done | bytes 5308432 | tf_op jit(solution)/shard_map/all_gather | solution.py:64
  426.7 112.8 %all-gather.33.cloned.1.call-done = bf16[1152,6,1152]{2,0,1:T(8,128)(2,1)} async-done(((bf16[72,6,1152]{2,0,1:T(8,128)(2,1)}), bf16[1152,6,1152]{2,0,1:T(8,128)(2,1)}) %all-gather.33.cloned.1.call-update) | async-done | bytes 15925264 | tf_op jit(solution)/shard_map/all_gather | solution.py:248
  539.4 22.4 %copy.125 = bf16[1152,6,1152]{0,2,1:T(8,128)(2,1)} copy(bf16[1152,6,1152]{2,0,1:T(8,128)(2,1)} %all-gather.33.cloned.1.call-done) | data formatting | bytes 31850496 | tf_op jit(solution)/shard_map/all_gather | solution.py:248
  602.5 21.7 %all-gather.37.cloned.1.call-done = bf16[1152,3,576]{2,0,1:T(8,128)(2,1)} async-done(((bf16[72,3,576]{2,0,1:T(8,128)(2,1)}), bf16[1152,3,576]{2,0,1:T(8,128)(2,1)}) %all-gather.37.cloned.1.call-update) | async-done | bytes 3981328 | tf_op jit(solution)/shard_map/all_gather | solution.py:56
  624.3 23.3 %all-gather.35.cloned.1.call-done = bf16[32,16,1152]{2,1,0:T(8,128)(2,1)} async-done(((bf16[32,8,1152]{2,1,0:T(8,128)(2,1)}), bf16[32,16,1152]{2,1,0:T(8,128)(2,1)}) %all-gather.35.cloned.1.call-update) | async-done | bytes 1179664 | tf_op jit(solution)/shard_map/all_gather | solution.py:35
  669.1 20.1 %all-gather.39.cloned.1.call-done = bf16[576,1152]{0,1:T(8,128)(2,1)} async-done(((bf16[576,72]{0,1:T(8,128)(2,1)}), bf16[576,1152]{0,1:T(8,128)(2,1)}) %all-gather.39.cloned.1.call-update) | async-done | bytes 1327120 | tf_op jit(solution)/shard_map/all_gather | solution.py:57
  722.2 50.2 %all-gather.43.cloned.1.call-done = bf16[1152,2304]{1,0:T(8,128)(2,1)} async-done(((bf16[72,2304]{1,0:T(8,128)(2,1)}), bf16[1152,2304]{1,0:T(8,128)(2,1)}) %all-gather.43.cloned.1.call-update) | async-done | bytes 5308432 | tf_op jit(solution)/shard_map/all_gather | solution.py:63
  772.4 23.4 %all-gather.41.cloned.1.call-done = bf16[32,16,1152]{2,1,0:T(8,128)(2,1)} async-done(((bf16[32,8,1152]{2,1,0:T(8,128)(2,1)}), bf16[32,16,1152]{2,1,0:T(8,128)(2,1)}) %all-gather.41.cloned.1.call-update) | async-done | bytes 1179664 | tf_op jit(solution)/shard_map/all_gather | solution.py:35
  804.1 50.4 %all-gather.45.cloned.1.call-done = bf16[2304,1152]{0,1:T(8,128)(2,1)} async-done(((bf16[2304,72]{0,1:T(8,128)(2,1)}), bf16[2304,1152]{0,1:T(8,128)(2,1)}) %all-gather.45.cloned.1.call-update) | async-done | bytes 5308432 | tf_op jit(solution)/shard_map/all_gather | solution.py:64
  866.0 20.4 %all_to_all.45 = bf16[2,128,1152]{2,0,1:T(2,128)(2,1)S(1)} all-to-all(bf16[2,128,1152]{2,0,1:T(2,128)(2,1)S(1)} %copy.283), channel_id=1, replica_groups=mesh['dp'=16,'tensor'=2] {'dp'}, dimensions={1} | all-to-all | bytes 1179648 | tf_op jit(solution)/shard_map/all_to_all | solution.py:69
  893.6 20.9 %all-gather.47.cloned.1.call-done = bf16[32,16,1152]{2,1,0:T(8,128)(2,1)} async-done(((bf16[32,8,1152]{2,1,0:T(8,128)(2,1)}), bf16[32,16,1152]{2,1,0:T(8,128)(2,1)}) %all-gather.47.cloned.1.call-update) | async-done | bytes 1179664 | tf_op jit(solution)/shard_map/all_gather | solution.py:45
  931.8 21.9 %reduce-scatter.53.cloned.1.call-done = bf16[8,36864]{1,0:T(8,128)(2,1)} async-done(((bf16[16,36864]{1,0:T(8,128)(2,1)}), bf16[8,36864]{1,0:T(8,128)(2,1)}) %reduce-scatter.53.cloned.1.call-update) | async-done | bytes 589840
  962.9 22.8 %all-gather.49.cloned.1.call-done = bf16[32,16,1152]{2,1,0:T(8,128)(2,1)} async-done(((bf16[32,8,1152]{2,1,0:T(8,128)(2,1)}), bf16[32,16,1152]{2,1,0:T(8,128)(2,1)}) %all-gather.49.cloned.1.call-update) | async-done | bytes 1179664 | tf_op jit(solution)/shard_map/all_gather | solution.py:45
  1028.1 21.7 %reduce-scatter.55.cloned.1.call-done = bf16[8,36864]{1,0:T(8,128)(2,1)} async-done(((bf16[16,36864]{1,0:T(8,128)(2,1)}), bf16[8,36864]{1,0:T(8,128)(2,1)}) %reduce-scatter.55.cloned.1.call-update) | async-done | bytes 589840
  1054.4 22.7 %all_to_all.46 = bf16[32,8,1152]{2,1,0:T(8,128)(2,1)S(1)} all-to-all(bf16[32,8,1152]{2,1,0:T(8,128)(2,1)S(1)} %fusion.184), channel_id=1, replica_groups=mesh['dp'=16,'tensor'=2] {'dp'}, dimensions={0} | all-to-all | bytes 1179648 | tf_op jit(solution)/shard_map/all_to_all | solution.py:75
  1078.1 20.3 %all-gather.51.cloned.1.call-done = bf16[2,256,1152]{2,1,0:T(8,128)(2,1)} async-done(((bf16[2,128,1152]{2,1,0:T(8,128)(2,1)}), bf16[2,256,1152]{2,1,0:T(8,128)(2,1)}) %all-gather.51.cloned.1.call-update) | async-done | bytes 1179664 | tf_op jit(solution)/shard_map/all_gather | solution.py:45
  1116.2 21.8 %reduce-scatter.37.cloned.1.call-done = bf16[2,128,1152]{2,1,0:T(8,128)(2,1)} async-done(((bf16[2,256,1152]{2,1,0:T(8,128)(2,1)}), bf16[2,128,1152]{2,1,0:T(8,128)(2,1)}) %reduce-scatter.37.cloned.1.call-update) | async-done | bytes 589840 | tf_op jit(solution)/shard_map/reduce_scatter | solution.py:49
  1144.9 22.4 %all-gather.53.cloned.1.call-done = bf16[2,256,1152]{2,1,0:T(8,128)(2,1)} async-done(((bf16[2,128,1152]{2,1,0:T(8,128)(2,1)}), bf16[2,256,1152]{2,1,0:T(8,128)(2,1)}) %all-gather.53.cloned.1.call-update) | async-done | bytes 1179664 | tf_op jit(solution)/shard_map/all_gather | solution.py:45
  1352.3 24.7 %reduce-scatter.47.cloned.1.call-done = bf16[2304,72]{0,1:T(8,128)(2,1)} async-done(((bf16[2304,1152]{0,1:T(8,128)(2,1)}), bf16[2304,72]{0,1:T(8,128)(2,1)}) %reduce-scatter.47.cloned.1.call-update) | async-done | bytes 331792 | tf_op jit(solution)/shard_map/reduce_scatter | solution.py:235
  1378.9 80.7 %reduce-scatter.45.cloned.1.call-done = bf16[72,2304]{1,0:T(8,128)(2,1)} async-done(((bf16[1152,2304]{1,0:T(8,128)(2,1)}), bf16[72,2304]{1,0:T(8,128)(2,1)}) %reduce-scatter.45.cloned.1.call-update) | async-done | bytes 331792 | tf_op jit(solution)/shard_map/reduce_scatter | solution.py:232
  1461.5 73.0 %reduce-scatter.59.cloned.1.call-done = bf16[72,1728]{1,0:T(8,128)(2,1)} async-done(((bf16[1152,1728]{1,0:T(8,128)(2,1)}), bf16[72,1728]{1,0:T(8,128)(2,1)}) %reduce-scatter.59.cloned.1.call-update) | async-done | bytes 248848
  1536.4 60.0 %reduce-scatter.61.cloned.1.call-done = bf16[576,72]{0,1:T(8,128)(2,1)} async-done(((bf16[576,1152]{0,1:T(8,128)(2,1)}), bf16[576,72]{0,1:T(8,128)(2,1)}) %reduce-scatter.61.cloned.1.call-update) | async-done | bytes 82960
  1599.5 124.9 %all-reduce.5.cloned.1.call-done = (f32[2,6912]{1,0:T(2,128)}, f32[2,6912]{1,0:T(2,128)}, f32[8,16]{1,0:T(8,128)}) async-done(((f32[2,6912]{1,0:T(2,128)}, f32[2,6912]{1,0:T(2,128)}, f32[8,16]{1,0:T(8,128)}), (f32[2,6912]{1,0:T(2,128)}, f32[2,6912]{1,0:T(2,128)}, f32[8,16]{1,0:T(8,128)})) %all-reduce.5.cloned.1.call-update) | async-done | bytes 111120 | tf_op jit(solution)/shard_map/psum | solution.py:330
  1737.1 71.8 %reduce-scatter.43.cloned.1.call-done = bf16[2304,72]{0,1:T(8,128)(2,1)} async-done(((bf16[2304,1152]{0,1:T(8,128)(2,1)}), bf16[2304,72]{0,1:T(8,128)(2,1)}) %reduce-scatter.43.cloned.1.call-update) | async-done | bytes 331792 | tf_op jit(solution)/shard_map/reduce_scatter | solution.py:235
  1810.7 80.9 %reduce-scatter.41.cloned.1.call-done = bf16[72,2304]{1,0:T(8,128)(2,1)} async-done(((bf16[1152,2304]{1,0:T(8,128)(2,1)}), bf16[72,2304]{1,0:T(8,128)(2,1)}) %reduce-scatter.41.cloned.1.call-update) | async-done | bytes 331792 | tf_op jit(solution)/shard_map/reduce_scatter | solution.py:232
  1893.5 73.2 %reduce-scatter.57.cloned.1.call-done = bf16[72,1728]{1,0:T(8,128)(2,1)} async-done(((bf16[1152,1728]{1,0:T(8,128)(2,1)}), bf16[72,1728]{1,0:T(8,128)(2,1)}) %reduce-scatter.57.cloned.1.call-update) | async-done | bytes 248848
  (483 shorter events, 522.3 us)
Async XLA Ops:
  7.2 127.3 %all-gather.19.cloned.1.call-start = ((), (), s32[]{:S(2)}) async-start(), calls=%async_computation.20 | async-start | bytes 16920576 | tf_op jit(solution)/shard_map/all_gather | solution.py:247
  7.9 178.7 %all-gather.23.cloned.1.call-start = ((), (), s32[]{:S(2)}) async-start(), calls=%async_computation.22 | async-start | bytes 4700160 | tf_op jit(solution)/shard_map/all_gather | solution.py:56
  8.7 201.4 %all-gather.21.cloned.1.call-start = ((), (), s32[]{:S(2)}) async-start(), calls=%async_computation.21 | async-start | bytes 1769472 | tf_op jit(solution)/shard_map/all_gather | solution.py:35
  169.4 82.1 %all-gather.25.cloned.1.call-start = ((), (), s32[]{:S(2)}) async-start(), calls=%async_computation.23 | async-start | bytes 1566720 | tf_op jit(solution)/shard_map/all_gather | solution.py:57
  170.0 105.8 %reduce-scatter.33.cloned.1.call-start = ((), (), s32[]{:S(2)}) async-start(), calls=%async_computation.24 | async-start | bytes 1769472 | tf_op jit(solution)/shard_map/reduce_scatter | solution.py:39
  255.1 79.4 %all-gather.29.cloned.1.call-start = ((), (), s32[]{:S(2)}) async-start(), calls=%async_computation.26 | async-start | bytes 5640192 | tf_op jit(solution)/shard_map/all_gather | solution.py:63
  255.7 102.4 %all-gather.27.cloned.1.call-start = ((), (), s32[]{:S(2)}) async-start(), calls=%async_computation.25 | async-start | bytes 1769472 | tf_op jit(solution)/shard_map/all_gather | solution.py:35
  279.9 136.9 %all-gather.31.cloned.1.call-start = ((), (), s32[]{:S(2)}) async-start(), calls=%async_computation.27 | async-start | bytes 5640192 | tf_op jit(solution)/shard_map/all_gather | solution.py:64
  280.7 258.8 %all-gather.33.cloned.1.call-start = ((), (), s32[]{:S(2)}) async-start(), calls=%async_computation.29 | async-start | bytes 16920576 | tf_op jit(solution)/shard_map/all_gather | solution.py:248
  281.4 290.1 %reduce-scatter.35.cloned.1.call-start = ((), (), s32[]{:S(2)}) async-start(), calls=%async_computation.28 | async-start | bytes 1769472 | tf_op jit(solution)/shard_map/reduce_scatter | solution.py:39
  425.9 198.4 %all-gather.37.cloned.1.call-start = ((), (), s32[]{:S(2)}) async-start(), calls=%async_computation.31 | async-start | bytes 4700160 | tf_op jit(solution)/shard_map/all_gather | solution.py:56
  578.0 69.6 %all-gather.35.cloned.1.call-start = ((), (), s32[]{:S(2)}) async-start(), calls=%async_computation.30 | async-start | bytes 1769472 | tf_op jit(solution)/shard_map/all_gather | solution.py:35
  601.3 87.8 %all-gather.39.cloned.1.call-start = ((), (), s32[]{:S(2)}) async-start(), calls=%async_computation.32 | async-start | bytes 1566720 | tf_op jit(solution)/shard_map/all_gather | solution.py:57
  602.1 111.7 %reduce-scatter.49.cloned.1.call-start = ((), (), s32[]{:S(2)}) async-start(), calls=%async_computation.46 | async-start | bytes 1769472
  693.0 79.4 %all-gather.43.cloned.1.call-start = ((), (), s32[]{:S(2)}) async-start(), calls=%async_computation.34 | async-start | bytes 5640192 | tf_op jit(solution)/shard_map/all_gather | solution.py:63
  693.6 102.2 %all-gather.41.cloned.1.call-start = ((), (), s32[]{:S(2)}) async-start(), calls=%async_computation.33 | async-start | bytes 1769472 | tf_op jit(solution)/shard_map/all_gather | solution.py:35
  721.4 133.1 %all-gather.45.cloned.1.call-start = ((), (), s32[]{:S(2)}) async-start(), calls=%async_computation.35 | async-start | bytes 5640192 | tf_op jit(solution)/shard_map/all_gather | solution.py:64
  722.0 166.1 %reduce-scatter.51.cloned.1.call-start = ((), (), s32[]{:S(2)}) async-start(), calls=%async_computation.47 | async-start | bytes 1769472
  893.3 60.4 %reduce-scatter.53.cloned.1.call-start = ((), (), s32[]{:S(2)}) async-start(), calls=%async_computation.48 | async-start | bytes 1769472
  962.8 86.9 %reduce-scatter.55.cloned.1.call-start = ((), (), s32[]{:S(2)}) async-start(), calls=%async_computation.49 | async-start | bytes 1769472
  1027.8 70.5 %all-gather.51.cloned.1.call-start = ((), (), s32[]{:S(2)}) async-start(), calls=%async_computation.38 | async-start | bytes 1769472 | tf_op jit(solution)/shard_map/all_gather | solution.py:45
  1078.0 59.9 %reduce-scatter.37.cloned.1.call-start = ((), (), s32[]{:S(2)}) async-start(), calls=%async_computation.39 | async-start | bytes 1769472 | tf_op jit(solution)/shard_map/reduce_scatter | solution.py:49
  1144.4 122.5 %reduce-scatter.39.cloned.1.call-start = ((), (), s32[]{:S(2)}) async-start(), calls=%async_computation.41 | async-start | bytes 1769472 | tf_op jit(solution)/shard_map/reduce_scatter | solution.py:49
  1199.5 151.2 %reduce-scatter.63.cloned.1.call-start = ((), (), s32[]{:S(2)}) async-start(), calls=%async_computation.53 | async-start | bytes 1566720
  1203.1 173.9 %reduce-scatter.47.cloned.1.call-start = ((), (), s32[]{:S(2)}) async-start(), calls=%async_computation.45 | async-start | bytes 5640192 | tf_op jit(solution)/shard_map/reduce_scatter | solution.py:235
  1211.0 248.6 %reduce-scatter.45.cloned.1.call-start = ((), (), s32[]{:S(2)}) async-start(), calls=%async_computation.44 | async-start | bytes 5640192 | tf_op jit(solution)/shard_map/reduce_scatter | solution.py:232
  1219.2 315.2 %reduce-scatter.59.cloned.1.call-start = ((), (), s32[]{:S(2)}) async-start(), calls=%async_computation.51 | async-start | bytes 4386816
  1255.2 341.2 %reduce-scatter.61.cloned.1.call-start = ((), (), s32[]{:S(2)}) async-start(), calls=%async_computation.52 | async-start | bytes 1566720
  1266.9 457.6 %all-reduce.5.cloned.1.call-start = ((), (), s32[]{:S(2)}) async-start(), calls=%async_computation.54 | async-start | bytes 229376 | tf_op jit(solution)/shard_map/psum | solution.py:330
  1270.0 538.9 %reduce-scatter.43.cloned.1.call-start = ((), (), s32[]{:S(2)}) async-start(), calls=%async_computation.43 | async-start | bytes 5640192 | tf_op jit(solution)/shard_map/reduce_scatter | solution.py:235
  1278.1 613.5 %reduce-scatter.41.cloned.1.call-start = ((), (), s32[]{:S(2)}) async-start(), calls=%async_computation.42 | async-start | bytes 5640192 | tf_op jit(solution)/shard_map/reduce_scatter | solution.py:232
  1286.4 680.2 %reduce-scatter.57.cloned.1.call-start = ((), (), s32[]{:S(2)}) async-start(), calls=%async_computation.50 | async-start | bytes 4386816
  (113 other events, 2170.4 us)
Sparse Core Ops, SparseCore 0:
  10.2 124.2 all-gather.18
  136.7 49.8 all-gather.22
  188.8 21.2 all-gather.20
  212.1 39.3 all-gather.24
  255.2 20.5 reduce-scatter.32
  278.0 56.3 all-gather.28
  336.6 21.3 all-gather.26
  360.4 56.3 all-gather.30
  419.3 120.1 all-gather.32
  564.3 59.8 all-gather.36
  626.2 21.3 all-gather.34
  649.7 39.3 all-gather.38
  693.2 20.5 reduce-scatter.48
  716.0 56.3 all-gather.42
  774.5 21.3 all-gather.40
  798.1 56.3 all-gather.44
  893.4 21.0 all-gather.46
  931.9 21.7 reduce-scatter.52
  962.9 22.7 all-gather.48
  1028.0 21.7 reduce-scatter.54
  1116.2 21.7 reduce-scatter.36
  1144.5 22.7 all-gather.52
  1199.6 21.7 reduce-scatter.38
  1225.5 58.7 reduce-scatter.62
  1288.3 88.6 reduce-scatter.46
  1381.0 78.5 reduce-scatter.44
  1463.4 71.0 reduce-scatter.58
  1538.8 57.6 reduce-scatter.60
  1603.6 120.8 all-reduce.4
  1728.3 80.5 reduce-scatter.42
  1812.9 78.6 reduce-scatter.40
  1895.5 71.0 reduce-scatter.56
  (3 shorter events, 60.2 us)
where the time goes:
time: 1990 us; the launch traced here: 1980 us
  waiting for transfers between devices  1440 us (72%)
  matrix products  225 us (11%)
  local copies, waits for them, and re-layouts  181 us (9%)
  other arithmetic  55.5 us (3%)
  blocking collectives  43.1 us (2%)
    unnamed x43, waiting for transfers between devices  273 us
    reduce_scatter x2, waiting for transfers between devices, mlp_back(): lax.psum_scatter(grad_up.astype(jnp.bfloat16), 'dp', scatter_dimension=0,...  162 us
    psum x1, waiting for transfers between devices, body(): lax.psum((grad_mod_spatial, grad_mod_temporal, squares), ('dp', 'tensor'))  125 us
    all_gather x1, waiting for transfers between devices, modulations(): lax.all_gather(adaln_spatial, 'dp', axis=0, tiled=True)  124 us
    all_gather x1, waiting for transfers between devices, modulations(): lax.all_gather(adaln_temporal, 'dp', axis=0, tiled=True)  113 us
    all_gather x2, waiting for transfers between devices, gather_mlp(): lax.all_gather(up_shard, 'dp', axis=0, tiled=True)  103 us
    all_gather x2, waiting for transfers between devices, gather_mlp(): lax.all_gather(down_shard, 'dp', axis=1, tiled=True)  101 us
    unnamed x249, local copies, waits for them, and re-layouts  97.5 us
  transfers between devices with their start and end apart: 37, of which 33 were waited for; matrix products, arithmetic and copies ran while one was open for 15% of the time, Pallas kernels for 0%

commit v1 on v0

v1 whole, which is shorter than its diff:
```python
import jax
import jax.numpy as jnp
from jax import lax
from jax.sharding import PartitionSpec as P

HEAD_DIM = 72
PATCHES = 256
FRAMES = 16

highest = lax.Precision.HIGHEST
epsilon = 1e-06
bf16 = jnp.bfloat16
f32 = jnp.float32


def dot(a, b):
    return jnp.dot(a, b, preferred_element_type=f32)


def dot_nt(a, b):
    return lax.dot_general(a, b, (((1,), (1,)), ((), ())), preferred_element_type=f32)


def dot_tn(a, b):
    return lax.dot_general(a, b, (((0,), (0,)), ((), ())), preferred_element_type=f32)


def layer_norm(stream):
    average = jnp.mean(stream, axis=-1, keepdims=True)
    centered = stream - average
    inverse = lax.rsqrt(jnp.mean(centered * centered, axis=-1, keepdims=True) + epsilon)
    return (centered * inverse, inverse)


def gelu_tanh(pre_act):
    return jax.nn.gelu(pre_act, approximate=True)


def swap(value, axis, stride, size):
    return lax.ppermute(value, axis, [(i, i ^ stride) for i in range(size)])


def all_sum(value, axes):
    for axis in axes:
        size = lax.axis_size(axis)
        if size & (size - 1):
            value = lax.psum(value, axis)
            continue
        stride = 1
        while stride < size:
            value = value + swap(value, axis, stride, size)
            stride *= 2
    return value


def gather_tokens(local):
    size = lax.axis_size("tensor")
    if size == 2:
        other = swap(local, "tensor", 1, 2)
        return [local, other]
    return list(lax.all_gather(local, "tensor", axis=0, tiled=False))


def scatter_tokens(parts):
    size = lax.axis_size("tensor")
    if size == 2:
        return parts[0] + swap(parts[1].astype(bf16), "tensor", 1, 2).astype(f32)
    stacked = jnp.stack([part.astype(bf16) for part in parts])
    return lax.psum_scatter(stacked, "tensor", scatter_dimension=0, tiled=False).astype(f32)


def split_heads(values, lead):
    heads = values.shape[-1] // (3 * HEAD_DIM)
    view = values.reshape(lead + (3, heads, HEAD_DIM))
    axis = len(lead)
    return [lax.index_in_dim(view, i, axis, keepdims=False) for i in range(3)]


spatial_forms = ("aqhe,akhe->ahqk", "ahqk,akhe->aqhe", "ahqk,aqhe->akhe")
temporal_forms = ("fshe,gshe->shfg", "shfg,gshe->fshe", "shfg,fshe->gshe")


def attend(qkv, forms):
    queries, keys, values = qkv
    scores = jnp.einsum(forms[0], queries, keys, preferred_element_type=f32) * HEAD_DIM ** (-0.5)
    top = jnp.max(scores, axis=-1, keepdims=True)
    unnormed = jnp.exp(scores - top)
    total = jnp.sum(unnormed, axis=-1, keepdims=True)
    probs = (unnormed / total).astype(bf16)
    out = jnp.einsum(forms[1], probs, values, preferred_element_type=f32).astype(bf16)
    return out, top + jnp.log(total)


def attend_back(qkv, log_total, grad_out, forms):
    queries, keys, values = qkv
    scale = HEAD_DIM ** (-0.5)
    scores = jnp.einsum(forms[0], queries, keys, preferred_element_type=f32) * scale
    probs = jnp.exp(scores - log_total)
    grad_probs = jnp.einsum(forms[0], grad_out, values, preferred_element_type=f32)
    grad_scores = probs * (grad_probs - jnp.sum(probs * grad_probs, axis=-1, keepdims=True))
    grad_scaled = (grad_scores * scale).astype(bf16)
    grad_q = jnp.einsum(forms[1], grad_scaled, keys, preferred_element_type=f32)
    grad_k = jnp.einsum(forms[2], grad_scaled, queries, preferred_element_type=f32)
    grad_v = jnp.einsum(forms[2], probs.astype(bf16), grad_out, preferred_element_type=f32)
    return [grad.astype(bf16) for grad in (grad_q, grad_k, grad_v)]


class Layer:
    def __init__(self, rows, tokens, clips, spatial, first_row):
        self.rows, self.tokens, self.clips, self.spatial = rows, tokens, clips, spatial
        self.first_row = first_row

    def by_row(self, table):
        if self.rows % self.clips == 0:
            width = table.shape[-1]
            spread = jnp.broadcast_to(table[None], (self.rows // self.clips, self.clips, width))
            return spread.reshape(self.rows, 1, width)
        start = lax.rem(self.first_row, self.clips)
        return lax.dynamic_slice_in_dim(table, start, self.rows, 0)[:, None, :]

    def by_clip(self, sums):
        width = sums.shape[-1]
        if self.rows % self.clips == 0:
            return jnp.sum(sums.reshape(self.rows // self.clips, self.clips, width), axis=0)
        start = lax.rem(self.first_row, self.clips)
        empty = jnp.zeros((self.clips, width), f32)
        return lax.dynamic_update_slice_in_dim(empty, sums, start, 0)

    def by_frame(self, entries):
        per_row = jnp.sum(entries * entries, axis=(1, 2))
        frames = max(self.rows // self.clips, 1)
        sums = jnp.sum(per_row.reshape(frames, -1), axis=1)
        if frames == FRAMES:
            return sums
        start = self.first_row // self.clips
        return lax.dynamic_update_slice_in_dim(jnp.zeros((FRAMES,), f32), sums, start, 0)

    def modulated(self, stream, mod, offset):
        normed = layer_norm(stream)[0]
        scale = 1.0 + self.by_row(mod[:, offset + 1])
        return (normed * scale + self.by_row(mod[:, offset])).astype(bf16)

    def flat(self, value):
        return value.reshape(self.rows * self.tokens, value.shape[-1])

    def full(self, value):
        return value.reshape(self.rows, self.tokens, value.shape[-1])

    def sequences(self, parts):
        if self.spatial:
            joined = jnp.stack([self.full(part) for part in parts], axis=1)
            joined = joined.reshape(self.rows, -1, joined.shape[-1])
            return [split_heads(joined, joined.shape[:2])]
        return [
            split_heads(part, (FRAMES, part.shape[0] // FRAMES)) for part in parts
        ]

    def parts(self, groups, count):
        if self.spatial:
            (value,) = groups
            value = value.reshape(self.rows, count, self.tokens, -1)
            return [self.flat(value[:, i]) for i in range(count)]
        return [value.reshape(self.rows * self.tokens, -1) for value in groups]

    def forms(self):
        return spatial_forms if self.spatial else temporal_forms

    def attention(self, stream, mod, weights):
        inner = weights.shape[1] // 4
        hidden = [self.flat(h) for h in gather_tokens(self.modulated(stream, mod, 0))]
        w_qkv, w_proj = weights[:, : 3 * inner], weights[:, 3 * inner :]
        qkv = [dot(h, w_qkv).astype(bf16) for h in hidden]
        groups = self.sequences(qkv)
        results = [attend(group, self.forms()) for group in groups]
        attended = self.parts([r[0] for r in results], len(hidden))
        partial = [self.full(dot_nt(a, w_proj)) for a in attended]
        branch = scatter_tokens(partial)
        gated = self.by_row(mod[:, 2]) * branch
        logs = [r[1] for r in results]
        return stream + gated, gated, (stream, branch, hidden, groups, attended, logs, w_qkv, w_proj)

    def mlp(self, stream, mod, weights):
        inner = weights.shape[1] // 2
        hidden = [self.flat(h) for h in gather_tokens(self.modulated(stream, mod, 3))]
        w_up, w_down = weights[:, :inner], weights[:, inner:]
        pre = [dot(h, w_up) for h in hidden]
        active = [gelu_tanh(p).astype(bf16) for p in pre]
        branch = scatter_tokens([self.full(dot_nt(a, w_down)) for a in active])
        gated = self.by_row(mod[:, 5]) * branch
        return stream + gated, gated, (stream, branch, hidden, pre, active, w_up, w_down)

    def branch_back(self, grad, mod, offset, branch):
        grad_branch = (grad * self.by_row(mod[:, offset + 2])).astype(bf16)
        grad_gate = self.by_clip(jnp.sum(grad * branch, axis=1))
        return [self.flat(g) for g in gather_tokens(grad_branch)], grad_gate

    def norm_back(self, grad, grad_hidden, stream, mod, offset):
        normed, inverse = layer_norm(stream)
        grad_normed = grad_hidden * (1.0 + self.by_row(mod[:, offset + 1]))
        centered = grad_normed - jnp.mean(grad_normed, axis=-1, keepdims=True)
        grad_in = inverse * (
            centered - normed * jnp.mean(grad_normed * normed, axis=-1, keepdims=True)
        )
        shift = self.by_clip(jnp.sum(grad_hidden, axis=1))
        scale = self.by_clip(jnp.sum(grad_hidden * normed, axis=1))
        return grad + grad_in, shift, scale

    def mlp_back(self, grad, mod, stored):
        stream, branch, hidden, pre, active, w_up, w_down = stored
        grad_branch, gate = self.branch_back(grad, mod, 3, branch)
        grad_pre = [
            jax.vjp(gelu_tanh, p)[1](dot(g, w_down))[0].astype(bf16)
            for p, g in zip(pre, grad_branch)
        ]
        grad_hidden = scatter_tokens([self.full(dot_nt(g, w_up)) for g in grad_pre])
        joined = [jnp.concatenate(v) for v in (hidden, grad_pre, grad_branch, active)]
        grad_w = jnp.concatenate(
            [dot_tn(joined[0], joined[1]).astype(bf16), dot_tn(joined[2], joined[3]).astype(bf16)],
            axis=1,
        )
        grad, shift, scale = self.norm_back(grad, grad_hidden, stream, mod, 3)
        return grad, jnp.stack([shift, scale, gate], axis=1), grad_w

    def attention_back(self, grad, mod, stored):
        stream, branch, hidden, groups, attended, logs, w_qkv, w_proj = stored
        grad_branch, gate = self.branch_back(grad, mod, 0, branch)
        grad_att = [dot(g, w_proj).astype(bf16) for g in grad_branch]
        heads = grad_att[0].shape[1] // HEAD_DIM
        if self.spatial:
            view = jnp.stack([self.full(g) for g in grad_att], axis=1)
            views = [view.reshape(self.rows, -1, heads, HEAD_DIM)]
        else:
            views = [g.reshape(FRAMES, -1, heads, HEAD_DIM) for g in grad_att]
        grads = [
            attend_back(group, log, view, self.forms())
            for group, log, view in zip(groups, logs, views)
        ]
        three = [self.parts([g[i] for g in grads], len(hidden)) for i in range(3)]
        grad_qkv = [jnp.concatenate([t[i] for t in three], axis=1) for i in range(len(hidden))]
        grad_hidden = scatter_tokens([self.full(dot_nt(g, w_qkv)) for g in grad_qkv])
        joined = [jnp.concatenate(v) for v in (hidden, grad_qkv, grad_branch, attended)]
        grad_w = jnp.concatenate(
            [dot_tn(joined[0], joined[1]).astype(bf16), dot_tn(joined[2], joined[3]).astype(bf16)],
            axis=1,
        )
        grad, shift, scale = self.norm_back(grad, grad_hidden, stream, mod, 0)
        return grad, jnp.stack([shift, scale, gate], axis=1), grad_w


def to_places(stream):
    return lax.all_to_all(
        stream.astype(bf16), "dp", split_axis=1, concat_axis=0, tiled=True
    ).astype(f32)


def to_frames(stream):
    return lax.all_to_all(stream.astype(bf16), "dp", split_axis=0, concat_axis=1, tiled=True)


def gather_weights(first, second):
    packed = jnp.concatenate([first.reshape(first.shape[0], -1), second.T], axis=1)
    return lax.all_gather(packed, "dp", axis=0, tiled=True)


def scatter_grads(grad_w, first, second):
    local = lax.psum_scatter(grad_w, "dp", scatter_dimension=0, tiled=True).astype(f32)
    cut = local.shape[1] - second.shape[0]
    return local[:, :cut].reshape(first.shape), local[:, cut:].T


def body(
    video_in,
    condition,
    adaln_spatial,
    qkv_spatial,
    proj_spatial,
    up_spatial,
    down_spatial,
    adaln_temporal,
    qkv_temporal,
    proj_temporal,
    up_temporal,
    down_temporal,
    grad_output,
):
    rows, tokens, width = video_in.shape
    clips = condition.shape[0]
    dp, me = lax.axis_size("dp"), lax.axis_index("dp")
    spatial = Layer(rows, tokens, clips, True, me * rows)
    temporal = Layer(rows * dp, tokens // dp, clips, False, 0)

    w_attn_s = gather_weights(qkv_spatial, proj_spatial)
    w_mlp_s = gather_weights(up_spatial, down_spatial)
    w_attn_t = gather_weights(qkv_temporal, proj_temporal)
    w_mlp_t = gather_weights(up_temporal, down_temporal)

    share = adaln_spatial.shape[0]
    cond_rows = lax.dynamic_slice_in_dim(condition, me * share, share, 1)
    silu_rows, silu_pull = jax.vjp(jax.nn.silu, cond_rows)
    silu_low = silu_rows.astype(bf16)
    flat_s = adaln_spatial.reshape(share, -1)
    flat_t = adaln_temporal.reshape(share, -1)
    mods = all_sum(jnp.stack([dot(silu_low, flat_s), dot(silu_low, flat_t)]), ("dp",))
    mod_s = mods[0].reshape(clips, 6, width)
    mod_t = mods[1].reshape(clips, 6, width)

    stream0 = video_in.astype(f32)
    s1, g1, kept1 = spatial.attention(stream0, mod_s, w_attn_s)
    s2, g2, kept2 = spatial.mlp(s1, mod_s, w_mlp_s)
    placed = to_places(s2)
    s3, g3, kept3 = temporal.attention(placed, mod_t, w_attn_t)
    s4, g4, kept4 = temporal.mlp(s3, mod_t, w_mlp_t)
    video_out = to_frames(s4)
    squares = jnp.stack(
        [spatial.by_frame(v) for v in (s1, s2)]
        + [temporal.by_frame(v) for v in (s3, s4)]
        + [spatial.by_frame(v) for v in (g1, g2)]
        + [temporal.by_frame(v) for v in (g3, g4)]
    )
    squares = all_sum(squares, ("dp", "tensor"))
    frame_rms = jnp.sqrt(squares / (clips * PATCHES * width))

    grad = to_places(grad_output)
    grad, dmod4, gw4 = temporal.mlp_back(grad, mod_t, kept4)
    grad_up_t, grad_down_t = scatter_grads(gw4, up_temporal, down_temporal)
    dmod4 = all_sum(dmod4, ("dp", "tensor"))
    grad, dmod3, gw3 = temporal.attention_back(grad, mod_t, kept3)
    grad_qkv_t, grad_proj_t = scatter_grads(gw3, qkv_temporal, proj_temporal)
    dmod3 = all_sum(dmod3, ("dp", "tensor"))
    grad = to_frames(grad).astype(f32)
    grad, dmod2, gw2 = spatial.mlp_back(grad, mod_s, kept2)
    grad_up_s, grad_down_s = scatter_grads(gw2, up_spatial, down_spatial)
    dmod2 = all_sum(dmod2, ("dp", "tensor"))
    grad, dmod1, gw1 = spatial.attention_back(grad, mod_s, kept1)
    grad_qkv_s, grad_proj_s = scatter_grads(gw1, qkv_spatial, proj_spatial)
    dmod1 = all_sum(dmod1, ("dp", "tensor"))

    shift_grad = jnp.stack([d[:, 0] for d in (dmod1, dmod2, dmod3, dmod4)])
    silu_wide = silu_low.astype(f32)

    def adaln_back(flat, dmod_attn, dmod_mlp, shape):
        dmod = jnp.concatenate([dmod_attn, dmod_mlp], axis=1).reshape(clips, -1)
        grad_w = jnp.sum(silu_wide[:, :, None] * dmod[:, None, :], axis=0).reshape(shape)
        back = lax.dot_general(
            dmod, flat.astype(f32), (((1,), (1,)), ((), ())), precision=highest
        )
        return grad_w, back

    adaln_t_grad, back_t = adaln_back(flat_t, dmod3, dmod4, adaln_temporal.shape)
    adaln_s_grad, back_s = adaln_back(flat_s, dmod1, dmod2, adaln_spatial.shape)
    condition_grad = silu_pull(back_s + back_t)[0]
    return (
        video_out,
        grad,
        condition_grad,
        adaln_s_grad,
        grad_qkv_s,
        grad_proj_s,
        grad_up_s,
        grad_down_s,
        adaln_t_grad,
        grad_qkv_t,
        grad_proj_t,
        grad_up_t,
        grad_down_t,
        frame_rms,
        shift_grad,
    )


def solution(mesh):
    return jax.shard_map(
        body,
        mesh=mesh,
        in_specs=(
            P("dp", "tensor", None),
            P(),
            P("dp", None, None),
            P("dp", None, "tensor"),
            P("tensor", "dp"),
            P("dp", "tensor"),
            P("tensor", "dp"),
            P("dp", None, None),
            P("dp", None, "tensor"),
            P("tensor", "dp"),
            P("dp", "tensor"),
            P("tensor", "dp"),
            P("dp", "tensor", None),
        ),
        out_specs=(
            P("dp", "tensor", None),
            P("dp", "tensor", None),
            P(None, "dp"),
            P("dp", None, None),
            P("dp", None, "tensor"),
            P("tensor", "dp"),
            P("dp", "tensor"),
            P("tensor", "dp"),
            P("dp", None, None),
            P("dp", None, "tensor"),
            P("tensor", "dp"),
            P("dp", "tensor"),
            P("tensor", "dp"),
            P(),
            P(),
        ),
        check_vma=False,
    )
```

time: 1990 us -> 963 us (0.48)
  waiting for transfers between devices: 1440 us -> 461 us
  starting transfers between devices: 12.6 us -> 67.9 us
  blocking collectives: 43.1 us -> 0 us
  local copies, waits for them, and re-layouts: 181 us -> 148 us
  matrix products: 225 us -> 200 us
    all_gather x18 -> x4, waiting for transfers between devices: 711 us -> 82.5 us  [gather_weights(): return lax.all_gather(packed, 'dp', axis=0, tiled=True)]
    unnamed x43 -> x10, waiting for transfers between devices: 273 us -> 0.13 us
    ppermute x0 -> x45, waiting for transfers between devices: none -> 168 us  [swap(): return lax.ppermute(value, axis, [(i, i ^ stride) for i in range(size)])]
    psum x1 -> x0, waiting for transfers between devices: 125 us -> none  [body(): lax.psum((grad_mod_spatial, grad_mod_temporal, squares), ('dp', 'tensor'))]
    reduce_scatter x8 -> x2, waiting for transfers between devices: 300 us -> 192 us  [scatter_grads(): lax.psum_scatter(grad_w, 'dp', scatter_dimension=0, tiled=True).astype(f32)]
    unnamed x249 -> x323, local copies, waits for them, and re-layouts: 97.5 us -> 42.4 us
    ppermute x0 -> x45, starting transfers between devices: none -> 50.8 us  [swap(): return lax.ppermute(value, axis, [(i, i ^ stride) for i in range(size)])]
    all_gather x2 -> x0, local copies, waits for them, and re-layouts: 44.8 us -> none  [the longest x1 22.4 us: modulations(): lax.all_gather(adaln_spatial, 'dp', axis=0, tiled=True)]
  transfers between devices with their start and end apart: 37 -> 57, of which waited for: 33 -> 37; matrix products, arithmetic and copies ran while one was open for 15% -> 36% of each run, Pallas kernels for 0% -> 0%
where the time goes in v1:
time: 963 us; the launch traced here: 955 us
  waiting for transfers between devices  461 us (48%)
  matrix products  200 us (21%)
  local copies, waits for them, and re-layouts  148 us (15%)
  starting transfers between devices  67.9 us (7%)
  other arithmetic  60.5 us (6%)
  between operations  17 us (2%)
    reduce_scatter x2, waiting for transfers between devices, scatter_grads(): lax.psum_scatter(grad_w, 'dp', scatter_dimension=0, tiled=True).astype(f32)  192 us
    ppermute x45, waiting for transfers between devices, swap(): return lax.ppermute(value, axis, [(i, i ^ stride) for i in range(size)])  168 us
    all_gather x4, waiting for transfers between devices, gather_weights(): return lax.all_gather(packed, 'dp', axis=0, tiled=True)  82.5 us
    dot_general x18, matrix products, dot(): return jnp.dot(a, b, preferred_element_type=f32)  66.4 us
    ppermute x45, starting transfers between devices, swap(): return lax.ppermute(value, axis, [(i, i ^ stride) for i in range(size)])  50.8 us
    dot_general x16, matrix products, dot_nt(): lax.dot_general(a, b, (((1,), (1,)), ((), ())), preferred_element_type=f32)  46.1 us
    unnamed x323, local copies, waits for them, and re-layouts  42.4 us
    dot_general x8, matrix products, dot_tn(): lax.dot_general(a, b, (((0,), (0,)), ((), ())), preferred_element_type=f32)  31.2 us
  transfers between devices with their start and end apart: 57, of which 37 were waited for; matrix products, arithmetic and copies ran while one was open for 36% of the time, Pallas kernels for 0%

profile of v1, /device:TPU:0, one launch (start us, length us, event | category | flops | bytes accessed | tf_op | source)
XLA Modules:
  0.0 955.1 jit_solution(9951771068518137174)
XLA Ops:
  21.7 5.2 collective-permute-done.1
  29.5 7.5 collective-permute-done.2
  38.6 6.2 collective-permute-done.3
  48.7 6.0 all-to-all-start.2
  56.7 26.1 %all-gather.5.cloned.1.call-done = bf16[1152,2304]{1,0:T(8,128)(2,1)} async-done(((bf16[72,2304]{1,0:T(8,128)(2,1)}), bf16[1152,2304]{1,0:T(8,128)(2,1)}) %all-gather.5.cloned.1.call-update) | async-done | bytes 5308432 | tf_op jit(solution)/shard_map/all_gather | solution.py:262
  91.1 5.2 fusion.67
  122.5 13.8 %collective-permute-done.5 = bf16[2,128,1152]{2,1,0:T(8,128)(2,1)S(1)} collective-permute-done((bf16[2,128,1152]{2,1,0:T(8,128)(2,1)}, bf16[2,128,1152]{2,1,0:T(8,128)(2,1)S(1)}, u32[]{:S(2)}, u32[]{:S(2)}) %collective-permute-start.5) | collective-permute-done | bytes 589856 | tf_op jit(solution)/shard_map/ppermute | solution.py:40
  142.3 13.1 %collective-permute-done.6 = bf16[2,128,1152]{2,1,0:T(8,128)(2,1)S(1)} collective-permute-done((bf16[2,128,1152]{2,1,0:T(8,128)(2,1)S(1)}, bf16[2,128,1152]{2,1,0:T(8,128)(2,1)S(1)}, u32[]{:S(2)}, u32[]{:S(2)}) %collective-permute-start.6) | collective-permute-done | bytes 589856 | tf_op jit(solution)/shard_map/ppermute | solution.py:40
  155.4 18.0 %all-gather.7.cloned.1.call-done = bf16[1152,4608]{1,0:T(8,128)(2,1)} async-done(((bf16[72,4608]{1,0:T(8,128)(2,1)}), bf16[1152,4608]{1,0:T(8,128)(2,1)}) %all-gather.7.cloned.1.call-update) | async-done | bytes 10616848 | tf_op jit(solution)/shard_map/all_gather | solution.py:262
  173.4 5.9 multiply_convert_fusion.3
  186.0 10.7 %collective-permute-done.7 = bf16[2,128,1152]{2,1,0:T(8,128)(2,1)S(1)} collective-permute-done((bf16[2,128,1152]{2,1,0:T(8,128)(2,1)S(1)}, bf16[2,128,1152]{2,1,0:T(8,128)(2,1)S(1)}, u32[]{:S(2)}, u32[]{:S(2)}) %collective-permute-start.7) | collective-permute-done | bytes 589856 | tf_op jit(solution)/shard_map/ppermute | solution.py:40
  212.4 17.5 %all-to-all-done = bf16[2,128,1152]{2,0,1:T(2,128)(2,1)S(1)} async-done(((bf16[2,128,1152]{2,0,1:T(2,128)(2,1)}), bf16[2,128,1152]{2,0,1:T(2,128)(2,1)S(1)}, u32[]{:S(2)}, u32[]{:S(2)}) %all-to-all-start) | async-done | bytes 589856 | tf_op jit(solution)/shard_map/all_to_all | solution.py:251
  234.0 7.2 all-gather.9.cloned.1.call-done
  283.6 7.4 collective-permute-done.9
  300.4 31.2 %all-gather.11.cloned.1.call-done = bf16[1152,4608]{1,0:T(8,128)(2,1)} async-done(((bf16[72,4608]{1,0:T(8,128)(2,1)}), bf16[1152,4608]{1,0:T(8,128)(2,1)}) %all-gather.11.cloned.1.call-update) | async-done | bytes 10616848 | tf_op jit(solution)/shard_map/all_gather | solution.py:262
  358.3 12.0 %collective-permute-done.13 = bf16[32,8,1152]{2,1,0:T(8,128)(2,1)S(1)} collective-permute-done((bf16[32,8,1152]{2,1,0:T(8,128)(2,1)S(1)}, bf16[32,8,1152]{2,1,0:T(8,128)(2,1)S(1)}, u32[]{:S(2)}, u32[]{:S(2)}) %collective-permute-start.13) | collective-permute-done | bytes 589856 | tf_op jit(solution)/shard_map/ppermute | solution.py:40
  453.7 5.7 convolution_convert_fusion.5
  459.4 7.2 collective-permute-done.15
  479.8 8.5 copy.644
  491.9 6.2 fusion.112
  498.1 7.2 collective-permute-done.16
  513.5 12.0 %collective-permute-done.17 = bf16[2,128,1152]{2,1,0:T(8,128)(2,1)S(1)} collective-permute-done((bf16[2,128,1152]{2,1,0:T(8,128)(2,1)S(1)}, bf16[2,128,1152]{2,1,0:T(8,128)(2,1)S(1)}, u32[]{:S(2)}, u32[]{:S(2)}) %collective-permute-start.17) | collective-permute-done | bytes 589856 | tf_op jit(solution)/shard_map/ppermute | solution.py:40
  536.2 7.8 collective-permute-done.18
  564.5 8.3 fusion.203
  573.0 9.0 fusion.206
  596.7 8.6 copy.642
  612.2 5.0 convolution_convert_fusion.1
  622.9 5.1 convolution_convert_fusion.3
  655.3 22.9 %collective-permute-done.38 = f32[2,3,1152]{2,0,1:T(2,128)S(1)} collective-permute-done((f32[2,3,1152]{2,0,1:T(2,128)S(1)}, f32[2,3,1152]{2,0,1:T(2,128)S(1)}, u32[]{:S(2)}, u32[]{:S(2)}) %collective-permute-start.38) | collective-permute-done | bytes 27680 | tf_op jit(solution)/shard_map/ppermute | solution.py:40
  711.8 5.6 collective-permute-done.19
  749.5 71.5 %reduce-scatter.11.cloned.1.call-done = bf16[72,4608]{1,0:T(8,128)(2,1)} async-done(((bf16[1152,4608]{1,0:T(8,128)(2,1)}), bf16[72,4608]{1,0:T(8,128)(2,1)}) %reduce-scatter.11.cloned.1.call-update) | async-done | bytes 663568 | tf_op jit(solution)/shard_map/reduce_scatter | solution.py:266
  824.9 120.1 %reduce-scatter.9.cloned.1.call-done = bf16[72,4608]{1,0:T(8,128)(2,1)} async-done(((bf16[1152,4608]{1,0:T(8,128)(2,1)}), bf16[72,4608]{1,0:T(8,128)(2,1)}) %reduce-scatter.9.cloned.1.call-update) | async-done | bytes 663568 | tf_op jit(solution)/shard_map/reduce_scatter | solution.py:266
  (708 shorter events, 434.5 us)
Async XLA Ops:
  7.2 75.6 %all-gather.5.cloned.1.call-start = ((), (), s32[]{:S(2)}) async-start(), calls=%async_computation.8 | async-start | bytes 5640192 | tf_op jit(solution)/shard_map/all_gather | solution.py:262
  10.5 163.0 %all-gather.7.cloned.1.call-start = ((), (), s32[]{:S(2)}) async-start(), calls=%async_computation.9 | async-start | bytes 11280384 | tf_op jit(solution)/shard_map/all_gather | solution.py:262
  11.5 229.7 %all-gather.9.cloned.1.call-start = ((), (), s32[]{:S(2)}) async-start(), calls=%async_computation.10 | async-start | bytes 5640192 | tf_op jit(solution)/shard_map/all_gather | solution.py:262
  12.8 318.8 %all-gather.11.cloned.1.call-start = ((), (), s32[]{:S(2)}) async-start(), calls=%async_computation.11 | async-start | bytes 11280384 | tf_op jit(solution)/shard_map/all_gather | solution.py:262
  45.4 11.3 %collective-permute-start.4 = (bf16[2,128,1152]{2,1,0:T(8,128)(2,1)S(1)}, bf16[2,128,1152]{2,1,0:T(8,128)(2,1)S(1)}, u32[]{:S(2)}, u32[]{:S(2)}) collective-permute-start(bf16[2,128,1152]{2,1,0:T(8,128)(2,1)S(1)} %fusion.222), channel_id=1, source_target_pairs={{0,1},{1,0},{2,3},{3,2},{4,5},{5,4},{6,7},{7,6},{8,9},{9,8},{10,11... | collective-permute-start | bytes 1769480 | tf_op jit(solution)/shard_map/ppermute | solution.py:40
  48.7 152.6 %all-to-all-start.2 = ((bf16[2,128,1152]{2,0,1:T(2,128)(2,1)}), bf16[2,128,1152]{2,0,1:T(2,128)(2,1)}, u32[]{:S(2)}, u32[]{:S(2)}) async-start(bf16[2,128,1152]{2,0,1:T(2,128)(2,1)} %copy.757), calls=%async_computation.2 | async-start | bytes 1179648 | tf_op jit(solution)/shard_map/all_to_all | solution.py:251
  120.5 15.8 %collective-permute-start.5 = (bf16[2,128,1152]{2,1,0:T(8,128)(2,1)}, bf16[2,128,1152]{2,1,0:T(8,128)(2,1)S(1)}, u32[]{:S(2)}, u32[]{:S(2)}) collective-permute-start(bf16[2,128,1152]{2,1,0:T(8,128)(2,1)} %convolution_convert_fusion.9), channel_id=1, source_target_pairs={{0,1},{1,0},{2,3},{3,2},{4,5},{5,4},{6,7},{7,6},{8,9},{9,8},{10,11... | collective-permute-start | bytes 1769480 | tf_op jit(solution)/shard_map/ppermute | solution.py:40
  140.5 15.0 %collective-permute-start.6 = (bf16[2,128,1152]{2,1,0:T(8,128)(2,1)S(1)}, bf16[2,128,1152]{2,1,0:T(8,128)(2,1)S(1)}, u32[]{:S(2)}, u32[]{:S(2)}) collective-permute-start(bf16[2,128,1152]{2,1,0:T(8,128)(2,1)S(1)} %add_convert_fusion.3), channel_id=1, source_target_pairs={{0,1},{1,0},{2,3},{3,2},{4,5},{5,4},{6,7},{7,6},{8,9},{9,8},{10,11... | collective-permute-start | bytes 1769480 | tf_op jit(solution)/shard_map/ppermute | solution.py:40
  181.1 15.6 %collective-permute-start.7 = (bf16[2,128,1152]{2,1,0:T(8,128)(2,1)S(1)}, bf16[2,128,1152]{2,1,0:T(8,128)(2,1)S(1)}, u32[]{:S(2)}, u32[]{:S(2)}) collective-permute-start(bf16[2,128,1152]{2,1,0:T(8,128)(2,1)S(1)} %bitcast.574), channel_id=1, source_target_pairs={{0,1},{1,0},{2,3},{3,2},{4,5},{5,4},{6,7},{7,6},{8,9},{9,8},{10,11... | collective-permute-start | bytes 1769480 | tf_op jit(solution)/shard_map/ppermute | solution.py:40
  201.2 28.7 %all-to-all-start = ((bf16[2,128,1152]{2,0,1:T(2,128)(2,1)}), bf16[2,128,1152]{2,0,1:T(2,128)(2,1)S(1)}, u32[]{:S(2)}, u32[]{:S(2)}) async-start(bf16[2,128,1152]{2,0,1:T(2,128)(2,1)} %copy.565), calls=%async_computation | async-start | bytes 1179648 | tf_op jit(solution)/shard_map/all_to_all | solution.py:251
  210.0 133.7 %collective-permute-start.12 = (bf16[32,8,1152]{2,1,0:T(8,128)(2,1)}, bf16[32,8,1152]{2,1,0:T(8,128)(2,1)}, u32[]{:S(2)}, u32[]{:S(2)}) collective-permute-start(bf16[32,8,1152]{2,1,0:T(8,128)(2,1)} %fusion.257), channel_id=1, source_target_pairs={{0,1},{1,0},{2,3},{3,2},{4,5},{5,4},{6,7},{7,6},{8,9},{9,8},{10,11... | collective-permute-start | bytes 1769480 | tf_op jit(solution)/shard_map/ppermute | solution.py:40
  232.2 23.2 %collective-permute-start.8 = (bf16[32,8,1152]{2,1,0:T(8,128)(2,1)}, bf16[32,8,1152]{2,1,0:T(8,128)(2,1)}, u32[]{:S(2)}, u32[]{:S(2)}) collective-permute-start(bf16[32,8,1152]{2,1,0:T(8,128)(2,1)} %add_convert_fusion.2), channel_id=1, source_target_pairs={{0,1},{1,0},{2,3},{3,2},{4,5},{5,4},{6,7},{7,6},{8,9},{9,8},{10,11... | collective-permute-start | bytes 1769480 | tf_op jit(solution)/shard_map/ppermute | solution.py:40
  275.1 15.8 %collective-permute-start.9 = (bf16[32,8,1152]{2,1,0:T(8,128)(2,1)}, bf16[32,8,1152]{2,1,0:T(8,128)(2,1)}, u32[]{:S(2)}, u32[]{:S(2)}) collective-permute-start(bf16[32,8,1152]{2,1,0:T(8,128)(2,1)} %convolution_convert_fusion.8), channel_id=1, source_target_pairs={{0,1},{1,0},{2,3},{3,2},{4,5},{5,4},{6,7},{7,6},{8,9},{9,8},{10,11... | collective-permute-start | bytes 1769480 | tf_op jit(solution)/shard_map/ppermute | solution.py:40
  298.9 37.5 %collective-permute-start.10 = (bf16[32,8,1152]{2,1,0:T(8,128)(2,1)}, bf16[32,8,1152]{2,1,0:T(8,128)(2,1)}, u32[]{:S(2)}, u32[]{:S(2)}) collective-permute-start(bf16[32,8,1152]{2,1,0:T(8,128)(2,1)} %add_convert_fusion.1), channel_id=1, source_target_pairs={{0,1},{1,0},{2,3},{3,2},{4,5},{5,4},{6,7},{7,6},{8,9},{9,8},{10,11... | collective-permute-start | bytes 1769480 | tf_op jit(solution)/shard_map/ppermute | solution.py:40
  342.1 16.2 %collective-permute-start.11 = (bf16[32,8,1152]{2,1,0:T(8,128)(2,1)S(1)}, bf16[32,8,1152]{2,1,0:T(8,128)(2,1)S(1)}, u32[]{:S(2)}, u32[]{:S(2)}) collective-permute-start(bf16[32,8,1152]{2,1,0:T(8,128)(2,1)S(1)} %fusion.100), channel_id=1, source_target_pairs={{0,1},{1,0},{2,3},{3,2},{4,5},{5,4},{6,7},{7,6},{8,9},{9,8},{10,11... | collective-permute-start | bytes 1769480 | tf_op jit(solution)/shard_map/ppermute | solution.py:40
  349.2 21.1 %collective-permute-start.13 = (bf16[32,8,1152]{2,1,0:T(8,128)(2,1)S(1)}, bf16[32,8,1152]{2,1,0:T(8,128)(2,1)S(1)}, u32[]{:S(2)}, u32[]{:S(2)}) collective-permute-start(bf16[32,8,1152]{2,1,0:T(8,128)(2,1)S(1)} %fusion.103), channel_id=1, source_target_pairs={{0,1},{1,0},{2,3},{3,2},{4,5},{5,4},{6,7},{7,6},{8,9},{9,8},{10,11... | collective-permute-start | bytes 1769480 | tf_op jit(solution)/shard_map/ppermute | solution.py:40
  378.1 35.0 %collective-permute-start.14 = (bf16[32,8,1152]{2,1,0:T(8,128)(2,1)}, bf16[32,8,1152]{2,1,0:T(8,128)(2,1)}, u32[]{:S(2)}, u32[]{:S(2)}) collective-permute-start(bf16[32,8,1152]{2,1,0:T(8,128)(2,1)} %multiply_convert_fusion.6), channel_id=1, source_target_pairs={{0,1},{1,0},{2,3},{3,2},{4,5},{5,4},{6,7},{7,6},{8,9},{9,8},{10,11... | collective-permute-start | bytes 1769480 | tf_op jit(solution)/shard_map/ppermute | solution.py:40
  452.1 14.5 %collective-permute-start.15 = (bf16[32,8,1152]{2,1,0:T(8,128)(2,1)S(1)}, bf16[32,8,1152]{2,1,0:T(8,128)(2,1)S(1)}, u32[]{:S(2)}, u32[]{:S(2)}) collective-permute-start(bf16[32,8,1152]{2,1,0:T(8,128)(2,1)S(1)} %fusion.97), channel_id=1, source_target_pairs={{0,1},{1,0},{2,3},{3,2},{4,5},{5,4},{6,7},{7,6},{8,9},{9,8},{10,11... | collective-permute-start | bytes 1769480 | tf_op jit(solution)/shard_map/ppermute | solution.py:40
  470.8 19.1 %all-to-all-start.3 = ((bf16[32,8,1152]{2,1,0:T(8,128)(2,1)}), bf16[32,8,1152]{2,1,0:T(8,128)(2,1)S(1)}, u32[]{:S(2)}, u32[]{:S(2)}) async-start(bf16[32,8,1152]{2,1,0:T(8,128)(2,1)} %add_convert_fusion), calls=%async_computation.3 | async-start | bytes 1179648 | tf_op jit(solution)/shard_map/all_to_all | solution.py:257
  474.4 268.2 %reduce-scatter.15.cloned.1.call-start = ((), (), s32[]{:S(2)}) async-start(), calls=%async_computation.15 | async-start | bytes 5640192
  488.4 257.6 %reduce-scatter.13.cloned.1.call-start = ((), (), s32[]{:S(2)}) async-start(), calls=%async_computation.14 | async-start | bytes 5640192
  490.0 15.3 %collective-permute-start.16 = (bf16[2,128,1152]{2,1,0:T(8,128)(2,1)S(1)}, bf16[2,128,1152]{2,1,0:T(8,128)(2,1)S(1)}, u32[]{:S(2)}, u32[]{:S(2)}) collective-permute-start(bf16[2,128,1152]{2,1,0:T(8,128)(2,1)S(1)} %fusion.255), channel_id=1, source_target_pairs={{0,1},{1,0},{2,3},{3,2},{4,5},{5,4},{6,7},{7,6},{8,9},{9,8},{10,11... | collective-permute-start | bytes 1769480 | tf_op jit(solution)/shard_map/ppermute | solution.py:40
  511.1 14.5 %collective-permute-start.17 = (bf16[2,128,1152]{2,1,0:T(8,128)(2,1)S(1)}, bf16[2,128,1152]{2,1,0:T(8,128)(2,1)S(1)}, u32[]{:S(2)}, u32[]{:S(2)}) collective-permute-start(bf16[2,128,1152]{2,1,0:T(8,128)(2,1)S(1)} %bitcast.573), channel_id=1, source_target_pairs={{0,1},{1,0},{2,3},{3,2},{4,5},{5,4},{6,7},{7,6},{8,9},{9,8},{10,11... | collective-permute-start | bytes 1769480 | tf_op jit(solution)/shard_map/ppermute | solution.py:40
  530.1 13.9 %collective-permute-start.18 = (bf16[2,128,1152]{2,1,0:T(8,128)(2,1)}, bf16[2,128,1152]{2,1,0:T(8,128)(2,1)}, u32[]{:S(2)}, u32[]{:S(2)}) collective-permute-start(bf16[2,128,1152]{2,1,0:T(8,128)(2,1)} %multiply_convert_fusion.5), channel_id=1, source_target_pairs={{0,1},{1,0},{2,3},{3,2},{4,5},{5,4},{6,7},{7,6},{8,9},{9,8},{10,11... | collective-permute-start | bytes 1769480 | tf_op jit(solution)/shard_map/ppermute | solution.py:40
  605.3 215.7 %reduce-scatter.11.cloned.1.call-start = ((), (), s32[]{:S(2)}) async-start(), calls=%async_computation.13 | async-start | bytes 11280384 | tf_op jit(solution)/shard_map/reduce_scatter | solution.py:266
  621.8 323.2 %reduce-scatter.9.cloned.1.call-start = ((), (), s32[]{:S(2)}) async-start(), calls=%async_computation.12 | async-start | bytes 11280384 | tf_op jit(solution)/shard_map/reduce_scatter | solution.py:266
  647.3 41.6 %all-to-all-start.1 = ((bf16[32,8,1152]{2,1,0:T(8,128)(2,1)}), bf16[32,8,1152]{2,1,0:T(8,128)(2,1)S(1)}, u32[]{:S(2)}, u32[]{:S(2)}) async-start(bf16[32,8,1152]{2,1,0:T(8,128)(2,1)} %get-tuple-element.193), calls=%async_computation.1 | async-start | bytes 1179648 | tf_op jit(solution)/shard_map/all_to_all | solution.py:257
  650.9 27.3 %collective-permute-start.38 = (f32[2,3,1152]{2,0,1:T(2,128)S(1)}, f32[2,3,1152]{2,0,1:T(2,128)S(1)}, u32[]{:S(2)}, u32[]{:S(2)}) collective-permute-start(f32[2,3,1152]{2,0,1:T(2,128)S(1)} %add.420), channel_id=1, source_target_pairs={{0,16},{2,18},{4,20},{6,22},{8,24},{10,26},{12,28},{14,30},{16,0},... | collective-permute-start | bytes 82952 | tf_op jit(solution)/shard_map/ppermute | solution.py:40
  653.7 25.1 %collective-permute-start.32 = (f32[2,3,1152]{2,0,1:T(2,128)S(1)}, f32[2,3,1152]{2,0,1:T(2,128)S(1)}, u32[]{:S(2)}, u32[]{:S(2)}) collective-permute-start(f32[2,3,1152]{2,0,1:T(2,128)S(1)} %fusion.415), channel_id=1, source_target_pairs={{0,8},{2,10},{4,12},{6,14},{8,0},{10,2},{12,4},{14,6},{16,24},{18,... | collective-permute-start | bytes 82952 | tf_op jit(solution)/shard_map/ppermute | solution.py:40
  703.7 13.6 %collective-permute-start.19 = (bf16[2,128,1152]{2,1,0:T(8,128)(2,1)S(1)}, bf16[2,128,1152]{2,1,0:T(8,128)(2,1)S(1)}, u32[]{:S(2)}, u32[]{:S(2)}) collective-permute-start(bf16[2,128,1152]{2,1,0:T(8,128)(2,1)S(1)} %bitcast.572), channel_id=1, source_target_pairs={{0,1},{1,0},{2,3},{3,2},{4,5},{5,4},{6,7},{7,6},{8,9},{9,8},{10,11... | collective-permute-start | bytes 1769480 | tf_op jit(solution)/shard_map/ppermute | solution.py:40
  705.4 12.8 %collective-permute-start.44 = (f32[8,16]{1,0:T(8,128)S(1)}, f32[8,16]{1,0:T(8,128)S(1)}, u32[]{:S(2)}, u32[]{:S(2)}) collective-permute-start(f32[8,16]{1,0:T(8,128)S(1)} %add.428), channel_id=1, source_target_pairs={{0,1},{1,0},{2,3},{3,2},{4,5},{5,4},{6,7},{7,6},{8,9},{9,8},{10,11... | collective-permute-start | bytes 1544 | tf_op jit(solution)/shard_map/ppermute | solution.py:40
  706.9 12.0 %collective-permute-start.29 = (f32[2,3,1152]{2,0,1:T(2,128)S(1)}, f32[2,3,1152]{2,0,1:T(2,128)S(1)}, u32[]{:S(2)}, u32[]{:S(2)}) collective-permute-start(f32[2,3,1152]{2,0,1:T(2,128)S(1)} %add.411), channel_id=1, source_target_pairs={{0,1},{1,0},{2,3},{3,2},{4,5},{5,4},{6,7},{7,6},{8,9},{9,8},{10,11... | collective-permute-start | bytes 82952 | tf_op jit(solution)/shard_map/ppermute | solution.py:40
  (172 other events, 1693.8 us)
Sparse Core Ops, SparseCore 0:
  10.8 71.9 all-gather.4
  85.6 87.7 all-gather.6
  176.2 64.9 all-gather.8
  243.9 87.6 all-gather.10
  488.5 80.1 reduce-scatter.14
  605.4 91.9 reduce-scatter.12
  701.5 119.4 reduce-scatter.10
  825.1 119.9 reduce-scatter.8

commit v2 on v1

--- a/solution.py
+++ b/solution.py
@@ -1,6 +1,10 @@
+import functools
+
 import jax
 import jax.numpy as jnp
 from jax import lax
+from jax.experimental import pallas as pl
+from jax.experimental.pallas import tpu as pltpu
 from jax.sharding import PartitionSpec as P
 
 HEAD_DIM = 72
@@ -11,6 +15,7 @@
 epsilon = 1e-06
 bf16 = jnp.bfloat16
 f32 = jnp.float32
+MESH = pl.DeviceIdType.MESH
 
 
 def dot(a, b):
@@ -69,40 +74,259 @@
     return lax.psum_scatter(stacked, "tensor", scatter_dimension=0, tiled=False).astype(f32)
 
 
-def split_heads(values, lead):
-    heads = values.shape[-1] // (3 * HEAD_DIM)
-    view = values.reshape(lead + (3, heads, HEAD_DIM))
-    axis = len(lead)
-    return [lax.index_in_dim(view, i, axis, keepdims=False) for i in range(3)]
-
-
-spatial_forms = ("aqhe,akhe->ahqk", "ahqk,akhe->aqhe", "ahqk,aqhe->akhe")
-temporal_forms = ("fshe,gshe->shfg", "shfg,gshe->fshe", "shfg,fshe->gshe")
-
-
-def attend(qkv, forms):
-    queries, keys, values = qkv
-    scores = jnp.einsum(forms[0], queries, keys, preferred_element_type=f32) * HEAD_DIM ** (-0.5)
-    top = jnp.max(scores, axis=-1, keepdims=True)
-    unnormed = jnp.exp(scores - top)
-    total = jnp.sum(unnormed, axis=-1, keepdims=True)
-    probs = (unnormed / total).astype(bf16)
-    out = jnp.einsum(forms[1], probs, values, preferred_element_type=f32).astype(bf16)
-    return out, top + jnp.log(total)
-
-
-def attend_back(qkv, log_total, grad_out, forms):
-    queries, keys, values = qkv
-    scale = HEAD_DIM ** (-0.5)
-    scores = jnp.einsum(forms[0], queries, keys, preferred_element_type=f32) * scale
-    probs = jnp.exp(scores - log_total)
-    grad_probs = jnp.einsum(forms[0], grad_out, values, preferred_element_type=f32)
-    grad_scores = probs * (grad_probs - jnp.sum(probs * grad_probs, axis=-1, keepdims=True))
-    grad_scaled = (grad_scores * scale).astype(bf16)
-    grad_q = jnp.einsum(forms[1], grad_scaled, keys, preferred_element_type=f32)
-    grad_k = jnp.einsum(forms[2], grad_scaled, queries, preferred_element_type=f32)
-    grad_v = jnp.einsum(forms[2], probs.astype(bf16), grad_out, preferred_element_type=f32)
-    return [grad.astype(bf16) for grad in (grad_q, grad_k, grad_v)]
+def softmax_scores(queries, keys, residue):
+    scores = dot_nt(queries, keys) * HEAD_DIM ** (-0.5)
+    if residue:
+        row = lax.broadcasted_iota(jnp.int32, scores.shape, 0)
+        col = lax.broadcasted_iota(jnp.int32, scores.shape, 1)
+        scores = jnp.where(lax.rem(row, residue) == lax.rem(col, residue), scores, -1e30)
+    unnormed = jnp.exp(scores - jnp.max(scores, axis=-1, keepdims=True))
+    return unnormed * (1.0 / jnp.sum(unnormed, axis=-1, keepdims=True))
+
+
+def joined(refs):
+    blocks = [ref[0] for ref in refs]
+    return blocks[0] if len(blocks) == 1 else jnp.concatenate(blocks, axis=0)
+
+
+def store_rows(refs, columns, value):
+    start = 0
+    for ref in refs:
+        ref[0, :, columns] = value[start : start + ref.shape[1]]
+        start += ref.shape[1]
+
+
+def attend_kernel(count, residue, *refs):
+    ins, outs = refs[:count], refs[count:]
+    qkv = joined(ins)
+    inner = qkv.shape[1] // 3
+    for start in range(0, inner, HEAD_DIM):
+        q, k, v = (
+            qkv[:, part * inner + start : part * inner + start + HEAD_DIM] for part in range(3)
+        )
+        probs = softmax_scores(q, k, residue).astype(bf16)
+        store_rows(outs, slice(start, start + HEAD_DIM), dot(probs, v).astype(bf16))
+
+
+def attend_back_kernel(count, residue, *refs):
+    ins, grads, outs = refs[:count], refs[count : 2 * count], refs[2 * count :]
+    qkv, grad_att = joined(ins), joined(grads)
+    inner = grad_att.shape[1]
+    for start in range(0, inner, HEAD_DIM):
+        q, k, v = (
+            qkv[:, part * inner + start : part * inner + start + HEAD_DIM] for part in range(3)
+        )
+        grad_out = grad_att[:, start : start + HEAD_DIM]
+        probs = softmax_scores(q, k, residue)
+        grad_probs = dot_nt(grad_out, v)
+        mean = jnp.sum(probs * grad_probs, axis=-1, keepdims=True)
+        grad_scaled = (probs * (grad_probs - mean) * HEAD_DIM ** (-0.5)).astype(bf16)
+        results = (
+            dot(grad_scaled, k),
+            dot_tn(grad_scaled, q),
+            dot_tn(probs.astype(bf16), grad_out),
+        )
+        for part, value in enumerate(results):
+            left = part * inner + start
+            store_rows(outs, slice(left, left + HEAD_DIM), value.astype(bf16))
+
+
+def attend_call(kernel, residue, operands, widths):
+    count = len(operands[0])
+    rows, tokens = operands[0][0].shape[:2]
+    spec = lambda width: pl.BlockSpec((1, tokens, width), lambda r: (r, 0, 0))
+    flat = [value for group in operands for value in group]
+    length = count * tokens
+    heads = widths // HEAD_DIM
+    return pl.pallas_call(
+        functools.partial(kernel, count, residue),
+        grid=(rows,),
+        in_specs=[spec(value.shape[2]) for value in flat],
+        out_specs=[spec(widths) for _ in range(count)],
+        out_shape=[jax.ShapeDtypeStruct((rows, tokens, widths), bf16) for _ in range(count)],
+        cost_estimate=pl.CostEstimate(
+            flops=rows * heads * length * length * HEAD_DIM * 4,
+            bytes_accessed=sum(v.size * 2 for v in flat),
+            transcendentals=rows * heads * length * length,
+        ),
+        compiler_params=pltpu.CompilerParams(vmem_limit_bytes=48 << 20),
+    )(*flat)
+
+
+def weight_grad_kernel(count, *refs):
+    ins, outs = refs[: 4 * count], refs[4 * count :]
+    left = 0
+    for pair in range(2):
+        base = 2 * pair * count
+        out = outs[pair % len(outs)]
+        left = left if len(outs) == 1 else 0
+        rows = jnp.concatenate([ref[...] for ref in ins[base : base + count]], axis=0)
+        cols = ins[base + count : base + 2 * count]
+        width = cols[0].shape[1]
+        step = width if width % 1152 else 1152
+        for start in range(0, width, step):
+            right = jnp.concatenate([ref[:, start : start + step] for ref in cols], axis=0)
+            out[:, left + start : left + start + step] = dot_tn(rows, right).astype(bf16)
+        left += width
+
+
+def weight_grad(first, second, split):
+    count, width = len(first[0]), first[0][0].shape[1]
+    block = 384 if width % 384 == 0 else width
+    ins, specs = [], []
+    for rows, cols in (first, second):
+        ins += rows + cols
+        specs += [pl.BlockSpec((r.shape[0], block), lambda i: (0, i)) for r in rows]
+        specs += [pl.BlockSpec(c.shape, lambda i: (0, 0)) for c in cols]
+    wide = [first[1][0].shape[1], second[1][0].shape[1]]
+    total = sum(wide)
+    wide = wide if split else [total]
+    tokens = count * first[0][0].shape[0]
+    return pl.pallas_call(
+        functools.partial(weight_grad_kernel, count),
+        grid=(width // block,),
+        in_specs=specs,
+        out_specs=[pl.BlockSpec((block, w), lambda i: (i, 0)) for w in wide],
+        out_shape=[jax.ShapeDtypeStruct((width, w), bf16) for w in wide],
+        cost_estimate=pl.CostEstimate(
+            flops=2 * tokens * width * total,
+            bytes_accessed=2 * width * total + 2 * tokens * (2 * width + total),
+            transcendentals=0,
+        ),
+        compiler_params=pltpu.CompilerParams(vmem_limit_bytes=48 << 20),
+    )(*ins)
+
+
+def tie(*values):
+    return lax.optimization_barrier(values)
+
+
+class GradScatter:
+    def __init__(self, grad_w, order):
+        self.size, me = lax.axis_size("dp"), lax.axis_index("dp")
+        ring = self.size // 4
+        self.value = grad_w.reshape(ring, 2, 2, -1, grad_w.shape[1])
+        self.at = (me // 4, (me // 2) % 2, me % 2)
+        self.order = list(order)
+        self.wait = None
+        self.begin()
+
+    def pick(self, axis, index):
+        return lax.dynamic_slice_in_dim(self.value, index, 1, axis)
+
+    def begin(self):
+        axis = self.order[0]
+        count, at = self.value.shape[axis], self.at[axis]
+        if axis:
+            self.wait = swap(self.pick(axis, 1 - at), "dp", 3 - axis, self.size)
+        else:
+            self.left = count - 1
+            self.hop(self.pick(0, lax.rem(at + count - 1, count)))
+
+    def hop(self, total):
+        links = [(i, (i + 4) % self.size) for i in range(self.size)]
+        self.wait = lax.ppermute(total, "dp", links)
+
+    def step(self, value=None):
+        if not self.order:
+            return value
+        if value is not None:
+            value, self.wait = tie(value, self.wait)
+        axis = self.order[0]
+        at = self.at[axis]
+        if axis == 0:
+            self.left -= 1
+            at = lax.rem(at + self.left, self.value.shape[0])
+        total = self.pick(axis, at).astype(f32) + self.wait.astype(f32)
+        if axis == 0 and self.left:
+            self.hop(total.astype(bf16))
+            return value
+        self.order.pop(0)
+        self.value = total
+        if self.order:
+            self.value = total.astype(bf16)
+            self.begin()
+        return value
+
+    def finish(self):
+        while self.order:
+            self.step()
+        return self.value.reshape(-1, self.value.shape[-1])
+
+
+class AllSum:
+    def __init__(self, value):
+        self.value = value
+        self.pairs = [
+            (axis, 1 << bit)
+            for axis in ("tensor", "dp")
+            for bit in range(lax.axis_size(axis).bit_length() - 1)
+        ]
+        self.begin()
+
+    def begin(self):
+        axis, stride = self.pairs[0]
+        self.wait = swap(self.value, axis, stride, lax.axis_size(axis))
+
+    def step(self, value=None):
+        if not self.pairs:
+            return value
+        if value is not None:
+            value, self.wait = tie(value, self.wait)
+        self.value = self.value + self.wait
+        self.pairs.pop(0)
+        if self.pairs:
+            self.begin()
+        return value
+
+    def finish(self):
+        while self.pairs:
+            self.step()
+        return self.value
+
+
+def all_sum_kernel(pairs, value, out, slots, landed, send_sem, recv_sem):
+    barrier = pltpu.get_barrier_semaphore()
+    partners = [{axis: lax.axis_index(axis) ^ stride} for axis, stride in pairs]
+    for partner in partners:
+        pl.semaphore_signal(barrier, inc=1, device_id=partner, device_id_type=MESH)
+    pl.semaphore_wait(barrier, len(partners))
+    slots[0] = value[...]
+    for k, partner in enumerate(partners):
+        copy = pltpu.make_async_remote_copy(
+            src_ref=slots.at[k],
+            dst_ref=landed.at[k],
+            send_sem=send_sem.at[k],
+            recv_sem=recv_sem.at[k],
+            device_id=partner,
+            device_id_type=MESH,
+        )
+        copy.start()
+        copy.wait()
+        slots[k + 1] = slots[k] + landed[k]
+    out[...] = slots[len(partners)]
+
+
+def all_sum_now(value):
+    pairs = [
+        (axis, 1 << bit)
+        for axis in ("tensor", "dp")
+        for bit in range(lax.axis_size(axis).bit_length() - 1)
+    ]
+    count = len(pairs)
+    return pl.pallas_call(
+        functools.partial(all_sum_kernel, pairs),
+        in_specs=[pl.BlockSpec(memory_space=pltpu.VMEM)],
+        out_specs=pl.BlockSpec(memory_space=pltpu.VMEM),
+        out_shape=jax.ShapeDtypeStruct(value.shape, f32),
+        scratch_shapes=[
+            pltpu.VMEM((count + 1,) + value.shape, f32),
+            pltpu.VMEM((count,) + value.shape, f32),
+            pltpu.SemaphoreType.DMA((count,)),
+            pltpu.SemaphoreType.DMA((count,)),
+        ],
+        compiler_params=pltpu.CompilerParams(collective_id=0, has_side_effects=True),
+    )(value)
 
 
 class Layer:
@@ -146,38 +370,27 @@
     def full(self, value):
         return value.reshape(self.rows, self.tokens, value.shape[-1])
 
-    def sequences(self, parts):
+    def attend(self, kernel, operands, widths):
         if self.spatial:
-            joined = jnp.stack([self.full(part) for part in parts], axis=1)
-            joined = joined.reshape(self.rows, -1, joined.shape[-1])
-            return [split_heads(joined, joined.shape[:2])]
-        return [
-            split_heads(part, (FRAMES, part.shape[0] // FRAMES)) for part in parts
-        ]
-
-    def parts(self, groups, count):
-        if self.spatial:
-            (value,) = groups
-            value = value.reshape(self.rows, count, self.tokens, -1)
-            return [self.flat(value[:, i]) for i in range(count)]
-        return [value.reshape(self.rows * self.tokens, -1) for value in groups]
-
-    def forms(self):
-        return spatial_forms if self.spatial else temporal_forms
+            views = [[self.full(value) for value in group] for group in operands]
+            return [self.flat(v) for v in attend_call(kernel, 0, views, widths)]
+        count = self.rows * self.tokens
+        out = []
+        for i in range(len(operands[0])):
+            views = [[group[i][None]] for group in operands]
+            out.append(attend_call(kernel, count // FRAMES, views, widths)[0][0])
+        return out
 
     def attention(self, stream, mod, weights):
         inner = weights.shape[1] // 4
         hidden = [self.flat(h) for h in gather_tokens(self.modulated(stream, mod, 0))]
         w_qkv, w_proj = weights[:, : 3 * inner], weights[:, 3 * inner :]
         qkv = [dot(h, w_qkv).astype(bf16) for h in hidden]
-        groups = self.sequences(qkv)
-        results = [attend(group, self.forms()) for group in groups]
-        attended = self.parts([r[0] for r in results], len(hidden))
+        attended = self.attend(attend_kernel, [qkv], inner)
         partial = [self.full(dot_nt(a, w_proj)) for a in attended]
         branch = scatter_tokens(partial)
         gated = self.by_row(mod[:, 2]) * branch
-        logs = [r[1] for r in results]
-        return stream + gated, gated, (stream, branch, hidden, groups, attended, logs, w_qkv, w_proj)
+        return stream + gated, gated, (stream, branch, hidden, qkv, attended, w_qkv, w_proj)
 
     def mlp(self, stream, mod, weights):
         inner = weights.shape[1] // 2
@@ -205,44 +418,33 @@
         scale = self.by_clip(jnp.sum(grad_hidden * normed, axis=1))
         return grad + grad_in, shift, scale
 
-    def mlp_back(self, grad, mod, stored):
+    def mlp_back(self, grad, mod, stored, split, pump):
         stream, branch, hidden, pre, active, w_up, w_down = stored
         grad_branch, gate = self.branch_back(grad, mod, 3, branch)
+        grad_branch[-1] = pump(grad_branch[-1])
         grad_pre = [
             jax.vjp(gelu_tanh, p)[1](dot(g, w_down))[0].astype(bf16)
             for p, g in zip(pre, grad_branch)
         ]
+        grad_pre[-1] = pump(grad_pre[-1])
         grad_hidden = scatter_tokens([self.full(dot_nt(g, w_up)) for g in grad_pre])
-        joined = [jnp.concatenate(v) for v in (hidden, grad_pre, grad_branch, active)]
-        grad_w = jnp.concatenate(
-            [dot_tn(joined[0], joined[1]).astype(bf16), dot_tn(joined[2], joined[3]).astype(bf16)],
-            axis=1,
-        )
+        grad_w = weight_grad((hidden, grad_pre), (grad_branch, active), split)
+        grad_hidden, *grad_w = tie(grad_hidden, *grad_w)
+        grad_hidden = pump(grad_hidden)
         grad, shift, scale = self.norm_back(grad, grad_hidden, stream, mod, 3)
         return grad, jnp.stack([shift, scale, gate], axis=1), grad_w
 
-    def attention_back(self, grad, mod, stored):
-        stream, branch, hidden, groups, attended, logs, w_qkv, w_proj = stored
+    def attention_back(self, grad, mod, stored, split, pump):
+        stream, branch, hidden, qkv, attended, w_qkv, w_proj = stored
         grad_branch, gate = self.branch_back(grad, mod, 0, branch)
+        grad_branch[-1] = pump(grad_branch[-1])
         grad_att = [dot(g, w_proj).astype(bf16) for g in grad_branch]
-        heads = grad_att[0].shape[1] // HEAD_DIM
-        if self.spatial:
-            view = jnp.stack([self.full(g) for g in grad_att], axis=1)
-            views = [view.reshape(self.rows, -1, heads, HEAD_DIM)]
-        else:
-            views = [g.reshape(FRAMES, -1, heads, HEAD_DIM) for g in grad_att]
-        grads = [
-            attend_back(group, log, view, self.forms())
-            for group, log, view in zip(groups, logs, views)
-        ]
-        three = [self.parts([g[i] for g in grads], len(hidden)) for i in range(3)]
-        grad_qkv = [jnp.concatenate([t[i] for t in three], axis=1) for i in range(len(hidden))]
+        grad_qkv = self.attend(attend_back_kernel, [qkv, grad_att], w_qkv.shape[1])
+        grad_qkv[-1] = pump(grad_qkv[-1])
         grad_hidden = scatter_tokens([self.full(dot_nt(g, w_qkv)) for g in grad_qkv])
-        joined = [jnp.concatenate(v) for v in (hidden, grad_qkv, grad_branch, attended)]
-        grad_w = jnp.concatenate(
-            [dot_tn(joined[0], joined[1]).astype(bf16), dot_tn(joined[2], joined[3]).astype(bf16)],
-            axis=1,
-        )
+        grad_w = weight_grad((hidden, grad_qkv), (grad_branch, attended), split)
+        grad_hidden, *grad_w = tie(grad_hidden, *grad_w)
+        grad_hidden = pump(grad_hidden)
         grad, shift, scale = self.norm_back(grad, grad_hidden, stream, mod, 0)
         return grad, jnp.stack([shift, scale, gate], axis=1), grad_w
 
@@ -317,24 +519,43 @@
         + [spatial.by_frame(v) for v in (g1, g2)]
         + [temporal.by_frame(v) for v in (g3, g4)]
     )
-    squares = all_sum(squares, ("dp", "tensor"))
+
+    keep = lambda value: value
+    grad = to_places(grad_output)
+    grad, dmod4, (gw4,) = temporal.mlp_back(grad, mod_t, kept4, False, keep)
+    grad_up_t, grad_down_t = scatter_grads(gw4, up_temporal, down_temporal)
+    grad, dmod3, (gw3,) = temporal.attention_back(grad, mod_t, kept3, False, keep)
+    grad_qkv_t, grad_proj_t = scatter_grads(gw3, qkv_temporal, proj_temporal)
+    early = AllSum(
+        jnp.concatenate([dmod3.reshape(-1), dmod4.reshape(-1), squares.reshape(-1)]).reshape(-1, 128)
+    )
+    grad = early.step(to_frames(grad).astype(f32))
+    grad, dmod2, gw2 = spatial.mlp_back(grad, mod_s, kept2, True, early.step)
+    chains = [GradScatter(gw2[0], (2, 1, 0)), GradScatter(gw2[1], (2, 0, 1))]
+
+    def pump(value):
+        turn = pump.turn
+        pump.turn += 1
+        value = early.step(value)
+        if turn != 1:
+            value = chains[0].step(value)
+        return chains[1].step(value)
+
+    pump.turn = 0
+    grad, dmod1, gw1 = spatial.attention_back(grad, mod_s, kept1, True, pump)
+    chains += [GradScatter(gw1[0], (2, 1, 0)), GradScatter(gw1[1], (2, 0, 1))]
+    late = all_sum_now(jnp.concatenate([dmod1.reshape(-1), dmod2.reshape(-1)]).reshape(-1, 128))
+    late = late.reshape(2, clips, 3, width)
+    dmod1, dmod2 = late[0], late[1]
+    cut = clips * 3 * width
+    flat_early = early.finish().reshape(-1)
+    dmod3 = flat_early[:cut].reshape(clips, 3, width)
+    dmod4 = flat_early[cut : 2 * cut].reshape(clips, 3, width)
+    squares = flat_early[2 * cut :].reshape(8, FRAMES)
     frame_rms = jnp.sqrt(squares / (clips * PATCHES * width))
-
-    grad = to_places(grad_output)
-    grad, dmod4, gw4 = temporal.mlp_back(grad, mod_t, kept4)
-    grad_up_t, grad_down_t = scatter_grads(gw4, up_temporal, down_temporal)
-    dmod4 = all_sum(dmod4, ("dp", "tensor"))
-    grad, dmod3, gw3 = temporal.attention_back(grad, mod_t, kept3)
-    grad_qkv_t, grad_proj_t = scatter_grads(gw3, qkv_temporal, proj_temporal)
-    dmod3 = all_sum(dmod3, ("dp", "tensor"))
-    grad = to_frames(grad).astype(f32)
-    grad, dmod2, gw2 = spatial.mlp_back(grad, mod_s, kept2)
-    grad_up_s, grad_down_s = scatter_grads(gw2, up_spatial, down_spatial)
-    dmod2 = all_sum(dmod2, ("dp", "tensor"))
-    grad, dmod1, gw1 = spatial.attention_back(grad, mod_s, kept1)
-    grad_qkv_s, grad_proj_s = scatter_grads(gw1, qkv_spatial, proj_spatial)
-    dmod1 = all_sum(dmod1, ("dp", "tensor"))
-
+    done = [chain.finish() for chain in chains]
+    grad_up_s, grad_down_s = done[0], done[1].T
+    grad_qkv_s, grad_proj_s = done[2].reshape(qkv_spatial.shape), done[3].T
     shift_grad = jnp.stack([d[:, 0] for d in (dmod1, dmod2, dmod3, dmod4)])
     silu_wide = silu_low.astype(f32)
 

time: 963 us -> 742 us (0.77)
  waiting for transfers between devices: 461 us -> 327 us
  Pallas kernels: 0 us -> 103 us
  local copies, waits for them, and re-layouts: 148 us -> 46.5 us
  matrix products: 200 us -> 108 us
  starting transfers between devices: 67.9 us -> 81.1 us
  other arithmetic: 60.5 us -> 48.7 us
    reduce_scatter x2, waiting for transfers between devices: 192 us -> 0.01 us  [scatter_grads(): lax.psum_scatter(grad_w, 'dp', scatter_dimension=0, tiled=True).astype(f32)]
    pallas_call x0 -> x11, Pallas kernels: none -> 103 us  [the longest x1 37.1 us: all_sum_now(): pl.pallas_call(functools.partial(all_sum_kernel, pairs), in_specs=[pl.Blo...]
    dot_general x26 -> x0, matrix products: 84.9 us -> none  [the longest x8 31.2 us: dot_tn(): lax.dot_general(a, b, (((0,), (0,)), ((), ())), preferred_element_type=f32)]
    ppermute x0 -> x12, waiting for transfers between devices: none -> 48.5 us  [hop(): self.wait = lax.ppermute(total, 'dp', links)]
    ppermute x45 -> x33, waiting for transfers between devices: 168 us -> 129 us  [swap(): return lax.ppermute(value, axis, [(i, i ^ stride) for i in range(size)])]
    all_gather x4, waiting for transfers between devices: 82.5 us -> 120 us  [gather_weights(): return lax.all_gather(packed, 'dp', axis=0, tiled=True)]
    reshape x17 -> x6, local copies, waits for them, and re-layouts: 33 us -> 0.42 us  [the longest x1 0.28 us: scatter_grads(): return (local[:, :cut].reshape(first.shape), local[:, cut:].T)]
    unnamed x323 -> x263, local copies, waits for them, and re-layouts: 42.4 us -> 12.6 us
  transfers between devices with their start and end apart: 57 -> 55, of which waited for: 37 -> 30; matrix products, arithmetic and copies ran while one was open for 36% -> 23% of each run, Pallas kernels for 0% -> 13%
where the time goes in v2:
time: 742 us; the launch traced here: 731 us
  waiting for transfers between devices  327 us (44%)
  matrix products  108 us (15%)
  Pallas kernels  103 us (14%)
  starting transfers between devices  81.1 us (11%)
  other arithmetic  48.7 us (7%)
  local copies, waits for them, and re-layouts  46.5 us (6%)
  between operations  16.9 us (2%)
    ppermute x33, waiting for transfers between devices, swap(): return lax.ppermute(value, axis, [(i, i ^ stride) for i in range(size)])  129 us
    all_gather x4, waiting for transfers between devices, gather_weights(): return lax.all_gather(packed, 'dp', axis=0, tiled=True)  120 us
    dot_general x18, matrix products, dot(): return jnp.dot(a, b, preferred_element_type=f32)  56.9 us
    ppermute x12, waiting for transfers between devices, hop(): self.wait = lax.ppermute(total, 'dp', links)  48.5 us
    dot_general x16, matrix products, dot_nt(): lax.dot_general(a, b, (((1,), (1,)), ((), ())), preferred_element_type=f32)  48 us
    ppermute x33, starting transfers between devices, swap(): return lax.ppermute(value, axis, [(i, i ^ stride) for i in range(size)])  45.3 us
    pallas_call x1, Pallas kernels, all_sum_now(): pl.pallas_call(functools.partial(all_sum_kernel, pairs), in_specs=[pl.Blo...  37.1 us
    pallas_call x6, Pallas kernels, attend_call(): pl.pallas_call(functools.partial(kernel, count, residue), grid=(rows,), i...  36 us
  transfers between devices with their start and end apart: 55, of which 30 were waited for; matrix products, arithmetic and copies ran while one was open for 23% of the time, Pallas kernels for 13%

profile of v2, /device:TPU:0, one launch (start us, length us, event | category | flops | bytes accessed | tf_op | source)
XLA Modules:
  0.0 731.1 jit_solution(2485415215374166632)
XLA Ops:
  29.4 7.6 %collective-permute-done.2 = f32[2,2,6912]{2,1,0:T(2,128)S(1)} collective-permute-done((f32[2,2,6912]{2,1,0:T(2,128)S(1)}, f32[2,2,6912]{2,1,0:T(2,128)S(1)}, u32[]{:S(2)}, u32[]{:S(2)}) %collective-permute-start.2) | collective-permute-done | bytes 110624 | tf_op jit(solution)/shard_map/ppermute | solution.py:45
  38.5 6.3 collective-permute-done.3
  47.3 10.0 %collective-permute-done.4 = bf16[2,128,1152]{2,1,0:T(8,128)(2,1)S(1)} collective-permute-done((bf16[2,128,1152]{2,1,0:T(8,128)(2,1)S(1)}, bf16[2,128,1152]{2,1,0:T(8,128)(2,1)S(1)}, u32[]{:S(2)}, u32[]{:S(2)}) %collective-permute-start.4) | collective-permute-done | bytes 589856 | tf_op jit(solution)/shard_map/ppermute | solution.py:45
  57.3 15.7 %all-gather.5.cloned.1.call-done = bf16[1152,2304]{1,0:T(8,128)(2,1)} async-done(((bf16[72,2304]{1,0:T(8,128)(2,1)}), bf16[1152,2304]{1,0:T(8,128)(2,1)}) %all-gather.5.cloned.1.call-update) | async-done | bytes 5308432 | tf_op jit(solution)/shard_map/all_gather | solution.py:464
  85.7 7.3 %shard_map.244 = (bf16[2,128,576]{2,1,0:T(8,128)(2,1)S(1)}, bf16[2,128,576]{2,1,0:T(8,128)(2,1)S(1)}) custom-call(bf16[2,128,1728]{2,1,0:T(8,128)(2,1)S(1)} %bitcast.327, bf16[2,128,1728]{2,1,0:T(8,128)(2,1)S(1)} %bitcast.325), custom_call_target="tpu_custom_call" | custom-call | flops 301989888 | bytes 1769472 | tf_op jit(solution)/shard_map/pallas_call | solution.py:141
  96.9 14.0 %collective-permute-done.5 = bf16[2,128,1152]{2,1,0:T(8,128)(2,1)S(1)} collective-permute-done((bf16[2,128,1152]{2,1,0:T(8,128)(2,1)S(1)}, bf16[2,128,1152]{2,1,0:T(8,128)(2,1)S(1)}, u32[]{:S(2)}, u32[]{:S(2)}) %collective-permute-start.5) | collective-permute-done | bytes 589856 | tf_op jit(solution)/shard_map/ppermute | solution.py:45
  123.3 7.5 %collective-permute-done.6 = bf16[2,128,1152]{2,1,0:T(8,128)(2,1)S(1)} collective-permute-done((bf16[2,128,1152]{2,1,0:T(8,128)(2,1)S(1)}, bf16[2,128,1152]{2,1,0:T(8,128)(2,1)S(1)}, u32[]{:S(2)}, u32[]{:S(2)}) %collective-permute-start.6) | collective-permute-done | bytes 589856 | tf_op jit(solution)/shard_map/ppermute | solution.py:45
  130.8 42.5 %all-gather.7.cloned.1.call-done = bf16[1152,4608]{1,0:T(8,128)(2,1)} async-done(((bf16[72,4608]{1,0:T(8,128)(2,1)}), bf16[1152,4608]{1,0:T(8,128)(2,1)}) %all-gather.7.cloned.1.call-update) | async-done | bytes 10616848 | tf_op jit(solution)/shard_map/all_gather | solution.py:464
  173.3 5.9 multiply_convert_fusion.2
  187.6 8.9 %collective-permute-done.7 = bf16[2,128,1152]{2,1,0:T(8,128)(2,1)S(1)} collective-permute-done((bf16[2,128,1152]{2,1,0:T(8,128)(2,1)S(1)}, bf16[2,128,1152]{2,1,0:T(8,128)(2,1)S(1)}, u32[]{:S(2)}, u32[]{:S(2)}) %collective-permute-start.7) | collective-permute-done | bytes 589856 | tf_op jit(solution)/shard_map/ppermute | solution.py:45
  208.1 19.7 %all-to-all-done = bf16[2,128,1152]{2,0,1:T(2,128)(2,1)S(1)} async-done(((bf16[2,128,1152]{2,0,1:T(2,128)(2,1)}), bf16[2,128,1152]{2,0,1:T(2,128)(2,1)S(1)}, u32[]{:S(2)}, u32[]{:S(2)}) %all-to-all-start) | async-done | bytes 589856 | tf_op jit(solution)/shard_map/all_to_all | solution.py:453
  234.0 7.9 %all-gather.9.cloned.1.call-done = bf16[1152,2304]{1,0:T(8,128)(2,1)} async-done(((bf16[72,2304]{1,0:T(8,128)(2,1)}), bf16[1152,2304]{1,0:T(8,128)(2,1)}) %all-gather.9.cloned.1.call-update) | async-done | bytes 5308432 | tf_op jit(solution)/shard_map/all_gather | solution.py:464
  261.6 8.5 %collective-permute-done.9 = bf16[32,8,1152]{2,1,0:T(8,128)(2,1)S(1)} collective-permute-done((bf16[32,8,1152]{2,1,0:T(8,128)(2,1)S(1)}, bf16[32,8,1152]{2,1,0:T(8,128)(2,1)S(1)}, u32[]{:S(2)}, u32[]{:S(2)}) %collective-permute-start.9) | collective-permute-done | bytes 589856 | tf_op jit(solution)/shard_map/ppermute | solution.py:45
  278.4 54.0 %all-gather.11.cloned.1.call-done = bf16[1152,4608]{1,0:T(8,128)(2,1)} async-done(((bf16[72,4608]{1,0:T(8,128)(2,1)}), bf16[1152,4608]{1,0:T(8,128)(2,1)}) %all-gather.11.cloned.1.call-update) | async-done | bytes 10616848 | tf_op jit(solution)/shard_map/all_gather | solution.py:464
  355.7 10.4 %shard_map.247 = bf16[1152,4608]{1,0:T(8,128)(2,1)} custom-call(bf16[256,1152]{1,0:T(8,128)(2,1)S(1)} %fusion.239.refs_0_, bf16[256,1152]{1,0:T(8,128)(2,1)} %bitcast.32.refs_1_, bf16[256,2304]{1,0:T(8,128)(2,1)S(1)} %fusion.119.refs_2_, bf16[256,2304]{1,0:T(8,128)(2,1)S(1)} %fusion.126.refs_3_, bf16[256,1152]{1,0:T(8,128)(2,1)S(1)} %copy-done.12, ...), custom_call_target="tpu_custom_call" | custom-call | flops 5435817984 | bytes 17694720 | tf_op jit(solution)/shard_map/pallas_call | solution.py:185
  372.5 7.1 collective-permute-done.11
  379.6 7.3 multiply_reduce_fusion.6
  396.2 7.3 %collective-permute-done.14 = bf16[32,8,1152]{2,1,0:T(8,128)(2,1)S(1)} collective-permute-done((bf16[32,8,1152]{2,1,0:T(8,128)(2,1)S(1)}, bf16[32,8,1152]{2,1,0:T(8,128)(2,1)S(1)}, u32[]{:S(2)}, u32[]{:S(2)}) %collective-permute-start.14) | collective-permute-done | bytes 589856 | tf_op jit(solution)/shard_map/ppermute | solution.py:45
  404.3 5.5 shard_map.249
  413.7 5.4 shard_map.250
  419.1 7.0 collective-permute-done.15
  442.6 9.1 %all-to-all-done.3 = bf16[32,8,1152]{2,1,0:T(8,128)(2,1)S(1)} async-done(((bf16[32,8,1152]{2,1,0:T(8,128)(2,1)}), bf16[32,8,1152]{2,1,0:T(8,128)(2,1)S(1)}, u32[]{:S(2)}, u32[]{:S(2)}) %all-to-all-start.3) | async-done | bytes 589856 | tf_op jit(solution)/shard_map/all_to_all | solution.py:459
  458.5 5.5 fusion.105.refs_2_
  464.0 8.3 %collective-permute-done.17 = bf16[2,128,1152]{2,1,0:T(8,128)(2,1)S(1)} collective-permute-done((bf16[2,128,1152]{2,1,0:T(8,128)(2,1)S(1)}, bf16[2,128,1152]{2,1,0:T(8,128)(2,1)S(1)}, u32[]{:S(2)}, u32[]{:S(2)}) %collective-permute-start.17) | collective-permute-done | bytes 589856 | tf_op jit(solution)/shard_map/ppermute | solution.py:45
  484.9 9.4 %shard_map.251 = (bf16[1152,2304]{1,0:T(8,128)(2,1)}, bf16[1152,2304]{1,0:T(8,128)(2,1)}) custom-call(bf16[256,1152]{1,0:T(8,128)(2,1)S(1)} %bitcast.332, bf16[256,1152]{1,0:T(8,128)(2,1)S(1)} %bitcast.345, bf16[256,2304]{1,0:T(8,128)(2,1)S(1)} %fusion.105.refs_2_, bf16[256,2304]{1,0:T(8,128)(2,1)S(1)} %fusion.112.refs_3_, bf16[256,1152]{1,0:T(8,128)(2,1)S(1)} %bitcast.336, ...), custom_call_target="tpu_custom_call" | custom-call | flops 5435817984 | bytes 17694720 | tf_op jit(solution)/shard_map/pallas_call | solution.py:185
  532.2 10.7 %shard_map.252 = (bf16[2,128,1728]{2,1,0:T(8,128)(2,1)S(1)}, bf16[2,128,1728]{2,1,0:T(8,128)(2,1)S(1)}) custom-call(bf16[2,128,1728]{2,1,0:T(8,128)(2,1)S(1)} %bitcast.328, bf16[2,128,1728]{2,1,0:T(8,128)(2,1)S(1)} %bitcast.326, bf16[2,128,576]{2,1,0:T(8,128)(2,1)S(1)} %bitcast.340, bf16[2,128,576]{2,1,0:T(8,128)(2,1)S(1)} %bitcast.341), custom_call_target="tpu_custom_call" | custom-call | flops 905969664 | bytes 2359296 | tf_op jit(solution)/shard_map/pallas_call | solution.py:141
  555.4 6.5 collective-permute-done.27
  571.4 37.1 %shard_map.254 = f32[108,128]{1,0:T(8,128)} custom-call(f32[108,128]{1,0:T(8,128)} %pad_maximum_fusion.5.value), custom_call_target="tpu_custom_call" | custom-call | tf_op jit(solution)/shard_map/pallas_call | solution.py:317
  622.1 12.0 %collective-permute-done.40 = bf16[1,1,1,72,2304]{4,3,2,1,0:T(8,128)(2,1)S(1)} collective-permute-done((bf16[1,1,1,72,2304]{4,3,2,1,0:T(8,128)(2,1)S(1)}, bf16[1,1,1,72,2304]{4,3,2,1,0:T(8,128)(2,1)S(1)}, u32[]{:S(2)}, u32[]{:S(2)}) %collective-permute-start.40) | collective-permute-done | bytes 331808 | tf_op jit(solution)/shard_map/ppermute | solution.py:228
  640.3 20.1 %collective-permute-done.36 = bf16[1,2,1,72,576]{4,3,2,1,0:T(8,128)(2,1)S(1)} collective-permute-done((bf16[1,2,1,72,576]{4,3,2,1,0:T(8,128)(2,1)S(1)}, bf16[1,2,1,72,576]{4,3,2,1,0:T(8,128)(2,1)S(1)}, u32[]{:S(2)}, u32[]{:S(2)}) %collective-permute-start.36) | collective-permute-done | bytes 165920 | tf_op jit(solution)/shard_map/ppermute | solution.py:228
  660.5 6.4 collective-permute-start.37
  676.4 17.4 %collective-permute-done.31 = bf16[4,1,1,72,1728]{4,3,2,1,0:T(8,128)(2,1)S(1)} collective-permute-done((bf16[4,1,1,72,1728]{4,3,2,1,0:T(8,128)(2,1)S(1)}, bf16[4,1,1,72,1728]{4,3,2,1,0:T(8,128)(2,1)S(1)}, u32[]{:S(2)}, u32[]{:S(2)}) %collective-permute-start.31) | collective-permute-done | bytes 995360 | tf_op jit(solution)/shard_map/ppermute | solution.py:45
  (595 shorter events, 305.6 us)
Async XLA Ops:
  7.2 65.8 %all-gather.5.cloned.1.call-start = ((), (), s32[]{:S(2)}) async-start(), calls=%async_computation.6 | async-start | bytes 5640192 | tf_op jit(solution)/shard_map/all_gather | solution.py:464
  10.4 162.9 %all-gather.7.cloned.1.call-start = ((), (), s32[]{:S(2)}) async-start(), calls=%async_computation.7 | async-start | bytes 11280384 | tf_op jit(solution)/shard_map/all_gather | solution.py:464
  11.4 230.5 %all-gather.9.cloned.1.call-start = ((), (), s32[]{:S(2)}) async-start(), calls=%async_computation.8 | async-start | bytes 5640192 | tf_op jit(solution)/shard_map/all_gather | solution.py:464
  12.8 319.6 %all-gather.11.cloned.1.call-start = ((), (), s32[]{:S(2)}) async-start(), calls=%async_computation.9 | async-start | bytes 11280384 | tf_op jit(solution)/shard_map/all_gather | solution.py:464
  95.4 15.5 %collective-permute-start.5 = (bf16[2,128,1152]{2,1,0:T(8,128)(2,1)S(1)}, bf16[2,128,1152]{2,1,0:T(8,128)(2,1)S(1)}, u32[]{:S(2)}, u32[]{:S(2)}) collective-permute-start(bf16[2,128,1152]{2,1,0:T(8,128)(2,1)S(1)} %convolution_convert_fusion.1), channel_id=1, source_target_pairs={{0,1},{1,0},{2,3},{3,2},{4,5},{5,4},{6,7},{7,6},{8,9},{9,8},{10,11... | collective-permute-start | bytes 1769480 | tf_op jit(solution)/shard_map/ppermute | solution.py:45
  119.3 79.9 %all-to-all-start.2 = ((bf16[2,128,1152]{2,0,1:T(2,128)(2,1)}), bf16[2,128,1152]{2,0,1:T(2,128)(2,1)S(1)}, u32[]{:S(2)}, u32[]{:S(2)}) async-start(bf16[2,128,1152]{2,0,1:T(2,128)(2,1)} %copy.284), calls=%async_computation.2 | async-start | bytes 1179648 | tf_op jit(solution)/shard_map/all_to_all | solution.py:453
  180.9 15.6 %collective-permute-start.7 = (bf16[2,128,1152]{2,1,0:T(8,128)(2,1)S(1)}, bf16[2,128,1152]{2,1,0:T(8,128)(2,1)S(1)}, u32[]{:S(2)}, u32[]{:S(2)}) collective-permute-start(bf16[2,128,1152]{2,1,0:T(8,128)(2,1)S(1)} %bitcast.413), channel_id=1, source_target_pairs={{0,1},{1,0},{2,3},{3,2},{4,5},{5,4},{6,7},{7,6},{8,9},{9,8},{10,11... | collective-permute-start | bytes 1769480 | tf_op jit(solution)/shard_map/ppermute | solution.py:45
  199.2 28.6 %all-to-all-start = ((bf16[2,128,1152]{2,0,1:T(2,128)(2,1)}), bf16[2,128,1152]{2,0,1:T(2,128)(2,1)S(1)}, u32[]{:S(2)}, u32[]{:S(2)}) async-start(bf16[2,128,1152]{2,0,1:T(2,128)(2,1)} %copy.195), calls=%async_computation | async-start | bytes 1179648 | tf_op jit(solution)/shard_map/all_to_all | solution.py:453
  229.9 16.5 %collective-permute-start.8 = (bf16[32,8,1152]{2,1,0:T(8,128)(2,1)}, bf16[32,8,1152]{2,1,0:T(8,128)(2,1)S(1)}, u32[]{:S(2)}, u32[]{:S(2)}) collective-permute-start(bf16[32,8,1152]{2,1,0:T(8,128)(2,1)} %add_convert_fusion.11), channel_id=1, source_target_pairs={{0,1},{1,0},{2,3},{3,2},{4,5},{5,4},{6,7},{7,6},{8,9},{9,8},{10,11... | collective-permute-start | bytes 1769480 | tf_op jit(solution)/shard_map/ppermute | solution.py:45
  232.3 112.1 %collective-permute-start.12 = (bf16[32,8,1152]{2,1,0:T(8,128)(2,1)}, bf16[32,8,1152]{2,1,0:T(8,128)(2,1)}, u32[]{:S(2)}, u32[]{:S(2)}) collective-permute-start(bf16[32,8,1152]{2,1,0:T(8,128)(2,1)} %fusion.162), channel_id=1, source_target_pairs={{0,1},{1,0},{2,3},{3,2},{4,5},{5,4},{6,7},{7,6},{8,9},{9,8},{10,11... | collective-permute-start | bytes 1769480 | tf_op jit(solution)/shard_map/ppermute | solution.py:45
  254.7 15.5 %collective-permute-start.9 = (bf16[32,8,1152]{2,1,0:T(8,128)(2,1)S(1)}, bf16[32,8,1152]{2,1,0:T(8,128)(2,1)S(1)}, u32[]{:S(2)}, u32[]{:S(2)}) collective-permute-start(bf16[32,8,1152]{2,1,0:T(8,128)(2,1)S(1)} %convolution_convert_fusion), channel_id=1, source_target_pairs={{0,1},{1,0},{2,3},{3,2},{4,5},{5,4},{6,7},{7,6},{8,9},{9,8},{10,11... | collective-permute-start | bytes 1769480 | tf_op jit(solution)/shard_map/ppermute | solution.py:45
  276.9 64.2 %collective-permute-start.10 = (bf16[32,8,1152]{2,1,0:T(8,128)(2,1)}, bf16[32,8,1152]{2,1,0:T(8,128)(2,1)}, u32[]{:S(2)}, u32[]{:S(2)}) collective-permute-start(bf16[32,8,1152]{2,1,0:T(8,128)(2,1)} %add_convert_fusion.10), channel_id=1, source_target_pairs={{0,1},{1,0},{2,3},{3,2},{4,5},{5,4},{6,7},{7,6},{8,9},{9,8},{10,11... | collective-permute-start | bytes 1769480 | tf_op jit(solution)/shard_map/ppermute | solution.py:45
  351.1 16.5 %collective-permute-start.13 = (bf16[32,8,1152]{2,1,0:T(8,128)(2,1)}, bf16[32,8,1152]{2,1,0:T(8,128)(2,1)}, u32[]{:S(2)}, u32[]{:S(2)}) collective-permute-start(bf16[32,8,1152]{2,1,0:T(8,128)(2,1)} %fusion.96), channel_id=1, source_target_pairs={{0,1},{1,0},{2,3},{3,2},{4,5},{5,4},{6,7},{7,6},{8,9},{9,8},{10,11... | collective-permute-start | bytes 1769480 | tf_op jit(solution)/shard_map/ppermute | solution.py:45
  355.2 24.4 %collective-permute-start.11 = (bf16[32,8,1152]{2,1,0:T(8,128)(2,1)}, bf16[32,8,1152]{2,1,0:T(8,128)(2,1)}, u32[]{:S(2)}, u32[]{:S(2)}) collective-permute-start(bf16[32,8,1152]{2,1,0:T(8,128)(2,1)} %fusion.93), channel_id=1, source_target_pairs={{0,1},{1,0},{2,3},{3,2},{4,5},{5,4},{6,7},{7,6},{8,9},{9,8},{10,11... | collective-permute-start | bytes 1769480 | tf_op jit(solution)/shard_map/ppermute | solution.py:45
  432.4 19.2 %all-to-all-start.3 = ((bf16[32,8,1152]{2,1,0:T(8,128)(2,1)}), bf16[32,8,1152]{2,1,0:T(8,128)(2,1)S(1)}, u32[]{:S(2)}, u32[]{:S(2)}) async-start(bf16[32,8,1152]{2,1,0:T(8,128)(2,1)} %add_convert_fusion.9), calls=%async_computation.3 | async-start | bytes 1179648 | tf_op jit(solution)/shard_map/all_to_all | solution.py:459
  436.2 276.0 %reduce-scatter.3.cloned.1.call-start = ((), (), s32[]{:S(2)}) async-start(), calls=%async_computation.10 | async-start | bytes 5640192 | tf_op jit(solution)/shard_map/reduce_scatter | solution.py:468
  451.7 51.9 %all-to-all-start.1 = ((bf16[32,8,1152]{2,1,0:T(8,128)(2,1)}), bf16[32,8,1152]{2,1,0:T(8,128)(2,1)S(1)}, u32[]{:S(2)}, u32[]{:S(2)}) async-start(bf16[32,8,1152]{2,1,0:T(8,128)(2,1)} %get-tuple-element.218), calls=%async_computation.1 | async-start | bytes 1179648 | tf_op jit(solution)/shard_map/all_to_all | solution.py:459
  456.2 264.6 %reduce-scatter.5.cloned.1.call-start = ((), (), s32[]{:S(2)}) async-start(), calls=%async_computation.11 | async-start | bytes 11280384 | tf_op jit(solution)/shard_map/reduce_scatter | solution.py:468
  456.9 15.4 %collective-permute-start.17 = (bf16[2,128,1152]{2,1,0:T(8,128)(2,1)S(1)}, bf16[2,128,1152]{2,1,0:T(8,128)(2,1)S(1)}, u32[]{:S(2)}, u32[]{:S(2)}) collective-permute-start(bf16[2,128,1152]{2,1,0:T(8,128)(2,1)S(1)} %multiply_convert_fusion.5), channel_id=1, source_target_pairs={{0,1},{1,0},{2,3},{3,2},{4,5},{5,4},{6,7},{7,6},{8,9},{9,8},{10,11... | collective-permute-start | bytes 1769480 | tf_op jit(solution)/shard_map/ppermute | solution.py:45
  515.9 27.0 %collective-permute-start.26 = (bf16[1,2,1,72,2304]{4,3,2,1,0:T(8,128)(2,1)}, bf16[1,2,1,72,2304]{4,3,2,1,0:T(8,128)(2,1)}, u32[]{:S(2)}, u32[]{:S(2)}) collective-permute-start(bf16[1,2,1,72,2304]{4,3,2,1,0:T(8,128)(2,1)} %constant_dynamic-slice_fusion.9), channel_id=1, source_target_pairs={{0,8},{2,10},{4,12},{6,14},{8,16},{10,18},{12,20},{14,22},{16,24},... | collective-permute-start | bytes 1990664 | tf_op jit(solution)/shard_map/ppermute | solution.py:228
  530.5 39.0 %collective-permute-start.28 = (bf16[4,1,1,72,2304]{4,3,2,1,0:T(8,128)(2,1)S(1)}, bf16[4,1,1,72,2304]{4,3,2,1,0:T(8,128)(2,1)S(1)}, u32[]{:S(2)}, u32[]{:S(2)}) collective-permute-start(bf16[4,1,1,72,2304]{4,3,2,1,0:T(8,128)(2,1)S(1)} %constant_dynamic-slice_fusion.8), channel_id=1, source_target_pairs={{0,4},{2,6},{4,0},{6,2},{8,12},{10,14},{12,8},{14,10},{16,20},{18,... | collective-permute-start | bytes 3981320 | tf_op jit(solution)/shard_map/ppermute | solution.py:45
  550.0 19.4 %collective-permute-start.29 = (bf16[1,2,1,72,2304]{4,3,2,1,0:T(8,128)(2,1)S(1)}, bf16[1,2,1,72,2304]{4,3,2,1,0:T(8,128)(2,1)S(1)}, u32[]{:S(2)}, u32[]{:S(2)}) collective-permute-start(bf16[1,2,1,72,2304]{4,3,2,1,0:T(8,128)(2,1)S(1)} %add_convert_fusion.8), channel_id=1, source_target_pairs={{0,8},{2,10},{4,12},{6,14},{8,16},{10,18},{12,20},{14,22},{16,24},... | collective-permute-start | bytes 1990664 | tf_op jit(solution)/shard_map/ppermute | solution.py:228
  567.4 66.8 %collective-permute-start.35 = (bf16[4,2,1,72,576]{4,3,2,1,0:T(8,128)(2,1)}, bf16[4,2,1,72,576]{4,3,2,1,0:T(8,128)(2,1)}, u32[]{:S(2)}, u32[]{:S(2)}) collective-permute-start(bf16[4,2,1,72,576]{4,3,2,1,0:T(8,128)(2,1)} %constant_dynamic-slice_fusion.4), channel_id=1, source_target_pairs={{0,2},{2,0},{4,6},{6,4},{8,10},{10,8},{12,14},{14,12},{16,18},{18,... | collective-permute-start | bytes 1990664 | tf_op jit(solution)/shard_map/ppermute | solution.py:45
  568.9 98.0 %collective-permute-start.30 = (bf16[4,2,1,72,1728]{4,3,2,1,0:T(8,128)(2,1)}, bf16[4,2,1,72,1728]{4,3,2,1,0:T(8,128)(2,1)}, u32[]{:S(2)}, u32[]{:S(2)}) collective-permute-start(bf16[4,2,1,72,1728]{4,3,2,1,0:T(8,128)(2,1)} %constant_dynamic-slice_fusion.7), channel_id=1, source_target_pairs={{0,2},{2,0},{4,6},{6,4},{8,10},{10,8},{12,14},{14,12},{16,18},{18,... | collective-permute-start | bytes 5971976 | tf_op jit(solution)/shard_map/ppermute | solution.py:45
  611.4 26.5 %collective-permute-start.43 = (bf16[1,2,1,72,2304]{4,3,2,1,0:T(8,128)(2,1)S(1)}, bf16[1,2,1,72,2304]{4,3,2,1,0:T(8,128)(2,1)S(1)}, u32[]{:S(2)}, u32[]{:S(2)}) collective-permute-start(bf16[1,2,1,72,2304]{4,3,2,1,0:T(8,128)(2,1)S(1)} %add_convert_fusion.7), channel_id=1, source_target_pairs={{0,8},{2,10},{4,12},{6,14},{8,16},{10,18},{12,20},{14,22},{16,24},... | collective-permute-start | bytes 1990664 | tf_op jit(solution)/shard_map/ppermute | solution.py:228
  613.3 20.8 %collective-permute-start.40 = (bf16[1,1,1,72,2304]{4,3,2,1,0:T(8,128)(2,1)S(1)}, bf16[1,1,1,72,2304]{4,3,2,1,0:T(8,128)(2,1)S(1)}, u32[]{:S(2)}, u32[]{:S(2)}) collective-permute-start(bf16[1,1,1,72,2304]{4,3,2,1,0:T(8,128)(2,1)S(1)} %constant_dynamic-slice_fusion.1), channel_id=1, source_target_pairs={{0,8},{2,10},{4,12},{6,14},{8,16},{10,18},{12,20},{14,22},{16,24},... | collective-permute-start | bytes 995336 | tf_op jit(solution)/shard_map/ppermute | solution.py:228
  634.2 37.0 %collective-permute-start.41 = (bf16[1,1,1,72,2304]{4,3,2,1,0:T(8,128)(2,1)S(1)}, bf16[1,1,1,72,2304]{4,3,2,1,0:T(8,128)(2,1)S(1)}, u32[]{:S(2)}, u32[]{:S(2)}) collective-permute-start(bf16[1,1,1,72,2304]{4,3,2,1,0:T(8,128)(2,1)S(1)} %add_convert_fusion.14), channel_id=1, source_target_pairs={{0,8},{2,10},{4,12},{6,14},{8,16},{10,18},{12,20},{14,22},{16,24},... | collective-permute-start | bytes 995336 | tf_op jit(solution)/shard_map/ppermute | solution.py:228
  635.8 24.6 %collective-permute-start.36 = (bf16[1,2,1,72,576]{4,3,2,1,0:T(8,128)(2,1)S(1)}, bf16[1,2,1,72,576]{4,3,2,1,0:T(8,128)(2,1)S(1)}, u32[]{:S(2)}, u32[]{:S(2)}) collective-permute-start(bf16[1,2,1,72,576]{4,3,2,1,0:T(8,128)(2,1)S(1)} %constant_dynamic-slice_fusion.3), channel_id=1, source_target_pairs={{0,8},{2,10},{4,12},{6,14},{8,16},{10,18},{12,20},{14,22},{16,24},... | collective-permute-start | bytes 497672 | tf_op jit(solution)/shard_map/ppermute | solution.py:228
  638.1 37.4 %collective-permute-start.44 = (bf16[1,1,1,72,2304]{4,3,2,1,0:T(8,128)(2,1)S(1)}, bf16[1,1,1,72,2304]{4,3,2,1,0:T(8,128)(2,1)S(1)}, u32[]{:S(2)}, u32[]{:S(2)}) collective-permute-start(bf16[1,1,1,72,2304]{4,3,2,1,0:T(8,128)(2,1)S(1)} %constant_dynamic-slice_fusion), channel_id=1, source_target_pairs={{0,4},{2,6},{4,0},{6,2},{8,12},{10,14},{12,8},{14,10},{16,20},{18,... | collective-permute-start | bytes 995336 | tf_op jit(solution)/shard_map/ppermute | solution.py:45
  669.1 24.7 %collective-permute-start.31 = (bf16[4,1,1,72,1728]{4,3,2,1,0:T(8,128)(2,1)S(1)}, bf16[4,1,1,72,1728]{4,3,2,1,0:T(8,128)(2,1)S(1)}, u32[]{:S(2)}, u32[]{:S(2)}) collective-permute-start(bf16[4,1,1,72,1728]{4,3,2,1,0:T(8,128)(2,1)S(1)} %constant_dynamic-slice_fusion.6), channel_id=1, source_target_pairs={{0,4},{2,6},{4,0},{6,2},{8,12},{10,14},{12,8},{14,10},{16,20},{18,... | collective-permute-start | bytes 2985992 | tf_op jit(solution)/shard_map/ppermute | solution.py:45
  671.3 25.5 %collective-permute-start.42 = (bf16[1,1,1,72,2304]{4,3,2,1,0:T(8,128)(2,1)S(1)}, bf16[1,1,1,72,2304]{4,3,2,1,0:T(8,128)(2,1)S(1)}, u32[]{:S(2)}, u32[]{:S(2)}) collective-permute-start(bf16[1,1,1,72,2304]{4,3,2,1,0:T(8,128)(2,1)S(1)} %add_convert_fusion.13), channel_id=1, source_target_pairs={{0,8},{2,10},{4,12},{6,14},{8,16},{10,18},{12,20},{14,22},{16,24},... | collective-permute-start | bytes 995336 | tf_op jit(solution)/shard_map/ppermute | solution.py:228
  675.1 28.9 %collective-permute-start.38 = (bf16[1,2,1,72,576]{4,3,2,1,0:T(8,128)(2,1)S(1)}, bf16[1,2,1,72,576]{4,3,2,1,0:T(8,128)(2,1)S(1)}, u32[]{:S(2)}, u32[]{:S(2)}) collective-permute-start(bf16[1,2,1,72,576]{4,3,2,1,0:T(8,128)(2,1)S(1)} %add_convert_fusion.18), channel_id=1, source_target_pairs={{0,8},{2,10},{4,12},{6,14},{8,16},{10,18},{12,20},{14,22},{16,24},... | collective-permute-start | bytes 497672 | tf_op jit(solution)/shard_map/ppermute | solution.py:228
  (147 other events, 1435.7 us)
Sparse Core Ops, SparseCore 0:
  10.8 62.2 all-gather.4
  75.9 97.3 all-gather.6
  176.1 65.8 all-gather.8
  244.6 87.6 all-gather.10
  441.2 84.5 reduce-scatter.2
  529.7 140.2 reduce-scatter.4

commit v3 on v2

--- a/solution.py
+++ b/solution.py
@@ -201,59 +201,6 @@
     return lax.optimization_barrier(values)
 
 
-class GradScatter:
-    def __init__(self, grad_w, order):
-        self.size, me = lax.axis_size("dp"), lax.axis_index("dp")
-        ring = self.size // 4
-        self.value = grad_w.reshape(ring, 2, 2, -1, grad_w.shape[1])
-        self.at = (me // 4, (me // 2) % 2, me % 2)
-        self.order = list(order)
-        self.wait = None
-        self.begin()
-
-    def pick(self, axis, index):
-        return lax.dynamic_slice_in_dim(self.value, index, 1, axis)
-
-    def begin(self):
-        axis = self.order[0]
-        count, at = self.value.shape[axis], self.at[axis]
-        if axis:
-            self.wait = swap(self.pick(axis, 1 - at), "dp", 3 - axis, self.size)
-        else:
-            self.left = count - 1
-            self.hop(self.pick(0, lax.rem(at + count - 1, count)))
-
-    def hop(self, total):
-        links = [(i, (i + 4) % self.size) for i in range(self.size)]
-        self.wait = lax.ppermute(total, "dp", links)
-
-    def step(self, value=None):
-        if not self.order:
-            return value
-        if value is not None:
-            value, self.wait = tie(value, self.wait)
-        axis = self.order[0]
-        at = self.at[axis]
-        if axis == 0:
-            self.left -= 1
-            at = lax.rem(at + self.left, self.value.shape[0])
-        total = self.pick(axis, at).astype(f32) + self.wait.astype(f32)
-        if axis == 0 and self.left:
-            self.hop(total.astype(bf16))
-            return value
-        self.order.pop(0)
-        self.value = total
-        if self.order:
-            self.value = total.astype(bf16)
-            self.begin()
-        return value
-
-    def finish(self):
-        while self.order:
-            self.step()
-        return self.value.reshape(-1, self.value.shape[-1])
-
-
 class AllSum:
     def __init__(self, value):
         self.value = value
@@ -285,48 +232,224 @@
         return self.value
 
 
-def all_sum_kernel(pairs, value, out, slots, landed, send_sem, recv_sem):
-    barrier = pltpu.get_barrier_semaphore()
-    partners = [{axis: lax.axis_index(axis) ^ stride} for axis, stride in pairs]
-    for partner in partners:
-        pl.semaphore_signal(barrier, inc=1, device_id=partner, device_id_type=MESH)
-    pl.semaphore_wait(barrier, len(partners))
-    slots[0] = value[...]
-    for k, partner in enumerate(partners):
-        copy = pltpu.make_async_remote_copy(
-            src_ref=slots.at[k],
-            dst_ref=landed.at[k],
-            send_sem=send_sem.at[k],
-            recv_sem=recv_sem.at[k],
-            device_id=partner,
-            device_id_type=MESH,
-        )
-        copy.start()
-        copy.wait()
-        slots[k + 1] = slots[k] + landed[k]
-    out[...] = slots[len(partners)]
-
-
-def all_sum_now(value):
-    pairs = [
+def exchange_pairs():
+    return [
         (axis, 1 << bit)
         for axis in ("tensor", "dp")
         for bit in range(lax.axis_size(axis).bit_length() - 1)
     ]
-    count = len(pairs)
-    return pl.pallas_call(
-        functools.partial(all_sum_kernel, pairs),
-        in_specs=[pl.BlockSpec(memory_space=pltpu.VMEM)],
-        out_specs=pl.BlockSpec(memory_space=pltpu.VMEM),
-        out_shape=jax.ShapeDtypeStruct(value.shape, f32),
-        scratch_shapes=[
-            pltpu.VMEM((count + 1,) + value.shape, f32),
-            pltpu.VMEM((count,) + value.shape, f32),
+
+
+class Scatter:
+    def __init__(self, grad, out, refs, flipped):
+        self.grad, self.out, self.flipped = grad, out, flipped
+        self.own, self.core_in, self.y_in, self.ring_in, self.own_sem, self.send_sem, self.recv_sem = refs
+        self.ring = grad.shape[0]
+        self.stages = self.ring + 2
+        self.chunks = self.send_sem.shape[1]
+        self.width = grad.shape[-1] // self.chunks
+        me, size = lax.axis_index("dp"), 4 * self.ring
+        self.me, self.at, self.y, self.core = me, me // 4, lax.rem(me // 2, 2), lax.rem(me, 2)
+        self.after, self.before = lax.rem(me + 4, size), lax.rem(me + size - 4, size)
+        self.pending = {}
+        self.load = None
+
+    @staticmethod
+    def scratch(ring, rows, cols):
+        chunks = cols // 384 if cols % 384 == 0 else 1
+        return [
+            pltpu.VMEM((ring, 2, rows, cols), bf16),
+            pltpu.VMEM((ring, 2, rows, cols), bf16),
+            pltpu.VMEM((ring, rows, cols), bf16),
+            pltpu.VMEM((ring - 1, 2, rows, cols), bf16),
+            pltpu.SemaphoreType.DMA,
+            pltpu.SemaphoreType.DMA((ring + 1, chunks)),
+            pltpu.SemaphoreType.DMA((ring + 1, chunks)),
+        ]
+
+    def begin(self):
+        self.load = pltpu.make_async_copy(self.grad.at[:, :, self.core], self.own, self.own_sem)
+        self.load.start()
+
+    def send(self, s, j, source, target, partner):
+        copy = pltpu.make_async_remote_copy(
+            src_ref=source, dst_ref=target, send_sem=self.send_sem.at[s, j], recv_sem=self.recv_sem.at[s, j],
+            device_id={"dp": partner}, device_id_type=MESH,
+        )
+        copy.start()
+        self.pending[s, j] = copy
+
+    def stage(self, s, j):
+        cols = pl.ds(j * self.width, self.width)
+        ring, y, at = self.ring, self.y, self.at
+        if s == 0:
+            source = self.grad.at[:, :, 1 - self.core, :, cols]
+            return self.send(s, j, source, self.core_in.at[:, :, :, cols], self.me ^ 1)
+        if self.load is not None:
+            self.load.wait()
+            self.load = None
+        self.pending[s - 1, j].wait_recv()
+        flipped = self.flipped(j)
+        if s == 1:
+            total = self.own[:, :, :, cols].astype(f32) + self.core_in[:, :, :, cols].astype(f32)
+            self.own[:, :, :, cols] = total.astype(bf16)
+        if not flipped:
+            if s == 1:
+                return self.send(s, j, self.own.at[:, 1 - y, :, cols], self.y_in.at[:, :, cols], self.me ^ 2)
+            h = s - 2
+            if h == 0:
+                total = self.own[:, y, :, cols].astype(f32) + self.y_in[:, :, cols].astype(f32)
+                self.y_in[:, :, cols] = total.astype(bf16)
+                source = self.y_in.at[lax.rem(at + ring - 1, ring), :, cols]
+            else:
+                total = self.y_in[lax.rem(at + ring - 1 - h, ring), :, cols].astype(f32)
+                total = total + self.ring_in[h - 1, 0, :, cols].astype(f32)
+                if h == ring - 1:
+                    self.out[:, cols] = total
+                    return None
+                self.ring_in[h - 1, 0, :, cols] = total.astype(bf16)
+                source = self.ring_in.at[h - 1, 0, :, cols]
+            return self.send(s, j, source, self.ring_in.at[h, 0, :, cols], self.after)
+        h = s - 1
+        if h == 0:
+            source = self.own.at[lax.rem(at + ring - 1, ring), :, :, cols]
+            return self.send(s, j, source, self.ring_in.at[h, :, :, cols], self.after)
+        if h < ring:
+            total = self.own[lax.rem(at + ring - 1 - h, ring), :, :, cols].astype(f32)
+            total = total + self.ring_in[h - 1, :, :, cols].astype(f32)
+            self.ring_in[h - 1, :, :, cols] = total.astype(bf16)
+            if h < ring - 1:
+                source = self.ring_in.at[h - 1, :, :, cols]
+                return self.send(s, j, source, self.ring_in.at[h, :, :, cols], self.after)
+            source = self.ring_in.at[h - 1, 1 - y, :, cols]
+            return self.send(s, j, source, self.y_in.at[0, :, cols], self.me ^ 2)
+        total = self.ring_in[ring - 2, y, :, cols].astype(f32)
+        self.out[:, cols] = total + self.y_in[0, :, cols].astype(f32)
+        return None
+
+    def finish(self):
+        for copy in self.pending.values():
+            copy.wait_send()
+
+
+class Pipeline:
+    def __init__(self, jobs):
+        self.jobs = jobs
+        self.queue = [(job, j) for job in jobs for j in range(job.chunks)]
+        self.flight = []
+        for job in jobs:
+            job.begin()
+
+    def tick(self):
+        for entry in self.flight:
+            job, j, s, age = entry
+            if age >= max(2 * s - 1, 1):
+                job.stage(s, j)
+                entry[2] += 1
+            entry[3] += 1
+        self.flight = [entry for entry in self.flight if entry[2] < entry[0].stages]
+        if self.queue:
+            job, j = self.queue.pop(0)
+            job.stage(0, j)
+            self.flight.append([job, j, 1, 1])
+        return bool(self.queue or self.flight)
+
+    def finish(self):
+        while self.tick():
+            pass
+        for job in self.jobs:
+            job.finish()
+
+
+class SmallSum:
+    def __init__(self, pairs, value, out, refs):
+        self.slots, self.landed, self.send_sem, self.recv_sem = refs
+        self.value, self.out, self.copies = value, out, []
+        self.partners = [{axis: lax.axis_index(axis) ^ stride} for axis, stride in pairs]
+        self.k = 0
+
+    @staticmethod
+    def scratch(count, shape):
+        return [
+            pltpu.VMEM((count + 1,) + shape, f32),
+            pltpu.VMEM((count,) + shape, f32),
             pltpu.SemaphoreType.DMA((count,)),
             pltpu.SemaphoreType.DMA((count,)),
-        ],
-        compiler_params=pltpu.CompilerParams(collective_id=0, has_side_effects=True),
-    )(value)
+        ]
+
+    def tick(self):
+        k, self.k = self.k, self.k + 1
+        if k > len(self.partners):
+            return False
+        if k == 0:
+            self.slots[0] = self.value[...]
+        else:
+            self.copies[k - 1].wait_recv()
+            self.slots[k] = self.slots[k - 1] + self.landed[k - 1]
+        if k == len(self.partners):
+            self.out[...] = self.slots[k]
+            return False
+        copy = pltpu.make_async_remote_copy(
+            src_ref=self.slots.at[k], dst_ref=self.landed.at[k],
+            send_sem=self.send_sem.at[k], recv_sem=self.recv_sem.at[k],
+            device_id=self.partners[k], device_id_type=MESH,
+        )
+        copy.start()
+        self.copies.append(copy)
+        return True
+
+    def finish(self):
+        while self.tick():
+            pass
+        for copy in self.copies:
+            copy.wait_send()
+
+
+def greet(partners):
+    barrier = pltpu.get_barrier_semaphore()
+    for partner in partners:
+        pl.semaphore_signal(barrier, inc=1, device_id=partner, device_id_type=MESH)
+    pl.semaphore_wait(barrier, len(partners))
+
+
+def tail_kernel(count, pairs, *refs):
+    grads, small = refs[:count], refs[count]
+    outs, small_out = refs[count + 1 : 2 * count + 1], refs[2 * count + 1]
+    scratch = refs[2 * count + 2 :]
+    jobs = [
+        Scatter(grads[i], outs[i], scratch[7 * i : 7 * i + 7], lambda j: j % 6 == 5)
+        for i in range(count)
+    ]
+    total = SmallSum(pairs, small, small_out, scratch[7 * count :])
+    greet(total.partners + [{"dp": jobs[0].after}, {"dp": jobs[0].before}])
+    pipeline = Pipeline(jobs)
+    total.tick()
+    for _ in range(len(pairs)):
+        pipeline.tick()
+        total.tick()
+    pipeline.finish()
+    total.finish()
+
+
+def tail(grads, small):
+    ring = lax.axis_size("dp") // 4
+    grads = [grad.reshape(ring, 2, 2, -1, grad.shape[1]) for grad in grads]
+    pairs = exchange_pairs()
+    anywhere, vmem = pl.BlockSpec(memory_space=pl.ANY), pl.BlockSpec(memory_space=pltpu.VMEM)
+    scratch = []
+    for grad in grads:
+        scratch += Scatter.scratch(ring, *grad.shape[3:])
+    return pl.pallas_call(
+        functools.partial(tail_kernel, len(grads), pairs),
+        in_specs=[anywhere] * len(grads) + [vmem],
+        out_specs=[vmem] * (len(grads) + 1),
+        out_shape=[jax.ShapeDtypeStruct(grad.shape[3:], f32) for grad in grads]
+        + [jax.ShapeDtypeStruct(small.shape, f32)],
+        scratch_shapes=scratch + SmallSum.scratch(len(pairs), small.shape),
+        compiler_params=pltpu.CompilerParams(
+            collective_id=0, has_side_effects=True, vmem_limit_bytes=56 << 20
+        ),
+    )(*grads, small)
 
 
 class Layer:
@@ -381,24 +504,30 @@
             out.append(attend_call(kernel, count // FRAMES, views, widths)[0][0])
         return out
 
-    def attention(self, stream, mod, weights):
+    def attention(self, stream, mod, weights, pump, hidden=None):
         inner = weights.shape[1] // 4
-        hidden = [self.flat(h) for h in gather_tokens(self.modulated(stream, mod, 0))]
+        if hidden is None:
+            hidden = gather_tokens(self.modulated(stream, mod, 0))
+        hidden = [self.flat(h) for h in hidden]
         w_qkv, w_proj = weights[:, : 3 * inner], weights[:, 3 * inner :]
         qkv = [dot(h, w_qkv).astype(bf16) for h in hidden]
         attended = self.attend(attend_kernel, [qkv], inner)
+        attended[-1] = pump(attended[-1])
         partial = [self.full(dot_nt(a, w_proj)) for a in attended]
         branch = scatter_tokens(partial)
+        branch = pump(branch)
         gated = self.by_row(mod[:, 2]) * branch
         return stream + gated, gated, (stream, branch, hidden, qkv, attended, w_qkv, w_proj)
 
-    def mlp(self, stream, mod, weights):
+    def mlp(self, stream, mod, weights, pump):
         inner = weights.shape[1] // 2
         hidden = [self.flat(h) for h in gather_tokens(self.modulated(stream, mod, 3))]
+        hidden[-1] = pump(hidden[-1])
         w_up, w_down = weights[:, :inner], weights[:, inner:]
         pre = [dot(h, w_up) for h in hidden]
         active = [gelu_tanh(p).astype(bf16) for p in pre]
         branch = scatter_tokens([self.full(dot_nt(a, w_down)) for a in active])
+        branch = pump(branch)
         gated = self.by_row(mod[:, 5]) * branch
         return stream + gated, gated, (stream, branch, hidden, pre, active, w_up, w_down)
 
@@ -459,13 +588,222 @@
     return lax.all_to_all(stream.astype(bf16), "dp", split_axis=0, concat_axis=1, tiled=True)
 
 
+def pack(first, second):
+    return jnp.concatenate([first.reshape(first.shape[0], -1), second.T], axis=1)
+
+
 def gather_weights(first, second):
-    packed = jnp.concatenate([first.reshape(first.shape[0], -1), second.T], axis=1)
-    return lax.all_gather(packed, "dp", axis=0, tiled=True)
-
-
-def scatter_grads(grad_w, first, second):
-    local = lax.psum_scatter(grad_w, "dp", scatter_dimension=0, tiled=True).astype(f32)
+    return lax.all_gather(pack(first, second), "dp", axis=0, tiled=True)
+
+
+def norm_rows(value):
+    centered = value - jnp.mean(value, axis=-1, keepdims=True)
+    return centered * lax.rsqrt(jnp.mean(centered * centered, axis=-1, keepdims=True) + epsilon)
+
+
+def head_kernel(
+    ring, clips, pairs, shard, small, video, out, small_out, hidden, other,
+    slots, landed_small, own_sem, send_sem, recv_sem, pair_send, pair_recv, x_send, x_recv,
+):
+    size, me = 4 * ring, lax.axis_index("dp")
+    tensor = lax.axis_index("tensor")
+    after, before = lax.rem(me + 4, size), lax.rem(me + size - 4, size)
+    beside, core = me ^ 2, me ^ 1
+    exchange = lax.axis_size("tensor") == 2
+    barrier = pltpu.get_barrier_semaphore()
+    partners = [{"dp": me ^ stride} for stride in pairs]
+    greeted = partners + [{"dp": after}, {"dp": before}]
+    if exchange:
+        greeted.append({"tensor": 1 - tensor})
+    for partner in greeted:
+        pl.semaphore_signal(barrier, inc=1, device_id=partner, device_id_type=MESH)
+    pl.semaphore_wait(barrier, len(greeted))
+    keep = pltpu.make_async_copy(shard, out.at[me], own_sem)
+    keep.start()
+    sent = []
+
+    def send(source, target, out_sem, in_sem, partner):
+        copy = pltpu.make_async_remote_copy(
+            src_ref=source, dst_ref=target, send_sem=out_sem, recv_sem=in_sem,
+            device_id=partner, device_id_type=MESH,
+        )
+        copy.start()
+        sent.append(copy)
+        return copy
+
+    def pass_on(source, place, slot, partner):
+        send(source, out.at[place], send_sem.at[slot], recv_sem.at[slot], {"dp": partner})
+
+    def landed(place, slot):
+        pltpu.make_async_remote_copy(
+            src_ref=out.at[place], dst_ref=out.at[place],
+            send_sem=send_sem.at[slot], recv_sem=recv_sem.at[slot],
+            device_id={"dp": core}, device_id_type=MESH,
+        ).wait_recv()
+
+    flying = []
+
+    def pair_step(k):
+        if k == 0:
+            slots[0] = small[...]
+        else:
+            flying[k - 1].wait_recv()
+            slots[k] = slots[k - 1] + landed_small[k - 1]
+        if k < len(partners):
+            flying.append(
+                send(slots.at[k], landed_small.at[k], pair_send.at[k], pair_recv.at[k], partners[k])
+            )
+
+    pair_step(0)
+    step = 1
+    for k in range(ring):
+        place = lax.rem(me + size - 4 * k, size)
+        if k:
+            landed(place, k - 1)
+        source = shard if k == 0 else out.at[place]
+        if k < ring - 1:
+            pass_on(source, place, k, after)
+        pass_on(source, place, ring + k, beside)
+        pass_on(source, place, 2 * ring + k, core)
+        if k:
+            place = lax.rem((me ^ 2) + size - 4 * (k - 1), size)
+            landed(place, ring + k - 1)
+            pass_on(out.at[place], place, 3 * ring + k - 1, core)
+        if step <= len(partners):
+            pair_step(step)
+            step += 1
+    while step <= len(partners):
+        pair_step(step)
+        step += 1
+    small_out[...] = slots[len(partners)]
+    if exchange:
+        rows = video.shape[0]
+        for r in range(rows):
+            clip = r % clips if rows % clips == 0 else lax.rem(me * rows + r, clips)
+            shift = slots[len(partners), pl.ds(6 * clip, 1), :]
+            scale = slots[len(partners), pl.ds(6 * clip + 1, 1), :]
+            normed = norm_rows(video[r].astype(f32))
+            hidden[r] = (normed * (1.0 + scale) + shift).astype(bf16)
+        swapped = send(hidden, other, x_send, x_recv, {"tensor": 1 - tensor})
+    place = lax.rem((me ^ 2) + size - 4 * (ring - 1), size)
+    landed(place, 2 * ring - 1)
+    pass_on(out.at[place], place, 4 * ring - 1, core)
+    for k in range(ring):
+        landed(lax.rem(core + size - 4 * k, size), 2 * ring + k)
+        landed(lax.rem((core ^ 2) + size - 4 * k, size), 3 * ring + k)
+    keep.wait()
+    if exchange:
+        swapped.wait_recv()
+    for copy in sent:
+        copy.wait_send()
+
+
+def head(shard, small, video, clips):
+    ring = lax.axis_size("dp") // 4
+    rows, cols = shard.shape
+    pairs = [1 << bit for bit in range(lax.axis_size("dp").bit_length() - 1)]
+    count = len(pairs)
+    vmem, anywhere = pl.BlockSpec(memory_space=pltpu.VMEM), pl.BlockSpec(memory_space=pl.ANY)
+    full, total, mine, other = pl.pallas_call(
+        functools.partial(head_kernel, ring, clips, pairs),
+        in_specs=[anywhere, vmem, vmem],
+        out_specs=[anywhere, vmem, vmem, vmem],
+        out_shape=[
+            jax.ShapeDtypeStruct((4 * ring, rows, cols), bf16),
+            jax.ShapeDtypeStruct(small.shape, f32),
+            jax.ShapeDtypeStruct(video.shape, bf16),
+            jax.ShapeDtypeStruct(video.shape, bf16),
+        ],
+        scratch_shapes=[
+            pltpu.VMEM((count + 1,) + small.shape, f32),
+            pltpu.VMEM((count,) + small.shape, f32),
+            pltpu.SemaphoreType.DMA,
+            pltpu.SemaphoreType.DMA((4 * ring,)),
+            pltpu.SemaphoreType.DMA((4 * ring,)),
+            pltpu.SemaphoreType.DMA((count,)),
+            pltpu.SemaphoreType.DMA((count,)),
+            pltpu.SemaphoreType.DMA,
+            pltpu.SemaphoreType.DMA,
+        ],
+        cost_estimate=pl.CostEstimate(flops=1 << 35, bytes_accessed=8 * ring * rows * cols, transcendentals=0),
+        compiler_params=pltpu.CompilerParams(
+            collective_id=1, has_side_effects=True, vmem_limit_bytes=32 << 20
+        ),
+    )(shard, small, video)
+    hidden = [mine, other] if lax.axis_size("tensor") == 2 else None
+    return full.reshape(4 * ring * rows, cols), total, hidden
+
+
+def assemble_kernel(ring, own, *refs):
+    hops, beside, core, out, sems = refs[: ring - 1], *refs[ring - 1 :]
+    size, me = 4 * ring, lax.axis_index("dp")
+    copies = []
+
+    def put(source, place):
+        copy = pltpu.make_async_copy(source, out.at[place], sems.at[len(copies)])
+        copy.start()
+        copies.append(copy)
+
+    for k in range(ring):
+        back = lambda device: lax.rem(device + size - 4 * k, size)
+        put(own if k == 0 else hops[k - 1], back(me))
+        put(beside.at[k], back(me ^ 2))
+        put(core.at[k], back(me ^ 1))
+        put(core.at[ring + k], back(me ^ 3))
+    for copy in copies:
+        copy.wait()
+
+
+class WeightGather:
+    def __init__(self, shard):
+        self.size = lax.axis_size("dp")
+        self.ring = self.size // 4
+        self.pieces, self.stage = [shard], 0
+        self.begin()
+
+    def begin(self):
+        if self.stage < self.ring - 1:
+            links = [(i, (i + 4) % self.size) for i in range(self.size)]
+            self.wait = lax.ppermute(self.pieces[-1], "dp", links)
+        elif self.stage == self.ring - 1:
+            self.column = jnp.stack(self.pieces)
+            self.wait = swap(self.column, "dp", 2, self.size)
+        else:
+            self.wait = swap(jnp.concatenate([self.column, self.pieces[-1]]), "dp", 1, self.size)
+
+    def step(self, value=None):
+        if self.stage > self.ring:
+            return value
+        if value is not None:
+            value, self.wait = tie(value, self.wait)
+        self.pieces.append(self.wait)
+        self.stage += 1
+        if self.stage <= self.ring:
+            self.begin()
+        return value
+
+    def finish(self):
+        while self.stage <= self.ring:
+            self.step()
+        rows, cols = self.pieces[0].shape
+        anywhere = pl.BlockSpec(memory_space=pl.ANY)
+        full = pl.pallas_call(
+            functools.partial(assemble_kernel, self.ring),
+            in_specs=[anywhere] * (self.ring + 2),
+            out_specs=pl.BlockSpec(memory_space=pltpu.VMEM),
+            out_shape=jax.ShapeDtypeStruct((self.size, rows, cols), bf16),
+            scratch_shapes=[pltpu.SemaphoreType.DMA((self.size,))],
+            compiler_params=pltpu.CompilerParams(vmem_limit_bytes=32 << 20),
+        )(*self.pieces)
+        return full.reshape(self.size * rows, cols)
+
+
+def scatter_grads(grad_w):
+    return lax.psum_scatter(grad_w, "dp", scatter_dimension=0, tiled=True)
+
+
+def unpack(local, first, second):
+    local = local.astype(f32)
     cut = local.shape[1] - second.shape[0]
     return local[:, :cut].reshape(first.shape), local[:, cut:].T
 
@@ -491,9 +829,7 @@
     spatial = Layer(rows, tokens, clips, True, me * rows)
     temporal = Layer(rows * dp, tokens // dp, clips, False, 0)
 
-    w_attn_s = gather_weights(qkv_spatial, proj_spatial)
     w_mlp_s = gather_weights(up_spatial, down_spatial)
-    w_attn_t = gather_weights(qkv_temporal, proj_temporal)
     w_mlp_t = gather_weights(up_temporal, down_temporal)
 
     share = adaln_spatial.shape[0]
@@ -502,16 +838,22 @@
     silu_low = silu_rows.astype(bf16)
     flat_s = adaln_spatial.reshape(share, -1)
     flat_t = adaln_temporal.reshape(share, -1)
-    mods = all_sum(jnp.stack([dot(silu_low, flat_s), dot(silu_low, flat_t)]), ("dp",))
-    mod_s = mods[0].reshape(clips, 6, width)
-    mod_t = mods[1].reshape(clips, 6, width)
-
+    mods = jnp.stack([dot(silu_low, flat_s), dot(silu_low, flat_t)]).reshape(-1, width)
+    w_attn_s, mods, hidden = head(pack(qkv_spatial, proj_spatial), mods, video_in, clips)
+
+    keep = lambda value: value
     stream0 = video_in.astype(f32)
-    s1, g1, kept1 = spatial.attention(stream0, mod_s, w_attn_s)
-    s2, g2, kept2 = spatial.mlp(s1, mod_s, w_mlp_s)
-    placed = to_places(s2)
-    s3, g3, kept3 = temporal.attention(placed, mod_t, w_attn_t)
-    s4, g4, kept4 = temporal.mlp(s3, mod_t, w_mlp_t)
+    shard, mods = tie(pack(qkv_temporal, proj_temporal), mods)
+    mod_s, mod_t = mods.reshape(2, clips, 6, width)
+    later = WeightGather(shard)
+    s1, g1, kept1 = spatial.attention(stream0, mod_s, w_attn_s, later.step, hidden)
+    s2, g2, kept2 = spatial.mlp(s1, mod_s, w_mlp_s, later.step)
+    placed = later.step(to_places(s2))
+    w_attn_t = later.finish()
+    placed, grad_output = tie(placed, grad_output)
+    grad = to_places(grad_output)
+    s3, g3, kept3 = temporal.attention(placed, mod_t, w_attn_t, keep)
+    s4, g4, kept4 = temporal.mlp(s3, mod_t, w_mlp_t, keep)
     video_out = to_frames(s4)
     squares = jnp.stack(
         [spatial.by_frame(v) for v in (s1, s2)]
@@ -520,31 +862,23 @@
         + [temporal.by_frame(v) for v in (g3, g4)]
     )
 
-    keep = lambda value: value
-    grad = to_places(grad_output)
     grad, dmod4, (gw4,) = temporal.mlp_back(grad, mod_t, kept4, False, keep)
-    grad_up_t, grad_down_t = scatter_grads(gw4, up_temporal, down_temporal)
+    own4 = scatter_grads(gw4)
     grad, dmod3, (gw3,) = temporal.attention_back(grad, mod_t, kept3, False, keep)
-    grad_qkv_t, grad_proj_t = scatter_grads(gw3, qkv_temporal, proj_temporal)
     early = AllSum(
         jnp.concatenate([dmod3.reshape(-1), dmod4.reshape(-1), squares.reshape(-1)]).reshape(-1, 128)
     )
     grad = early.step(to_frames(grad).astype(f32))
     grad, dmod2, gw2 = spatial.mlp_back(grad, mod_s, kept2, True, early.step)
-    chains = [GradScatter(gw2[0], (2, 1, 0)), GradScatter(gw2[1], (2, 0, 1))]
-
-    def pump(value):
-        turn = pump.turn
-        pump.turn += 1
-        value = early.step(value)
-        if turn != 1:
-            value = chains[0].step(value)
-        return chains[1].step(value)
-
-    pump.turn = 0
-    grad, dmod1, gw1 = spatial.attention_back(grad, mod_s, kept1, True, pump)
-    chains += [GradScatter(gw1[0], (2, 1, 0)), GradScatter(gw1[1], (2, 0, 1))]
-    late = all_sum_now(jnp.concatenate([dmod1.reshape(-1), dmod2.reshape(-1)]).reshape(-1, 128))
+    grad, own4, gw3 = tie(grad, own4, gw3)
+    own3 = scatter_grads(gw3)
+    grad_up_t, grad_down_t = unpack(own4, up_temporal, down_temporal)
+    grad_qkv_t, grad_proj_t = unpack(own3, qkv_temporal, proj_temporal)
+    grad, dmod1, (gw1,) = spatial.attention_back(grad, mod_s, kept1, False, early.step)
+    small = jnp.concatenate([dmod1.reshape(-1), dmod2.reshape(-1)]).reshape(-1, 128)
+    grad_up_s, down_s, own1, late = tail([*gw2, gw1], small)
+    grad_down_s = down_s.T
+    grad_qkv_s, grad_proj_s = unpack(own1, qkv_spatial, proj_spatial)
     late = late.reshape(2, clips, 3, width)
     dmod1, dmod2 = late[0], late[1]
     cut = clips * 3 * width
@@ -553,9 +887,6 @@
     dmod4 = flat_early[cut : 2 * cut].reshape(clips, 3, width)
     squares = flat_early[2 * cut :].reshape(8, FRAMES)
     frame_rms = jnp.sqrt(squares / (clips * PATCHES * width))
-    done = [chain.finish() for chain in chains]
-    grad_up_s, grad_down_s = done[0], done[1].T
-    grad_qkv_s, grad_proj_s = done[2].reshape(qkv_spatial.shape), done[3].T
     shift_grad = jnp.stack([d[:, 0] for d in (dmod1, dmod2, dmod3, dmod4)])
     silu_wide = silu_low.astype(f32)
 

time: 742 us -> 686 us (0.925)
  waiting for transfers between devices: 327 us -> 146 us
  Pallas kernels: 103 us -> 246 us
  starting transfers between devices: 81.1 us -> 49.8 us
  local copies, waits for them, and re-layouts: 46.5 us -> 68.2 us
  other arithmetic: 48.7 us -> 32.6 us
  matrix products: 108 us -> 117 us
    pallas_call x1 -> x3, Pallas kernels: 37.1 us -> 179 us  [the longest x1 109 us: tail(): pl.pallas_call(functools.partial(tail_kernel, len(grads), pairs), in_spec...]
    all_gather x4 -> x2, waiting for transfers between devices: 120 us -> 0.01 us  [gather_weights(): return lax.all_gather(pack(first, second), 'dp', axis=0, tiled=True)]
    ppermute x12 -> x3, waiting for transfers between devices: 48.5 us -> 12.4 us  [begin(): self.wait = lax.ppermute(self.pieces[-1], 'dp', links)]
    ppermute x33 -> x22, starting transfers between devices: 45.3 us -> 20.7 us  [swap(): return lax.ppermute(value, axis, [(i, i ^ stride) for i in range(size)])]
    ppermute x33 -> x22, waiting for transfers between devices: 129 us -> 106 us  [swap(): return lax.ppermute(value, axis, [(i, i ^ stride) for i in range(size)])]
    convert_element_type x19 -> x2, other arithmetic: 18.6 us -> 0.14 us  [unpack(): local = local.astype(f32)]
    unnamed x263 -> x266, local copies, waits for them, and re-layouts: 12.6 us -> 28.9 us
    ppermute x12 -> x3, starting transfers between devices: 19.3 us -> 3.53 us  [begin(): self.wait = lax.ppermute(self.pieces[-1], 'dp', links)]
  transfers between devices with their start and end apart: 55 -> 33, of which waited for: 30 -> 16; matrix products, arithmetic and copies ran while one was open for 23% -> 27% of each run, Pallas kernels for 13% -> 36%
where the time goes in v3:
time: 686 us; the launch traced here: 676 us
  Pallas kernels  246 us (36%)
  waiting for transfers between devices  146 us (21%)
  matrix products  117 us (17%)
  local copies, waits for them, and re-layouts  68.2 us (10%)
  starting transfers between devices  49.8 us (7%)
  other arithmetic  32.6 us (5%)
  between operations  16 us (2%)
    pallas_call x1, Pallas kernels, tail(): pl.pallas_call(functools.partial(tail_kernel, len(grads), pairs), in_spec...  109 us
    ppermute x22, waiting for transfers between devices, swap(): return lax.ppermute(value, axis, [(i, i ^ stride) for i in range(size)])  106 us
    pallas_call x1, Pallas kernels, head(): pl.pallas_call(functools.partial(head_kernel, ring, clips, pairs), in_spe...  67 us
    dot_general x18, matrix products, dot(): return jnp.dot(a, b, preferred_element_type=f32)  62.1 us
    dot_general x16, matrix products, dot_nt(): lax.dot_general(a, b, (((1,), (1,)), ((), ())), preferred_element_type=f32)  52.3 us
    pallas_call x6, Pallas kernels, attend_call(): pl.pallas_call(functools.partial(kernel, count, residue), grid=(rows,), i...  35.7 us
    pallas_call x4, Pallas kernels, weight_grad(): pl.pallas_call(functools.partial(weight_grad_kernel, count), grid=(width...  31.5 us
    unnamed x266, local copies, waits for them, and re-layouts  28.9 us
  transfers between devices with their start and end apart: 33, of which 16 were waited for; matrix products, arithmetic and copies ran while one was open for 27% of the time, Pallas kernels for 36%

profile of v3, /device:TPU:0, one launch (start us, length us, event | category | flops | bytes accessed | tf_op | source)
XLA Modules:
  0.0 676.0 jit_solution(303562709423422189)
XLA Ops:
  15.8 67.0 %shard_map.244 = (bf16[16,72,2304]{2,1,0:T(8,128)(2,1)S(1)}, f32[24,1152]{1,0:T(8,128)S(1)}, bf16[2,128,1152]{2,1,0:T(8,128)(2,1)S(1)}, bf16[2,128,1152]{2,1,0:T(8,128)(2,1)S(1)}) custom-call(bf16[72,2304]{1,0:T(8,128)(2,1)S(1)} %pad_maximum_fusion.4.shard, f32[24,1152]{1,0:T(8,128)S(1)} %reshape.456.small, bf16[2,128,1152]{2,1,0:T(8,128)(2,1)S(1)} %copy-done), custom_call_target="tpu_custom_call" | custom-call | flops 34359738368 | bytes 5308416 | tf_op jit(solution)/shard_map/pallas_call | solution.py:707
  94.7 5.2 fusion.58
  102.8 7.3 %shard_map.245 = (bf16[2,128,576]{2,1,0:T(8,128)(2,1)S(1)}, bf16[2,128,576]{2,1,0:T(8,128)(2,1)S(1)}) custom-call(bf16[2,128,1728]{2,1,0:T(8,128)(2,1)S(1)} %bitcast.320, bf16[2,128,1728]{2,1,0:T(8,128)(2,1)S(1)} %bitcast.318), custom_call_target="tpu_custom_call" | custom-call | flops 301989888 | bytes 1769472 | tf_op jit(solution)/shard_map/pallas_call | solution.py:141
  116.0 10.6 %collective-permute-done.1 = bf16[2,128,1152]{2,1,0:T(8,128)(2,1)S(1)} collective-permute-done((bf16[2,128,1152]{2,1,0:T(8,128)(2,1)S(1)}, bf16[2,128,1152]{2,1,0:T(8,128)(2,1)S(1)}, u32[]{:S(2)}, u32[]{:S(2)}) %collective-permute-start.1) | collective-permute-done | bytes 589856 | tf_op jit(solution)/shard_map/ppermute | solution.py:45
  137.0 8.2 %collective-permute-done.4.refs_2_ = bf16[72,2304]{1,0:T(8,128)(2,1)S(1)} collective-permute-done((bf16[72,2304]{1,0:T(8,128)(2,1)S(1)}, bf16[72,2304]{1,0:T(8,128)(2,1)S(1)}, u32[]{:S(2)}, u32[]{:S(2)}) %collective-permute-start.4) | collective-permute-done | bytes 331808 | tf_op jit(solution)/shard_map/ppermute | solution.py:767
  150.4 6.1 multiply_convert_fusion.2
  164.2 5.0 collective-permute-done.5
  170.3 19.7 %collective-permute-done.6.refs_3_ = bf16[4,72,2304]{2,1,0:T(8,128)(2,1)S(1)} collective-permute-done((bf16[4,72,2304]{2,1,0:T(8,128)(2,1)}, bf16[4,72,2304]{2,1,0:T(8,128)(2,1)S(1)}, u32[]{:S(2)}, u32[]{:S(2)}) %collective-permute-start.6) | collective-permute-done | bytes 1327136 | tf_op jit(solution)/shard_map/ppermute | solution.py:45
  204.3 14.8 %all-to-all-done = bf16[2,128,1152]{2,0,1:T(2,128)(2,1)} async-done(((bf16[2,128,1152]{2,0,1:T(2,128)(2,1)}), bf16[2,128,1152]{2,0,1:T(2,128)(2,1)}, u32[]{:S(2)}, u32[]{:S(2)}) %all-to-all-start) | async-done | bytes 589856 | tf_op jit(solution)/shard_map/all_to_all | solution.py:582
  244.4 9.0 %all-to-all-start.2 = ((bf16[2,128,1152]{2,0,1:T(2,128)(2,1)}), bf16[2,128,1152]{2,0,1:T(2,128)(2,1)S(1)}, u32[]{:S(2)}, u32[]{:S(2)}) async-start(bf16[2,128,1152]{2,0,1:T(2,128)(2,1)} %copy.251), calls=%async_computation.2 | async-start | bytes 1179648 | tf_op jit(solution)/shard_map/all_to_all | solution.py:582
  272.4 13.2 %collective-permute-done.9 = bf16[32,8,1152]{2,1,0:T(8,128)(2,1)} collective-permute-done((bf16[32,8,1152]{2,1,0:T(8,128)(2,1)}, bf16[32,8,1152]{2,1,0:T(8,128)(2,1)}, u32[]{:S(2)}, u32[]{:S(2)}) %collective-permute-start.9) | collective-permute-done | bytes 589856 | tf_op jit(solution)/shard_map/ppermute | solution.py:45
  299.4 11.0 %collective-permute-done.10 = bf16[32,8,1152]{2,1,0:T(8,128)(2,1)S(1)} collective-permute-done((bf16[32,8,1152]{2,1,0:T(8,128)(2,1)}, bf16[32,8,1152]{2,1,0:T(8,128)(2,1)S(1)}, u32[]{:S(2)}, u32[]{:S(2)}) %collective-permute-start.10) | collective-permute-done | bytes 589856 | tf_op jit(solution)/shard_map/ppermute | solution.py:45
  319.2 10.0 %shard_map.249 = bf16[1152,4608]{1,0:T(8,128)(2,1)} custom-call(bf16[256,1152]{1,0:T(8,128)(2,1)S(1)} %fusion.230.refs_0_, bf16[256,1152]{1,0:T(8,128)(2,1)S(1)} %bitcast.348, bf16[256,2304]{1,0:T(8,128)(2,1)S(1)} %fusion.120.refs_2_, bf16[256,2304]{1,0:T(8,128)(2,1)S(1)} %fusion.127.refs_3_, bf16[256,1152]{1,0:T(8,128)(2,1)S(1)} %fusion.154.refs_4_, ...), custom_call_target="tpu_custom_call" | custom-call | flops 5435817984 | bytes 17694720 | tf_op jit(solution)/shard_map/pallas_call | solution.py:185
  333.9 5.8 convert_add_fusion.4
  344.8 13.7 %collective-permute-done.11 = bf16[32,8,1152]{2,1,0:T(8,128)(2,1)S(1)} collective-permute-done((bf16[32,8,1152]{2,1,0:T(8,128)(2,1)S(1)}, bf16[32,8,1152]{2,1,0:T(8,128)(2,1)S(1)}, u32[]{:S(2)}, u32[]{:S(2)}) %collective-permute-start.11) | collective-permute-done | bytes 589856 | tf_op jit(solution)/shard_map/ppermute | solution.py:45
  358.5 7.8 %multiply_reduce_fusion.6 = (f32[32]{0:T(128)}, f32[32]{0:T(128)}, f32[32,1152]{1,0:T(8,128)}, f32[32,8]{1,0:T(8,128)S(1)}, f32[32,8]{1,0:T(8,128)S(1)}, /*index...) fusion(f32[32,1152]{1,0:T(8,128)S(1)} %copy-done.69, ...), kind=kOutput, calls=%fused_computation.160 | convolution fusion | flops 1365331456 | bytes 11948416 | tf_op jit(solution)/shard_map/dot_general | solution.py:26
  370.3 5.7 all-to-all-start.1
  378.5 5.1 shard_map.250
  386.1 5.1 shard_map.251
  394.6 6.2 shard_map.252
  400.8 8.5 %collective-permute-done.15 = bf16[32,8,1152]{2,1,0:T(8,128)(2,1)S(1)} collective-permute-done((bf16[32,8,1152]{2,1,0:T(8,128)(2,1)}, bf16[32,8,1152]{2,1,0:T(8,128)(2,1)S(1)}, u32[]{:S(2)}, u32[]{:S(2)}) %collective-permute-start.15) | collective-permute-done | bytes 589856 | tf_op jit(solution)/shard_map/ppermute | solution.py:45
  415.9 5.8 all-to-all-start.3
  429.6 12.7 %all-to-all-done.3 = bf16[32,8,1152]{2,1,0:T(8,128)(2,1)S(1)} async-done(((bf16[32,8,1152]{2,1,0:T(8,128)(2,1)}), bf16[32,8,1152]{2,1,0:T(8,128)(2,1)S(1)}, u32[]{:S(2)}, u32[]{:S(2)}) %all-to-all-start.3) | async-done | bytes 589856 | tf_op jit(solution)/shard_map/all_to_all | solution.py:588
  444.1 5.2 fusion.106.refs_2_
  449.3 9.1 %collective-permute-done.17 = bf16[2,128,1152]{2,1,0:T(8,128)(2,1)S(1)} collective-permute-done((bf16[2,128,1152]{2,1,0:T(8,128)(2,1)S(1)}, bf16[2,128,1152]{2,1,0:T(8,128)(2,1)S(1)}, u32[]{:S(2)}, u32[]{:S(2)}) %collective-permute-start.17) | collective-permute-done | bytes 589856 | tf_op jit(solution)/shard_map/ppermute | solution.py:45
  460.0 5.2 fusion.113.refs_3_
  472.3 9.9 %shard_map.253 = (bf16[1152,2304]{1,0:T(8,128)(2,1)}, bf16[1152,2304]{1,0:T(8,128)(2,1)}) custom-call(bf16[256,1152]{1,0:T(8,128)(2,1)S(1)} %bitcast.330, bf16[256,1152]{1,0:T(8,128)(2,1)} %bitcast.15.refs_1_, bf16[256,2304]{1,0:T(8,128)(2,1)S(1)} %fusion.106.refs_2_, bf16[256,2304]{1,0:T(8,128)(2,1)S(1)} %fusion.113.refs_3_, ...), custom_call_target="tpu_custom_call" | custom-call | flops 5435817984 | bytes 17694720 | tf_op jit(solution)/shard_map/pallas_call | solution.py:185
  493.4 6.9 %collective-permute-done.22 = bf16[2,128,1152]{2,1,0:T(8,128)(2,1)S(1)} collective-permute-done((bf16[2,128,1152]{2,1,0:T(8,128)(2,1)S(1)}, bf16[2,128,1152]{2,1,0:T(8,128)(2,1)S(1)}, u32[]{:S(2)}, u32[]{:S(2)}) %collective-permute-start.22) | collective-permute-done | bytes 589856 | tf_op jit(solution)/shard_map/ppermute | solution.py:45
  508.9 10.9 %shard_map.254 = (bf16[2,128,1728]{2,1,0:T(8,128)(2,1)S(1)}, bf16[2,128,1728]{2,1,0:T(8,128)(2,1)S(1)}) custom-call(bf16[2,128,1728]{2,1,0:T(8,128)(2,1)S(1)} %bitcast.321, bf16[2,128,1728]{2,1,0:T(8,128)(2,1)S(1)} %bitcast.319, bf16[2,128,576]{2,1,0:T(8,128)(2,1)S(1)} %bitcast.343, bf16[2,128,576]{2,1,0:T(8,128)(2,1)S(1)} %bitcast.344), custom_call_target="tpu_custom_call" | custom-call | flops 905969664 | bytes 2359296 | tf_op jit(solution)/shard_map/pallas_call | solution.py:141
  519.8 5.1 fusion.73
  530.6 5.4 shard_map.255
  544.9 109.3 %shard_map.256 = (f32[72,2304]{1,0:T(8,128)}, f32[72,2304]{1,0:T(8,128)}, f32[72,2304]{1,0:T(8,128)}, f32[108,128]{1,0:T(8,128)}) custom-call(bf16[4,2,2,72,2304]{4,3,2,1,0:T(8,128)(2,1)} %bitcast.359, bf16[4,2,2,72,2304]{4,3,2,1,0:T(8,128)(2,1)} %bitcast.360, bf16[4,2,2,72,2304]{4,3,2,1,0:T(8,128)(2,1)} %bitcast.356, f32[108,128]{1,0:T(8,128)} %pad_maximum_fusion.6.refs_3_), custom_call_target="tpu_custom_call" | custom-call | tf_op jit(solution)/shard_map/pallas_call | solution.py:442
  (520 shorter events, 229.7 us)
Async XLA Ops:
  7.2 143.2 %all-gather.3.cloned.1.call-start = ((), (), s32[]{:S(2)}) async-start(), calls=%async_computation.6 | async-start | bytes 11280384 | tf_op jit(solution)/shard_map/all_gather | solution.py:596
  9.3 281.5 %all-gather.5.cloned.1.call-start = ((), (), s32[]{:S(2)}) async-start(), calls=%async_computation.7 | async-start | bytes 11280384 | tf_op jit(solution)/shard_map/all_gather | solution.py:596
  85.7 25.5 %collective-permute-start = (bf16[72,2304]{1,0:T(8,128)(2,1)S(1)}, bf16[72,2304]{1,0:T(8,128)(2,1)S(1)}, u32[]{:S(2)}, u32[]{:S(2)}) collective-permute-start(bf16[72,2304]{1,0:T(8,128)(2,1)S(1)} %pad_maximum_fusion.3.own), channel_id=1, source_target_pairs={{0,8},{2,10},{4,12},{6,14},{8,16},{10,18},{12,20},{14,22},{16,24},... | collective-permute-start | bytes 995336 | tf_op jit(solution)/shard_map/ppermute | solution.py:767
  113.4 13.1 %collective-permute-start.1 = (bf16[2,128,1152]{2,1,0:T(8,128)(2,1)S(1)}, bf16[2,128,1152]{2,1,0:T(8,128)(2,1)S(1)}, u32[]{:S(2)}, u32[]{:S(2)}) collective-permute-start(bf16[2,128,1152]{2,1,0:T(8,128)(2,1)S(1)} %bitcast.398), channel_id=1, source_target_pairs={{0,1},{1,0},{2,3},{3,2},{4,5},{5,4},{6,7},{7,6},{8,9},{9,8},{10,11... | collective-permute-start | bytes 1769480 | tf_op jit(solution)/shard_map/ppermute | solution.py:45
  114.4 18.7 %collective-permute-start.2 = (bf16[72,2304]{1,0:T(8,128)(2,1)S(1)}, bf16[72,2304]{1,0:T(8,128)(2,1)S(1)}, u32[]{:S(2)}, u32[]{:S(2)}) collective-permute-start(bf16[72,2304]{1,0:T(8,128)(2,1)S(1)} %collective-permute-done.refs_0_), channel_id=1, source_target_pairs={{0,8},{2,10},{4,12},{6,14},{8,16},{10,18},{12,20},{14,22},{16,24},... | collective-permute-start | bytes 995336 | tf_op jit(solution)/shard_map/ppermute | solution.py:767
  135.2 12.4 %collective-permute-start.3 = (bf16[2,128,1152]{2,1,0:T(8,128)(2,1)S(1)}, bf16[2,128,1152]{2,1,0:T(8,128)(2,1)}, u32[]{:S(2)}, u32[]{:S(2)}) collective-permute-start(bf16[2,128,1152]{2,1,0:T(8,128)(2,1)S(1)} %add_convert_fusion.3), channel_id=1, source_target_pairs={{0,1},{1,0},{2,3},{3,2},{4,5},{5,4},{6,7},{7,6},{8,9},{9,8},{10,11... | collective-permute-start | bytes 1769480 | tf_op jit(solution)/shard_map/ppermute | solution.py:45
  136.3 8.9 %collective-permute-start.4 = (bf16[72,2304]{1,0:T(8,128)(2,1)S(1)}, bf16[72,2304]{1,0:T(8,128)(2,1)S(1)}, u32[]{:S(2)}, u32[]{:S(2)}) collective-permute-start(bf16[72,2304]{1,0:T(8,128)(2,1)S(1)} %collective-permute-done.2.refs_1_), channel_id=1, source_target_pairs={{0,8},{2,10},{4,12},{6,14},{8,16},{10,18},{12,20},{14,22},{16,24},... | collective-permute-start | bytes 995336 | tf_op jit(solution)/shard_map/ppermute | solution.py:767
  148.8 41.2 %collective-permute-start.6 = (bf16[4,72,2304]{2,1,0:T(8,128)(2,1)}, bf16[4,72,2304]{2,1,0:T(8,128)(2,1)S(1)}, u32[]{:S(2)}, u32[]{:S(2)}) collective-permute-start(bf16[4,72,2304]{2,1,0:T(8,128)(2,1)} %pad_maximum_fusion), channel_id=1, source_target_pairs={{0,4},{2,6},{4,0},{6,2},{8,12},{10,14},{12,8},{14,10},{16,20},{18,... | collective-permute-start | bytes 3981320 | tf_op jit(solution)/shard_map/ppermute | solution.py:45
  158.2 11.0 %collective-permute-start.5 = (bf16[2,128,1152]{2,1,0:T(8,128)(2,1)S(1)}, bf16[2,128,1152]{2,1,0:T(8,128)(2,1)S(1)}, u32[]{:S(2)}, u32[]{:S(2)}) collective-permute-start(bf16[2,128,1152]{2,1,0:T(8,128)(2,1)S(1)} %bitcast.399), channel_id=1, source_target_pairs={{0,1},{1,0},{2,3},{3,2},{4,5},{5,4},{6,7},{7,6},{8,9},{9,8},{10,11... | collective-permute-start | bytes 1769480 | tf_op jit(solution)/shard_map/ppermute | solution.py:45
  191.2 30.1 %collective-permute-start.7 = (bf16[8,72,2304]{2,1,0:T(8,128)(2,1)}, bf16[8,72,2304]{2,1,0:T(8,128)(2,1)}, u32[]{:S(2)}, u32[]{:S(2)}) collective-permute-start(bf16[8,72,2304]{2,1,0:T(8,128)(2,1)} %constant_dynamic-update-slice_fusion), channel_id=1, source_target_pairs={{0,2},{2,0},{4,6},{6,4},{8,10},{10,8},{12,14},{14,12},{16,18},{18,... | collective-permute-start | bytes 7962632 | tf_op jit(solution)/shard_map/ppermute | solution.py:45
  195.3 23.8 %all-to-all-start = ((bf16[2,128,1152]{2,0,1:T(2,128)(2,1)}), bf16[2,128,1152]{2,0,1:T(2,128)(2,1)}, u32[]{:S(2)}, u32[]{:S(2)}) async-start(bf16[2,128,1152]{2,0,1:T(2,128)(2,1)} %copy.166), calls=%async_computation | async-start | bytes 1179648 | tf_op jit(solution)/shard_map/all_to_all | solution.py:582
  226.8 34.6 %collective-permute-start.8 = (bf16[32,8,1152]{2,1,0:T(8,128)(2,1)}, bf16[32,8,1152]{2,1,0:T(8,128)(2,1)}, u32[]{:S(2)}, u32[]{:S(2)}) collective-permute-start(bf16[32,8,1152]{2,1,0:T(8,128)(2,1)} %add_convert_fusion.2), channel_id=1, source_target_pairs={{0,1},{1,0},{2,3},{3,2},{4,5},{5,4},{6,7},{7,6},{8,9},{9,8},{10,11... | collective-permute-start | bytes 1769480 | tf_op jit(solution)/shard_map/ppermute | solution.py:45
  244.4 25.1 %all-to-all-start.2 = ((bf16[2,128,1152]{2,0,1:T(2,128)(2,1)}), bf16[2,128,1152]{2,0,1:T(2,128)(2,1)S(1)}, u32[]{:S(2)}, u32[]{:S(2)}) async-start(bf16[2,128,1152]{2,0,1:T(2,128)(2,1)} %copy.251), calls=%async_computation.2 | async-start | bytes 1179648 | tf_op jit(solution)/shard_map/all_to_all | solution.py:582
  253.3 232.1 %reduce-scatter.3.cloned.1.call-start = ((), (), s32[]{:S(2)}) async-start(), calls=%async_computation.8 | async-start | bytes 11280384 | tf_op jit(solution)/shard_map/reduce_scatter | solution.py:802
  269.2 16.4 %collective-permute-start.9 = (bf16[32,8,1152]{2,1,0:T(8,128)(2,1)}, bf16[32,8,1152]{2,1,0:T(8,128)(2,1)}, u32[]{:S(2)}, u32[]{:S(2)}) collective-permute-start(bf16[32,8,1152]{2,1,0:T(8,128)(2,1)} %convolution_convert_fusion), channel_id=1, source_target_pairs={{0,1},{1,0},{2,3},{3,2},{4,5},{5,4},{6,7},{7,6},{8,9},{9,8},{10,11... | collective-permute-start | bytes 1769480 | tf_op jit(solution)/shard_map/ppermute | solution.py:45
  271.0 42.4 %collective-permute-start.12 = (bf16[32,8,1152]{2,1,0:T(8,128)(2,1)}, bf16[32,8,1152]{2,1,0:T(8,128)(2,1)S(1)}, u32[]{:S(2)}, u32[]{:S(2)}) collective-permute-start(bf16[32,8,1152]{2,1,0:T(8,128)(2,1)} %fusion.155), channel_id=1, source_target_pairs={{0,1},{1,0},{2,3},{3,2},{4,5},{5,4},{6,7},{7,6},{8,9},{9,8},{10,11... | collective-permute-start | bytes 1769480 | tf_op jit(solution)/shard_map/ppermute | solution.py:45
  290.5 19.8 %collective-permute-start.10 = (bf16[32,8,1152]{2,1,0:T(8,128)(2,1)}, bf16[32,8,1152]{2,1,0:T(8,128)(2,1)S(1)}, u32[]{:S(2)}, u32[]{:S(2)}) collective-permute-start(bf16[32,8,1152]{2,1,0:T(8,128)(2,1)} %add_convert_fusion.1), channel_id=1, source_target_pairs={{0,1},{1,0},{2,3},{3,2},{4,5},{5,4},{6,7},{7,6},{8,9},{9,8},{10,11... | collective-permute-start | bytes 1769480 | tf_op jit(solution)/shard_map/ppermute | solution.py:45
  318.7 15.2 %collective-permute-start.13 = (bf16[32,8,1152]{2,1,0:T(8,128)(2,1)}, bf16[32,8,1152]{2,1,0:T(8,128)(2,1)}, u32[]{:S(2)}, u32[]{:S(2)}) collective-permute-start(bf16[32,8,1152]{2,1,0:T(8,128)(2,1)} %fusion.97), channel_id=1, source_target_pairs={{0,1},{1,0},{2,3},{3,2},{4,5},{5,4},{6,7},{7,6},{8,9},{9,8},{10,11... | collective-permute-start | bytes 1769480 | tf_op jit(solution)/shard_map/ppermute | solution.py:45
  344.4 14.0 %collective-permute-start.11 = (bf16[32,8,1152]{2,1,0:T(8,128)(2,1)S(1)}, bf16[32,8,1152]{2,1,0:T(8,128)(2,1)S(1)}, u32[]{:S(2)}, u32[]{:S(2)}) collective-permute-start(bf16[32,8,1152]{2,1,0:T(8,128)(2,1)S(1)} %fusion.94), channel_id=1, source_target_pairs={{0,1},{1,0},{2,3},{3,2},{4,5},{5,4},{6,7},{7,6},{8,9},{9,8},{10,11... | collective-permute-start | bytes 1769480 | tf_op jit(solution)/shard_map/ppermute | solution.py:45
  369.0 14.6 %collective-permute-start.14 = (bf16[32,8,1152]{2,1,0:T(8,128)(2,1)}, bf16[32,8,1152]{2,1,0:T(8,128)(2,1)S(1)}, u32[]{:S(2)}, u32[]{:S(2)}) collective-permute-start(bf16[32,8,1152]{2,1,0:T(8,128)(2,1)} %multiply_convert_fusion.6), channel_id=1, source_target_pairs={{0,1},{1,0},{2,3},{3,2},{4,5},{5,4},{6,7},{7,6},{8,9},{9,8},{10,11... | collective-permute-start | bytes 1769480 | tf_op jit(solution)/shard_map/ppermute | solution.py:45
  370.3 45.6 %all-to-all-start.1 = ((bf16[32,8,1152]{2,1,0:T(8,128)(2,1)}), bf16[32,8,1152]{2,1,0:T(8,128)(2,1)}, u32[]{:S(2)}, u32[]{:S(2)}) async-start(bf16[32,8,1152]{2,1,0:T(8,128)(2,1)} %get-tuple-element.227), calls=%async_computation.1 | async-start | bytes 1179648 | tf_op jit(solution)/shard_map/all_to_all | solution.py:588
  393.4 16.0 %collective-permute-start.15 = (bf16[32,8,1152]{2,1,0:T(8,128)(2,1)}, bf16[32,8,1152]{2,1,0:T(8,128)(2,1)S(1)}, u32[]{:S(2)}, u32[]{:S(2)}) collective-permute-start(bf16[32,8,1152]{2,1,0:T(8,128)(2,1)} %fusion.70), channel_id=1, source_target_pairs={{0,1},{1,0},{2,3},{3,2},{4,5},{5,4},{6,7},{7,6},{8,9},{9,8},{10,11... | collective-permute-start | bytes 1769480 | tf_op jit(solution)/shard_map/ppermute | solution.py:45
  415.9 26.4 %all-to-all-start.3 = ((bf16[32,8,1152]{2,1,0:T(8,128)(2,1)}), bf16[32,8,1152]{2,1,0:T(8,128)(2,1)S(1)}, u32[]{:S(2)}, u32[]{:S(2)}) async-start(bf16[32,8,1152]{2,1,0:T(8,128)(2,1)} %add_convert_fusion), calls=%async_computation.3 | async-start | bytes 1179648 | tf_op jit(solution)/shard_map/all_to_all | solution.py:588
  421.7 242.8 %reduce-scatter.5.cloned.1.call-start = ((), (), s32[]{:S(2)}) async-start(), calls=%async_computation.9 | async-start | bytes 5640192 | tf_op jit(solution)/shard_map/reduce_scatter | solution.py:802
  428.5 13.9 %collective-permute-start.16 = (f32[109,128]{1,0:T(8,128)S(1)}, f32[109,128]{1,0:T(8,128)S(1)}, u32[]{:S(2)}, u32[]{:S(2)}) collective-permute-start(f32[109,128]{1,0:T(8,128)S(1)} %maximum_bitcast_fusion), channel_id=1, source_target_pairs={{0,1},{1,0},{2,3},{3,2},{4,5},{5,4},{6,7},{7,6},{8,9},{9,8},{10,11... | collective-permute-start | bytes 167432 | tf_op jit(solution)/shard_map/ppermute | solution.py:45
  442.4 6.9 %collective-permute-start.18 = (f32[109,128]{1,0:T(8,128)S(1)}, f32[109,128]{1,0:T(8,128)S(1)}, u32[]{:S(2)}, u32[]{:S(2)}) collective-permute-start(f32[109,128]{1,0:T(8,128)S(1)} %fusion.227), channel_id=1, source_target_pairs={{0,2},{2,0},{4,6},{6,4},{8,10},{10,8},{12,14},{14,12},{16,18},{18,... | collective-permute-start | bytes 167432 | tf_op jit(solution)/shard_map/ppermute | solution.py:45
  442.7 15.7 %collective-permute-start.17 = (bf16[2,128,1152]{2,1,0:T(8,128)(2,1)S(1)}, bf16[2,128,1152]{2,1,0:T(8,128)(2,1)S(1)}, u32[]{:S(2)}, u32[]{:S(2)}) collective-permute-start(bf16[2,128,1152]{2,1,0:T(8,128)(2,1)S(1)} %multiply_convert_fusion.5), channel_id=1, source_target_pairs={{0,1},{1,0},{2,3},{3,2},{4,5},{5,4},{6,7},{7,6},{8,9},{9,8},{10,11... | collective-permute-start | bytes 1769480 | tf_op jit(solution)/shard_map/ppermute | solution.py:45
  467.0 15.3 %collective-permute-start.20 = (bf16[2,128,1152]{2,1,0:T(8,128)(2,1)S(1)}, bf16[2,128,1152]{2,1,0:T(8,128)(2,1)S(1)}, u32[]{:S(2)}, u32[]{:S(2)}) collective-permute-start(bf16[2,128,1152]{2,1,0:T(8,128)(2,1)S(1)} %bitcast.397), channel_id=1, source_target_pairs={{0,1},{1,0},{2,3},{3,2},{4,5},{5,4},{6,7},{7,6},{8,9},{9,8},{10,11... | collective-permute-start | bytes 1769480 | tf_op jit(solution)/shard_map/ppermute | solution.py:45
  470.1 12.3 %collective-permute-start.21 = (f32[109,128]{1,0:T(8,128)S(1)}, f32[109,128]{1,0:T(8,128)S(1)}, u32[]{:S(2)}, u32[]{:S(2)}) collective-permute-start(f32[109,128]{1,0:T(8,128)S(1)} %add.269), channel_id=1, source_target_pairs={{0,8},{2,10},{4,12},{6,14},{8,0},{10,2},{12,4},{14,6},{16,24},{18,... | collective-permute-start | bytes 167432 | tf_op jit(solution)/shard_map/ppermute | solution.py:45
  482.4 11.0 %collective-permute-start.23 = (f32[109,128]{1,0:T(8,128)S(1)}, f32[109,128]{1,0:T(8,128)S(1)}, u32[]{:S(2)}, u32[]{:S(2)}) collective-permute-start(f32[109,128]{1,0:T(8,128)S(1)} %add.272), channel_id=1, source_target_pairs={{0,16},{2,18},{4,20},{6,22},{8,24},{10,26},{12,28},{14,30},{16,0},... | collective-permute-start | bytes 167432 | tf_op jit(solution)/shard_map/ppermute | solution.py:45
  486.4 13.9 %collective-permute-start.22 = (bf16[2,128,1152]{2,1,0:T(8,128)(2,1)S(1)}, bf16[2,128,1152]{2,1,0:T(8,128)(2,1)S(1)}, u32[]{:S(2)}, u32[]{:S(2)}) collective-permute-start(bf16[2,128,1152]{2,1,0:T(8,128)(2,1)S(1)} %multiply_convert_fusion.4), channel_id=1, source_target_pairs={{0,1},{1,0},{2,3},{3,2},{4,5},{5,4},{6,7},{7,6},{8,9},{9,8},{10,11... | collective-permute-start | bytes 1769480 | tf_op jit(solution)/shard_map/ppermute | solution.py:45
  524.9 12.5 %collective-permute-start.24 = (bf16[2,128,1152]{2,1,0:T(8,128)(2,1)}, bf16[2,128,1152]{2,1,0:T(8,128)(2,1)}, u32[]{:S(2)}, u32[]{:S(2)}) collective-permute-start(bf16[2,128,1152]{2,1,0:T(8,128)(2,1)} %fusion.73), channel_id=1, source_target_pairs={{0,1},{1,0},{2,3},{3,2},{4,5},{5,4},{6,7},{7,6},{8,9},{9,8},{10,11... | collective-permute-start | bytes 1769480 | tf_op jit(solution)/shard_map/ppermute | solution.py:45
  (124 other events, 1237.5 us)
Sparse Core Ops, SparseCore 0:
  10.9 124.3 all-gather.2
  138.1 99.5 all-gather.4
  339.8 144.7 reduce-scatter.2
  493.5 84.8 reduce-scatter.4

commit v4 on v3

--- a/solution.py
+++ b/solution.py
@@ -243,7 +243,7 @@
 class Scatter:
     def __init__(self, grad, out, refs, flipped):
         self.grad, self.out, self.flipped = grad, out, flipped
-        self.own, self.core_in, self.y_in, self.ring_in, self.own_sem, self.send_sem, self.recv_sem = refs
+        self.own, self.own_sem, self.core_in, self.y_in, self.ring_in, self.send_sem, self.recv_sem = refs
         self.ring = grad.shape[0]
         self.stages = self.ring + 2
         self.chunks = self.send_sem.shape[1]
@@ -255,17 +255,20 @@
         self.load = None
 
     @staticmethod
-    def scratch(ring, rows, cols):
+    def scratch(ring, rows, cols, flips=True):
         chunks = cols // 384 if cols % 384 == 0 else 1
         return [
             pltpu.VMEM((ring, 2, rows, cols), bf16),
+            pltpu.SemaphoreType.DMA,
             pltpu.VMEM((ring, 2, rows, cols), bf16),
             pltpu.VMEM((ring, rows, cols), bf16),
-            pltpu.VMEM((ring - 1, 2, rows, cols), bf16),
-            pltpu.SemaphoreType.DMA,
+            pltpu.VMEM((ring - 1, 2 if flips else 1, rows, cols), bf16),
             pltpu.SemaphoreType.DMA((ring + 1, chunks)),
             pltpu.SemaphoreType.DMA((ring + 1, chunks)),
         ]
+
+    def neighbours(self):
+        return [{"dp": partner} for partner in (self.after, self.before, self.me ^ 1, self.me ^ 2)]
 
     def begin(self):
         self.load = pltpu.make_async_copy(self.grad.at[:, :, self.core], self.own, self.own_sem)
@@ -333,10 +336,12 @@
 
 
 class Pipeline:
-    def __init__(self, jobs):
-        self.jobs = jobs
-        self.queue = [(job, j) for job in jobs for j in range(job.chunks)]
-        self.flight = []
+    def __init__(self):
+        self.jobs, self.queue, self.flight = [], [], []
+
+    def add(self, jobs):
+        self.jobs = self.jobs + jobs
+        self.queue += [(job, j) for job in jobs for j in range(job.chunks)]
         for job in jobs:
             job.begin()
 
@@ -412,6 +417,632 @@
     pl.semaphore_wait(barrier, len(partners))
 
 
+class Swap:
+    def __init__(self, source, target, sems, k):
+        self.copy = pltpu.make_async_remote_copy(
+            src_ref=source, dst_ref=target, send_sem=sems.at[0, k], recv_sem=sems.at[1, k],
+            device_id={"tensor": 1 - lax.axis_index("tensor")}, device_id_type=MESH,
+        )
+        self.copy.start()
+
+
+def spread(value, rows, clips):
+    return value.reshape(rows // clips, clips, value.shape[0] // rows, value.shape[1])
+
+
+def clip_rows(mods, clips, span):
+    rows = [mods[6 * c + span : 6 * c + span + 1, :] for c in range(clips)]
+    return jnp.stack(rows, axis=0)[None]
+
+
+def clip_sums(value, rows, clips):
+    return jnp.sum(spread(value, rows, clips), axis=(0, 2))
+
+
+def norm_back_rows(grad, grad_hidden, stream, scale, rows, clips):
+    stream = stream.astype(f32)
+    centered = stream - jnp.mean(stream, axis=-1, keepdims=True)
+    inverse = lax.rsqrt(jnp.mean(centered * centered, axis=-1, keepdims=True) + epsilon)
+    normed = centered * inverse
+    grad_normed = (spread(grad_hidden, rows, clips) * (1.0 + scale)).reshape(grad_hidden.shape)
+    flat = grad_normed - jnp.mean(grad_normed, axis=-1, keepdims=True)
+    slope = jnp.mean(grad_normed * normed, axis=-1, keepdims=True)
+    grad_in = grad.astype(f32) + inverse * (flat - normed * slope)
+    return grad_in, clip_sums(grad_hidden, rows, clips), clip_sums(grad_hidden * normed, rows, clips)
+
+
+def gradient_blocks(target, value, cols):
+    ring, rows = target.shape[0], target.shape[3]
+    for k in range(4 * ring):
+        target[k // 4, (k // 2) % 2, k % 2, :, cols] = value[k * rows : (k + 1) * rows].astype(bf16)
+
+
+def attention_back_kernel(rows, clips, spatial, extra, tailing, pairs, *refs):
+    grad, branch, stream, mods, hidden0, hidden1, qkv0, qkv1, att0, att1, weights, *refs = refs
+    others, refs = refs[:extra], refs[extra:]
+    if tailing:
+        dmod_in, *refs = refs
+    grad_out, *refs = refs
+    other_outs, refs = refs[:extra], refs[extra:]
+    if tailing:
+        own_out, small_out, *refs = refs
+    else:
+        dmod_out, gw_out, *refs = refs
+    w, w_sem, db0, db1, part_out, part_in, keep, ga0, ga1, x_sems, *refs = refs
+    dqkv, refs = (refs[:3], refs[3:6]), refs[6:]
+    inner = att0.shape[1]
+    count = grad.shape[0]
+    jobs = []
+    for i in range(extra):
+        jobs.append(Scatter(others[i], other_outs[i], refs[7 * i : 7 * i + 7], lambda j: j % 6 == 5))
+    refs = refs[7 * extra :]
+    greeted = [{"tensor": 1 - lax.axis_index("tensor")}]
+    if tailing:
+        small, gw, *refs = refs
+        own_job = Scatter(gw, own_out, refs[:7], lambda j: False)
+        total = SmallSum(pairs, small, small_out, refs[7:])
+        greeted = total.partners + [{"dp": jobs[0].after}, {"dp": jobs[0].before}]
+    elif extra:
+        greeted += jobs[0].neighbours()
+    greet(greeted)
+    load = pltpu.make_async_copy(weights, w, w_sem)
+    load.start()
+    db0[...] = (
+        (spread(grad[...].astype(f32), rows, clips) * clip_rows(mods, clips, 2)).reshape(grad.shape).astype(bf16)
+    )
+    first = Swap(db0, db1, x_sems, 0)
+    pipeline = Pipeline()
+    pipeline.add(jobs)
+    tick = pipeline.tick
+    dgate = clip_sums(grad[...].astype(f32) * branch[...], rows, clips)
+    load.wait()
+    w_proj = w[:, 3 * inner :]
+    ga0[...] = dot(db0[...], w_proj).astype(bf16)
+    tick()
+    tick()
+
+    def heads(pieces):
+        take = lambda refs, cols: (
+            refs[pieces[0][0]][pl.ds(*pieces[0][1:]), cols]
+            if len(pieces) == 1
+            else jnp.concatenate([refs[i][pl.ds(r, n), cols] for i, r, n in pieces], axis=0)
+        )
+        residue = 0 if spatial else count // FRAMES
+        for h, start in enumerate(range(0, inner, HEAD_DIM)):
+            q, k, v = (
+                take((qkv0, qkv1), slice(p * inner + start, p * inner + start + HEAD_DIM)) for p in range(3)
+            )
+            cols = slice(start, start + HEAD_DIM)
+            grad_out_h = take((ga0, ga1), cols)
+            probs = softmax_scores(q, k, residue)
+            grad_probs = dot_nt(grad_out_h, v)
+            mean = jnp.sum(probs * grad_probs, axis=-1, keepdims=True)
+            scaled = (probs * (grad_probs - mean) * HEAD_DIM ** (-0.5)).astype(bf16)
+            results = (dot(scaled, k), dot_tn(scaled, q), dot_tn(probs.astype(bf16), grad_out_h))
+            for p, value in enumerate(results):
+                at = 0
+                for i, r, n in pieces:
+                    dqkv[i][p][pl.ds(r, n), cols] = value[at : at + n].astype(bf16)
+                    at += n
+            if h % 4 == 3:
+                tick()
+
+    def grad_hidden(i):
+        value = dot_nt(dqkv[i][0][...], w[:, :inner])
+        value += dot_nt(dqkv[i][1][...], w[:, inner : 2 * inner])
+        return value + dot_nt(dqkv[i][2][...], w[:, 2 * inner : 3 * inner])
+
+    if not spatial:
+        heads([(0, 0, count)])
+    first.copy.wait_recv()
+    ga1[...] = dot(db1[...], w_proj).astype(bf16)
+    tick()
+    if spatial:
+        tokens = count // rows
+        for r in range(rows):
+            heads([(0, r * tokens, tokens), (1, r * tokens, tokens)])
+    else:
+        heads([(1, 0, count)])
+    part_out[...] = grad_hidden(1).astype(bf16)
+    second = Swap(part_out, part_in, x_sems, 1)
+    tick()
+    keep[...] = grad_hidden(0)
+    tick()
+    both = lambda a, b: jnp.concatenate([a[...], b[...]], axis=0)
+    for p in range(4):
+        left = both(hidden0, hidden1) if p < 3 else both(db0, db1)
+        right = both(dqkv[0][p], dqkv[1][p]) if p < 3 else both(att0, att1)
+        value = dot_tn(left, right)
+        cols = slice(p * inner, (p + 1) * inner)
+        if tailing:
+            gradient_blocks(gw, value, cols)
+        else:
+            gw_out[:, cols] = value.astype(bf16)
+        if p % 2:
+            tick()
+    if tailing:
+        pipeline.add([own_job])
+    second.copy.wait_recv()
+    result, dshift, dscale = norm_back_rows(
+        grad[...], keep[...] + part_in[...].astype(f32), stream[...], clip_rows(mods, clips, 1), rows, clips
+    )
+    grad_out[...] = result
+    dmod = (dshift, dscale, dgate)
+    if tailing:
+        for k, value in enumerate(dmod):
+            small[k * clips : (k + 1) * clips] = value
+        small[3 * clips :] = dmod_in[...]
+        more = total.tick()
+        while more:
+            pipeline.tick()
+            more = total.tick()
+        pipeline.finish()
+        total.finish()
+    else:
+        for k, value in enumerate(dmod):
+            dmod_out[k * clips : (k + 1) * clips] = value
+        pipeline.finish()
+    for exchange in (first, second):
+        exchange.copy.wait_send()
+
+
+def attention_back_call(layer, grad, mod, stored, others=(), dmod_in=None):
+    stream, branch, hidden, qkv, attended, weights = stored
+    rows, clips, count = layer.rows, layer.clips, layer.rows * layer.tokens
+    width, inner, ring = weights.shape[0], attended[0].shape[1], lax.axis_size("dp") // 4
+    share = width // (4 * ring)
+    pairs = exchange_pairs()
+    others = [g.reshape(ring, 2, 2, share, g.shape[1]) for g in others]
+    vmem, anywhere = pl.BlockSpec(memory_space=pltpu.VMEM), pl.BlockSpec(memory_space=pl.ANY)
+    args = [layer.flat(grad), layer.flat(branch), layer.flat(stream), mod.reshape(-1, width)]
+    args += [*hidden, *qkv, *attended]
+    specs = [vmem] * len(args) + [anywhere] * (1 + len(others))
+    args += [weights, *others]
+    shape = jax.ShapeDtypeStruct
+    outs = [shape((count, width), f32)]
+    scratch = [pltpu.VMEM(weights.shape, bf16), pltpu.SemaphoreType.DMA]
+    scratch += [pltpu.VMEM((count, width), bf16)] * 4 + [pltpu.VMEM((count, width), f32)]
+    scratch += [pltpu.VMEM((count, inner), bf16)] * 2 + [pltpu.SemaphoreType.DMA((2, 2))]
+    scratch += [pltpu.VMEM((count, inner), bf16)] * 6
+    outs += [shape((share, g.shape[-1]), f32) for g in others]
+    for g in others:
+        scratch += Scatter.scratch(ring, share, g.shape[-1])
+    tailing = dmod_in is not None
+    if tailing:
+        args.append(dmod_in)
+        specs.append(vmem)
+        outs.append(shape((share, 4 * inner), f32))
+        total = (3 * clips + dmod_in.shape[0], width)
+        outs.append(shape(total, f32))
+        scratch.append(pltpu.VMEM(total, f32))
+        scratch.append(pltpu.VMEM((ring, 2, 2, share, 4 * inner), bf16))
+        scratch += Scatter.scratch(ring, share, 4 * inner, False)
+        scratch += SmallSum.scratch(len(pairs), total)
+    else:
+        outs += [shape((3 * clips, width), f32), shape((width, 4 * inner), bf16)]
+    return pl.pallas_call(
+        functools.partial(attention_back_kernel, rows, clips, layer.spatial, len(others), tailing, pairs),
+        in_specs=specs,
+        out_specs=[vmem] * len(outs),
+        out_shape=outs,
+        scratch_shapes=scratch,
+        cost_estimate=pl.CostEstimate(flops=1 << 35, bytes_accessed=1 << 25, transcendentals=0),
+        compiler_params=pltpu.CompilerParams(
+            collective_id=2 + layer.spatial, has_side_effects=True, vmem_limit_bytes=62 << 20
+        ),
+    )(*args)
+
+
+class Gather:
+    def __init__(self, ring, shard, out, refs):
+        self.ring, self.shard, self.out = ring, shard, out
+        self.own_sem, self.send_sem, self.recv_sem = refs
+        self.me, self.size, self.sent = lax.axis_index("dp"), 4 * ring, []
+        self.k = 0
+
+    @staticmethod
+    def scratch(ring):
+        return [pltpu.SemaphoreType.DMA] + [pltpu.SemaphoreType.DMA((4 * ring,))] * 2
+
+    def neighbours(self):
+        me, size = self.me, self.size
+        around = (lax.rem(me + 4, size), lax.rem(me + size - 4, size), me ^ 1, me ^ 2)
+        return [{"dp": partner} for partner in around]
+
+    def back(self, device, k):
+        return lax.rem(device + self.size - 4 * k, self.size)
+
+    def send(self, source, place, slot, partner):
+        copy = pltpu.make_async_remote_copy(
+            src_ref=source, dst_ref=self.out.at[place],
+            send_sem=self.send_sem.at[slot], recv_sem=self.recv_sem.at[slot],
+            device_id={"dp": partner}, device_id_type=MESH,
+        )
+        copy.start()
+        self.sent.append(copy)
+
+    def landed(self, place, slot):
+        pltpu.make_async_remote_copy(
+            src_ref=self.out.at[place], dst_ref=self.out.at[place],
+            send_sem=self.send_sem.at[slot], recv_sem=self.recv_sem.at[slot],
+            device_id={"dp": self.me ^ 1}, device_id_type=MESH,
+        ).wait_recv()
+
+    def step(self):
+        k, self.k = self.k, self.k + 1
+        ring, me = self.ring, self.me
+        if k == 0:
+            self.keep = pltpu.make_async_copy(self.shard, self.out.at[me], self.own_sem)
+            self.keep.start()
+        if k < ring:
+            place = self.back(me, k)
+            if k:
+                self.landed(place, k - 1)
+            source = self.out.at[place] if k else self.shard
+            if k < ring - 1:
+                self.send(source, place, k, lax.rem(me + 4, self.size))
+            self.send(source, place, ring + k, me ^ 2)
+            self.send(source, place, 2 * ring + k, me ^ 1)
+        if 0 < k <= ring:
+            place = self.back(me ^ 2, k - 1)
+            self.landed(place, ring + k - 1)
+            self.send(self.out.at[place], place, 3 * ring + k - 1, me ^ 1)
+
+    def finish(self):
+        while self.k <= self.ring:
+            self.step()
+        for k in range(self.ring):
+            self.landed(self.back(self.me ^ 1, k), 2 * self.ring + k)
+            self.landed(self.back(self.me ^ 3, k), 3 * self.ring + k)
+        self.keep.wait()
+        for copy in self.sent:
+            copy.wait_send()
+
+
+class Pieces:
+    def __init__(self, rows, clips, count, spatial):
+        self.number = rows if spatial else 2
+        self.rows, self.clips = rows // self.number, clips
+        self.count = count // self.number
+
+    def at(self, i):
+        return pl.ds(i * self.count, self.count)
+
+    def times(self, value, mods, span, i, one=0.0):
+        if self.rows % self.clips == 0:
+            rows = one + clip_rows(mods, self.clips, span)
+            return (spread(value, self.rows, self.clips) * rows).reshape(value.shape)
+        return value * (one + self.row(mods, span, i))
+
+    def plus(self, value, mods, span, i):
+        if self.rows % self.clips == 0:
+            rows = clip_rows(mods, self.clips, span)
+            return (spread(value, self.rows, self.clips) + rows).reshape(value.shape)
+        return value + self.row(mods, span, i)
+
+    def row(self, mods, span, i):
+        at = 6 * (i * self.rows % self.clips) + span
+        return mods[at : at + 1, :]
+
+    def swap(self, source, target, sems, i, first):
+        return Swap(source.at[self.at(i)], target.at[self.at(i)], sems, first + i).copy
+
+
+def frame_sums(value, rows, clips):
+    frames = rows // clips
+    view = (value * value).reshape(frames, value.shape[0] // frames, value.shape[1])
+    sums = jnp.sum(jnp.sum(view, axis=1), axis=-1, keepdims=True)
+    return jnp.broadcast_to(sums, (frames, 128))
+
+
+def sublayer_end(pieces, stream, mods, span, keep, part_in, swaps, outs):
+    stream_out, stream_low, branch_out, squares, rows, clips = outs
+    for i, swap_i in enumerate(swaps):
+        at = pieces.at(i)
+        swap_i.wait_recv()
+        branch = keep[at, :] + part_in[at, :].astype(f32)
+        branch_out[at, :] = branch
+        gated = pieces.times(branch, mods, span, i)
+        keep[at, :] = gated
+        total = stream[at, :].astype(f32) + gated
+        stream_out[at, :] = total
+        stream_low[at, :] = total.astype(bf16)
+    squares[0] = frame_sums(stream_out[...], rows, clips)
+    squares[1] = frame_sums(keep[...], rows, clips)
+
+
+def attention_kernel(rows, clips, spatial, given, ring, *refs):
+    stream, mods, *refs = refs
+    if given:
+        hidden0, hidden1, *refs = refs
+    weights, *refs = refs
+    if ring:
+        shard, *refs = refs
+    stream_out, stream_low, branch_out, squares, qkv0, qkv1, att0, att1, *refs = refs
+    if not given:
+        hidden0, hidden1, *refs = refs
+    if ring:
+        gathered, *refs = refs
+    w, w_sem, part_out, part_in, keep, x_sems, *refs = refs
+    pieces = Pieces(rows, clips, stream.shape[0], spatial)
+    inner, count = att0.shape[1], stream.shape[0]
+    gather = Gather(ring, shard, gathered, refs) if ring else None
+    step = gather.step if ring else (lambda: None)
+    greet([{"tensor": 1 - lax.axis_index("tensor")}] + (gather.neighbours() if ring else []))
+    load = pltpu.make_async_copy(weights, w, w_sem)
+    load.start()
+    step()
+    arrivals = []
+    for i in range(pieces.number if not given else 0):
+        normed = norm_rows(stream[pieces.at(i), :].astype(f32))
+        value = pieces.plus(pieces.times(normed, mods, 1, i, 1.0), mods, 0, i)
+        hidden0[pieces.at(i), :] = value.astype(bf16)
+        arrivals.append(pieces.swap(hidden0, hidden1, x_sems, i, 0))
+    load.wait()
+    w_qkv = w[:, : 3 * inner]
+    qkv0[...] = dot(hidden0[...], w_qkv).astype(bf16)
+    step()
+
+    def heads(group):
+        residue = 0 if spatial else count // FRAMES
+
+        def take(refs, cols):
+            values = [refs[i][pl.ds(r, n), cols] for i, r, n in group]
+            return values[0] if len(values) == 1 else jnp.concatenate(values, axis=0)
+
+        for start in range(0, inner, HEAD_DIM):
+            q, k, v = (
+                take((qkv0, qkv1), slice(p * inner + start, p * inner + start + HEAD_DIM)) for p in range(3)
+            )
+            value = dot(softmax_scores(q, k, residue).astype(bf16), v).astype(bf16)
+            at = 0
+            for i, r, n in group:
+                (att0, att1)[i][pl.ds(r, n), start : start + HEAD_DIM] = value[at : at + n]
+                at += n
+
+    swaps = []
+    w_proj = w[:, 3 * inner :]
+    if spatial:
+        tokens = pieces.count
+        for r in range(pieces.number):
+            if not given:
+                arrivals[r].wait_recv()
+            at = pieces.at(r)
+            qkv1[at, :] = dot(hidden1[at, :], w_qkv).astype(bf16)
+            heads([(0, r * tokens, tokens), (1, r * tokens, tokens)])
+            part_out[at, :] = dot_nt(att1[at, :], w_proj).astype(bf16)
+            swaps.append(pieces.swap(part_out, part_in, x_sems, r, pieces.number))
+            step()
+    else:
+        heads([(0, 0, count)])
+        for arrival in arrivals:
+            arrival.wait_recv()
+        qkv1[...] = dot(hidden1[...], w_qkv).astype(bf16)
+        heads([(1, 0, count)])
+        for i in range(pieces.number):
+            at = pieces.at(i)
+            part_out[at, :] = dot_nt(att1[at, :], w_proj).astype(bf16)
+            swaps.append(pieces.swap(part_out, part_in, x_sems, i, pieces.number))
+    keep[...] = dot_nt(att0[...], w_proj)
+    step()
+    sublayer_end(
+        pieces, stream, mods, 2, keep, part_in, swaps,
+        (stream_out, stream_low, branch_out, squares, rows, clips),
+    )
+    if ring:
+        gather.finish()
+    for copy in arrivals + swaps:
+        copy.wait_send()
+
+
+def mlp_kernel(rows, clips, spatial, *refs):
+    stream, mods, weights, *refs = refs
+    stream_out, stream_low, branch_out, squares, hidden0, hidden1, pre0, pre1, act0, act1, *refs = refs
+    w, w_sem, part_out, part_in, keep, x_sems = refs
+    pieces = Pieces(rows, clips, stream.shape[0], spatial)
+    inner = act0.shape[1]
+    greet([{"tensor": 1 - lax.axis_index("tensor")}])
+    load = pltpu.make_async_copy(weights, w, w_sem)
+    load.start()
+    arrivals, swaps = [], []
+    for i in range(pieces.number):
+        normed = norm_rows(stream[pieces.at(i), :].astype(f32))
+        value = pieces.plus(pieces.times(normed, mods, 4, i, 1.0), mods, 3, i)
+        hidden0[pieces.at(i), :] = value.astype(bf16)
+        arrivals.append(pieces.swap(hidden0, hidden1, x_sems, i, 0))
+    load.wait()
+    block = 768 if inner % 768 == 0 else inner
+
+    def through(hidden, pre, act, at):
+        for start in range(0, inner, block):
+            cols = slice(start, start + block)
+            value = dot(hidden[at, :], w[:, cols])
+            pre[at, cols] = value
+            act[at, cols] = gelu_tanh(value).astype(bf16)
+
+    w_down = w[:, inner:]
+    everything = pl.ds(0, stream.shape[0])
+    through(hidden0, pre0, act0, everything)
+    for i, arrival in enumerate(arrivals):
+        at = pieces.at(i)
+        arrival.wait_recv()
+        through(hidden1, pre1, act1, at)
+        part_out[at, :] = dot_nt(act1[at, :], w_down).astype(bf16)
+        swaps.append(pieces.swap(part_out, part_in, x_sems, i, pieces.number))
+    keep[...] = dot_nt(act0[...], w_down)
+    sublayer_end(
+        pieces, stream, mods, 5, keep, part_in, swaps,
+        (stream_out, stream_low, branch_out, squares, rows, clips),
+    )
+    for copy in arrivals + swaps:
+        copy.wait_send()
+
+
+def forward_call(layer, attends, stream, mod, weights, hidden=None, shard=None):
+    rows, clips, count = layer.rows, layer.clips, layer.rows * layer.tokens
+    width = weights.shape[0]
+    inner = weights.shape[1] // (4 if attends else 2)
+    number = rows if layer.spatial else 2
+    ring = lax.axis_size("dp") // 4 if shard is not None else 0
+    vmem, anywhere = pl.BlockSpec(memory_space=pltpu.VMEM), pl.BlockSpec(memory_space=pl.ANY)
+    args, specs = [stream, mod.reshape(-1, width)], [vmem, vmem]
+    if hidden:
+        args, specs = args + list(hidden), specs + [vmem, vmem]
+    args, specs = args + [weights], specs + [anywhere]
+    shape = jax.ShapeDtypeStruct
+    outs = [shape((count, width), kind) for kind in (f32, bf16, f32)]
+    outs.append(shape((2, rows // clips, 128), f32))
+    if attends:
+        outs += [shape((count, 3 * inner), bf16)] * 2 + [shape((count, inner), bf16)] * 2
+        if not hidden:
+            outs += [shape((count, width), bf16)] * 2
+    else:
+        outs += [shape((count, width), bf16)] * 2
+        outs += [shape((count, inner), f32)] * 2 + [shape((count, inner), bf16)] * 2
+    out_specs = [vmem] * len(outs)
+    scratch = [pltpu.VMEM(weights.shape, bf16), pltpu.SemaphoreType.DMA]
+    scratch += [pltpu.VMEM((count, width), bf16)] * 2 + [pltpu.VMEM((count, width), f32)]
+    scratch += [pltpu.SemaphoreType.DMA((2, 2 * number))]
+    if ring:
+        args, specs = args + [shard], specs + [anywhere]
+        outs.append(shape((4 * ring,) + shard.shape, bf16))
+        out_specs.append(anywhere)
+        scratch += Gather.scratch(ring)
+    if attends:
+        kernel = functools.partial(attention_kernel, rows, clips, layer.spatial, bool(hidden), ring)
+    else:
+        kernel = functools.partial(mlp_kernel, rows, clips, layer.spatial)
+    return pl.pallas_call(
+        kernel,
+        in_specs=specs,
+        out_specs=out_specs,
+        out_shape=outs,
+        scratch_shapes=scratch,
+        cost_estimate=pl.CostEstimate(flops=1 << 35, bytes_accessed=1 << 25, transcendentals=0),
+        compiler_params=pltpu.CompilerParams(
+            collective_id=6 + 2 * attends + layer.spatial, has_side_effects=True, vmem_limit_bytes=60 << 20
+        ),
+    )(*args)
+
+
+def gelu_slope(value):
+    root, cubic = 0.7978845608028654, 0.044715
+    square = value * value
+    bend = jnp.tanh(root * (value + cubic * square * value))
+    return 0.5 * (1.0 + bend) + 0.5 * value * (1.0 - bend * bend) * root * (1.0 + 3.0 * cubic * square)
+
+
+def mlp_back_kernel(rows, clips, extra, packed, *refs):
+    grad, branch, stream, mods, hidden0, hidden1, pre0, pre1, act0, act1, weights, *refs = refs
+    others, refs = refs[:extra], refs[extra:]
+    grad_out, dmod_out, *refs = refs
+    gw_outs, refs = refs[: 2 - packed], refs[2 - packed :]
+    other_outs, refs = refs[:extra], refs[extra:]
+    w, w_sem, db0, db1, part_out, part_in, keep, dpre0, dpre1, gw, gw_sem, x_sems, *refs = refs
+    inner = act0.shape[1]
+    jobs = [
+        Scatter(others[i], other_outs[i], refs[7 * i : 7 * i + 7], lambda j: False) for i in range(extra)
+    ]
+    greeted = [{"tensor": 1 - lax.axis_index("tensor")}]
+    if extra:
+        greeted += jobs[0].neighbours()
+    greet(greeted)
+    load = pltpu.make_async_copy(weights, w, w_sem)
+    load.start()
+    db0[...] = (
+        (spread(grad[...].astype(f32), rows, clips) * clip_rows(mods, clips, 5)).reshape(grad.shape).astype(bf16)
+    )
+    first = Swap(db0, db1, x_sems, 0)
+    pipeline = Pipeline()
+    pipeline.add(jobs)
+    tick = pipeline.tick
+    dgate = clip_sums(grad[...].astype(f32) * branch[...], rows, clips)
+    load.wait()
+    block = 768 if inner % 768 == 0 else inner
+
+    def through(db, pre, dpre):
+        for start in range(0, inner, block):
+            cols = slice(start, start + block)
+            dact = dot(db[...], w[:, inner + start : inner + start + block])
+            dpre[:, cols] = (dact * gelu_slope(pre[:, cols])).astype(bf16)
+        tick()
+
+    tick()
+    through(db0, pre0, dpre0)
+    first.copy.wait_recv()
+    through(db1, pre1, dpre1)
+    part_out[...] = dot_nt(dpre1[...], w[:, :inner]).astype(bf16)
+    second = Swap(part_out, part_in, x_sems, 1)
+    tick()
+    keep[...] = dot_nt(dpre0[...], w[:, :inner])
+    tick()
+    both = lambda a, b, cols: jnp.concatenate([a[:, cols], b[:, cols]], axis=0)
+    whole = slice(0, grad.shape[1])
+    stored = []
+    for p, (left, right) in enumerate((((hidden0, hidden1), (dpre0, dpre1)), ((db0, db1), (act0, act1)))):
+        tall = both(*left, whole)
+        for start in range(0, inner, block):
+            slot = len(stored) % 2
+            if len(stored) > 1:
+                stored[-2].wait()
+            gw[slot] = dot_tn(tall, both(*right, slice(start, start + block))).astype(bf16)
+            at = start + inner if packed and p else start
+            out = gw_outs[0 if packed else p].at[:, pl.ds(at, block)]
+            copy = pltpu.make_async_copy(gw.at[slot], out, gw_sem.at[slot])
+            copy.start()
+            stored.append(copy)
+            if len(stored) % 2:
+                tick()
+    second.copy.wait_recv()
+    result, dshift, dscale = norm_back_rows(
+        grad[...], keep[...] + part_in[...].astype(f32), stream[...], clip_rows(mods, clips, 4), rows, clips
+    )
+    grad_out[...] = result
+    for k, value in enumerate((dshift, dscale, dgate)):
+        dmod_out[k * clips : (k + 1) * clips] = value
+    pipeline.finish()
+    for copy in stored[-2:]:
+        copy.wait()
+    for exchange in (first, second):
+        exchange.copy.wait_send()
+
+
+def mlp_back_call(layer, grad, mod, stored, packed, others=()):
+    stream, branch, hidden, pre, active, weights = stored
+    rows, clips, count = layer.rows, layer.clips, layer.rows * layer.tokens
+    width, inner, ring = weights.shape[0], active[0].shape[1], lax.axis_size("dp") // 4
+    share = width // (4 * ring)
+    others = [g.reshape(ring, 2, 2, share, g.shape[1]) for g in others]
+    vmem, anywhere = pl.BlockSpec(memory_space=pltpu.VMEM), pl.BlockSpec(memory_space=pl.ANY)
+    args = [layer.flat(grad), layer.flat(branch), layer.flat(stream), mod.reshape(-1, width)]
+    args += [*hidden, *pre, *active]
+    specs = [vmem] * len(args) + [anywhere] * (1 + len(others))
+    args += [weights, *others]
+    shape = jax.ShapeDtypeStruct
+    gw = [shape((width, 2 * inner), bf16)] if packed else [shape((width, inner), bf16)] * 2
+    outs = [shape((count, width), f32), shape((3 * clips, width), f32)] + gw
+    outs += [shape((share, g.shape[-1]), f32) for g in others]
+    block = 768 if inner % 768 == 0 else inner
+    scratch = [pltpu.VMEM(weights.shape, bf16), pltpu.SemaphoreType.DMA]
+    scratch += [pltpu.VMEM((count, width), bf16)] * 4 + [pltpu.VMEM((count, width), f32)]
+    scratch += [pltpu.VMEM((count, inner), bf16)] * 2
+    scratch += [pltpu.VMEM((2, width, block), bf16), pltpu.SemaphoreType.DMA((2,))]
+    scratch += [pltpu.SemaphoreType.DMA((2, 2))]
+    for g in others:
+        scratch += Scatter.scratch(ring, share, g.shape[-1], False)
+    return pl.pallas_call(
+        functools.partial(mlp_back_kernel, rows, clips, len(others), packed),
+        in_specs=specs,
+        out_specs=[vmem, vmem] + [anywhere] * len(gw) + [vmem] * len(others),
+        out_shape=outs,
+        scratch_shapes=scratch,
+        cost_estimate=pl.CostEstimate(flops=1 << 35, bytes_accessed=1 << 25, transcendentals=0),
+        compiler_params=pltpu.CompilerParams(
+            collective_id=4 + layer.spatial, has_side_effects=True, vmem_limit_bytes=62 << 20
+        ),
+    )(*args)
+
+
 def tail_kernel(count, pairs, *refs):
     grads, small = refs[:count], refs[count]
     outs, small_out = refs[count + 1 : 2 * count + 1], refs[2 * count + 1]
@@ -422,8 +1053,9 @@
     ]
     total = SmallSum(pairs, small, small_out, scratch[7 * count :])
     greet(total.partners + [{"dp": jobs[0].after}, {"dp": jobs[0].before}])
-    pipeline = Pipeline(jobs)
+    pipeline = Pipeline()
     total.tick()
+    pipeline.add(jobs)
     for _ in range(len(pairs)):
         pipeline.tick()
         total.tick()
@@ -578,10 +1210,10 @@
         return grad, jnp.stack([shift, scale, gate], axis=1), grad_w
 
 
-def to_places(stream):
+def to_places(stream, kind=f32):
     return lax.all_to_all(
         stream.astype(bf16), "dp", split_axis=1, concat_axis=0, tiled=True
-    ).astype(f32)
+    ).astype(kind)
 
 
 def to_frames(stream):
@@ -808,6 +1440,11 @@
     return local[:, :cut].reshape(first.shape), local[:, cut:].T
 
 
+def finish_spatial(gw_mlp, gw_attn, dmod_attn, dmod_mlp):
+    small = jnp.concatenate([dmod_attn.reshape(-1), dmod_mlp.reshape(-1)]).reshape(-1, 128)
+    return tail([*gw_mlp, gw_attn], small)
+
+
 def body(
     video_in,
     condition,
@@ -842,50 +1479,102 @@
     w_attn_s, mods, hidden = head(pack(qkv_spatial, proj_spatial), mods, video_in, clips)
 
     keep = lambda value: value
-    stream0 = video_in.astype(f32)
-    shard, mods = tie(pack(qkv_temporal, proj_temporal), mods)
     mod_s, mod_t = mods.reshape(2, clips, 6, width)
-    later = WeightGather(shard)
-    s1, g1, kept1 = spatial.attention(stream0, mod_s, w_attn_s, later.step, hidden)
-    s2, g2, kept2 = spatial.mlp(s1, mod_s, w_mlp_s, later.step)
-    placed = later.step(to_places(s2))
-    w_attn_t = later.finish()
-    placed, grad_output = tie(placed, grad_output)
-    grad = to_places(grad_output)
-    s3, g3, kept3 = temporal.attention(placed, mod_t, w_attn_t, keep)
-    s4, g4, kept4 = temporal.mlp(s3, mod_t, w_mlp_t, keep)
-    video_out = to_frames(s4)
-    squares = jnp.stack(
-        [spatial.by_frame(v) for v in (s1, s2)]
-        + [temporal.by_frame(v) for v in (s3, s4)]
-        + [spatial.by_frame(v) for v in (g1, g2)]
-        + [temporal.by_frame(v) for v in (g3, g4)]
-    )
-
-    grad, dmod4, (gw4,) = temporal.mlp_back(grad, mod_t, kept4, False, keep)
-    own4 = scatter_grads(gw4)
-    grad, dmod3, (gw3,) = temporal.attention_back(grad, mod_t, kept3, False, keep)
-    early = AllSum(
-        jnp.concatenate([dmod3.reshape(-1), dmod4.reshape(-1), squares.reshape(-1)]).reshape(-1, 128)
-    )
-    grad = early.step(to_frames(grad).astype(f32))
-    grad, dmod2, gw2 = spatial.mlp_back(grad, mod_s, kept2, True, early.step)
-    grad, own4, gw3 = tie(grad, own4, gw3)
-    own3 = scatter_grads(gw3)
+    fused = lax.axis_size("tensor") == 2 and rows % clips == 0
+    if fused:
+        flat = video_in.reshape(rows * tokens, width)
+        mine = [spatial.flat(h) for h in hidden]
+        s1, _, b1, q1, *kept1, w_attn_t = forward_call(
+            spatial, True, flat, mod_s, w_attn_s, mine, pack(qkv_temporal, proj_temporal)
+        )
+        w_attn_t = w_attn_t.reshape(width, -1)
+        kept1 = (flat, b1, mine, kept1[:2], kept1[2:])
+        s2, low2, b2, q2, *kept2 = forward_call(spatial, False, s1, mod_s, w_mlp_s)
+        kept2 = (s1, b2, kept2[:2], kept2[2:4], kept2[4:])
+        placed = to_places(spatial.full(low2), bf16).reshape(-1, width)
+        placed, grad_output = tie(placed, grad_output)
+        s3, _, b3, q3, *kept3 = forward_call(temporal, True, placed, mod_t, w_attn_t)
+        kept3 = (placed, b3, kept3[4:], kept3[:2], kept3[2:4])
+        grad = to_places(grad_output, bf16)
+        _, low4, b4, q4, *kept4 = forward_call(temporal, False, s3, mod_t, w_mlp_t)
+        kept4 = (s3, b4, kept4[:2], kept4[2:4], kept4[4:])
+        spots = []
+        for layer, values in ((spatial, (q1, q2)), (temporal, (q3, q4))):
+            for value in values:
+                empty = jnp.zeros((2, FRAMES), f32)
+                spots.append(
+                    lax.dynamic_update_slice_in_dim(empty, value[:, :, 0], layer.first_row // clips, 1)
+                )
+        squares = jnp.concatenate([jnp.stack([v[i] for v in spots]) for i in range(2)])
+    else:
+        stream0 = video_in.astype(f32)
+        shard, mods = tie(pack(qkv_temporal, proj_temporal), mods)
+        mod_s, mod_t = mods.reshape(2, clips, 6, width)
+        later = WeightGather(shard)
+        s1, g1, kept1 = spatial.attention(stream0, mod_s, w_attn_s, later.step, hidden)
+        s2, g2, kept2 = spatial.mlp(s1, mod_s, w_mlp_s, later.step)
+        placed = later.step(to_places(s2))
+        w_attn_t = later.finish()
+        placed, grad_output = tie(placed, grad_output)
+        grad = to_places(grad_output)
+        s3, g3, kept3 = temporal.attention(placed, mod_t, w_attn_t, keep)
+        s4, g4, kept4 = temporal.mlp(s3, mod_t, w_mlp_t, keep)
+        video_out = to_frames(s4)
+        squares = jnp.stack(
+            [spatial.by_frame(v) for v in (s1, s2)]
+            + [temporal.by_frame(v) for v in (s3, s4)]
+            + [spatial.by_frame(v) for v in (g1, g2)]
+            + [temporal.by_frame(v) for v in (g3, g4)]
+        )
+    by_span = lambda dmod: jnp.moveaxis(dmod.reshape(3, clips, width), 0, 1)
+    if fused:
+        grad, dmod4, gw4 = mlp_back_call(temporal, grad, mod_t, (*kept4[:5], w_mlp_t), True)
+        own4 = scatter_grads(gw4)
+        video_out = to_frames(temporal.full(low4))
+        grad, video_out = tie(grad, video_out)
+        grad, dmod3, gw3 = attention_back_call(temporal, grad, mod_t, (*kept3[:5], w_attn_t))
+        grad = temporal.full(grad)
+    else:
+        grad, dmod4, (gw4,) = temporal.mlp_back(grad, mod_t, kept4, False, keep)
+        own4 = scatter_grads(gw4)
+        grad, dmod3, (gw3,) = temporal.attention_back(grad, mod_t, kept3, False, keep)
+        own3 = scatter_grads(gw3)
+    if fused:
+        grad, dmod2, up, down = mlp_back_call(
+            spatial, to_frames(grad), mod_s, (*kept2[:5], w_mlp_s), False
+        )
+        own4, gw3 = tie(own4, gw3)
+        own3 = scatter_grads(gw3)
+        line = jnp.pad(squares.reshape(1, -1), ((0, 0), (0, width - squares.size)))
+        small = jnp.concatenate([dmod2, dmod3, dmod4, line], axis=0)
+        grad, grad_up_s, down_s, own1, late = attention_back_call(
+            spatial, grad, mod_s, (*kept1[:5], w_attn_s), (up, down), small
+        )
+        grad = spatial.full(grad)
+        dmod1, dmod2, dmod3, dmod4 = [
+            by_span(late[3 * clips * i : 3 * clips * (i + 1)]) for i in range(4)
+        ]
+        squares = late[12 * clips, : squares.size].reshape(8, FRAMES)
+    else:
+        early = AllSum(
+            jnp.concatenate([dmod3.reshape(-1), dmod4.reshape(-1), squares.reshape(-1)]).reshape(-1, 128)
+        )
+        grad = early.step(to_frames(grad).astype(f32))
+        grad, dmod2, gw2 = spatial.mlp_back(grad, mod_s, kept2, True, early.step)
+        grad, own4 = tie(grad, own4)
+        grad, dmod1, (gw1,) = spatial.attention_back(grad, mod_s, kept1, False, early.step)
+        grad_up_s, down_s, own1, late = finish_spatial(gw2, gw1, dmod1, dmod2)
+        late = late.reshape(2, clips, 3, width)
+        dmod1, dmod2 = late[0], late[1]
+        cut = clips * 3 * width
+        flat_early = early.finish().reshape(-1)
+        dmod3 = flat_early[:cut].reshape(clips, 3, width)
+        dmod4 = flat_early[cut : 2 * cut].reshape(clips, 3, width)
+        squares = flat_early[2 * cut :].reshape(8, FRAMES)
     grad_up_t, grad_down_t = unpack(own4, up_temporal, down_temporal)
     grad_qkv_t, grad_proj_t = unpack(own3, qkv_temporal, proj_temporal)
-    grad, dmod1, (gw1,) = spatial.attention_back(grad, mod_s, kept1, False, early.step)
-    small = jnp.concatenate([dmod1.reshape(-1), dmod2.reshape(-1)]).reshape(-1, 128)
-    grad_up_s, down_s, own1, late = tail([*gw2, gw1], small)
     grad_down_s = down_s.T
     grad_qkv_s, grad_proj_s = unpack(own1, qkv_spatial, proj_spatial)
-    late = late.reshape(2, clips, 3, width)
-    dmod1, dmod2 = late[0], late[1]
-    cut = clips * 3 * width
-    flat_early = early.finish().reshape(-1)
-    dmod3 = flat_early[:cut].reshape(clips, 3, width)
-    dmod4 = flat_early[cut : 2 * cut].reshape(clips, 3, width)
-    squares = flat_early[2 * cut :].reshape(8, FRAMES)
     frame_rms = jnp.sqrt(squares / (clips * PATCHES * width))
     shift_grad = jnp.stack([d[:, 0] for d in (dmod1, dmod2, dmod3, dmod4)])
     silu_wide = silu_low.astype(f32)

time: 686 us -> 681 us (level)
  Pallas kernels: 246 us -> 528 us
  waiting for transfers between devices: 146 us -> 17.3 us
  matrix products: 117 us -> 3.61 us
  blocking collectives: 0 us -> 55.9 us
  starting transfers between devices: 49.8 us -> 8.27 us
  local copies, waits for them, and re-layouts: 68.2 us -> 31.6 us
  other arithmetic: 32.6 us -> 10.4 us
    pallas_call x12 -> x8, Pallas kernels: 179 us -> 461 us  [the longest x2 210 us: attention_back_call(): pl.pallas_call(functools.partial(attention_back_kernel, rows, clips, laye...]
    ppermute x25 -> x0, waiting for transfers between devices: 118 us -> none  [the longest x22 106 us: swap(): return lax.ppermute(value, axis, [(i, i ^ stride) for i in range(size)])]
    dot_general x18 -> x2, matrix products: 62.1 us -> 0.56 us  [dot(): return jnp.dot(a, b, preferred_element_type=f32)]
    all_to_all x0 -> x2, blocking collectives: none -> 55.9 us  [the longest x1 34.6 us: to_places(): lax.all_to_all(stream.astype(bf16), 'dp', split_axis=1, concat_axis=0, ti...]
    dot_general x16 -> x0, matrix products: 52.3 us -> none  [dot_nt(): lax.dot_general(a, b, (((1,), (1,)), ((), ())), preferred_element_type=f32)]
    ppermute x25 -> x0, starting transfers between devices: 24.2 us -> none  [the longest x22 20.7 us: swap(): return lax.ppermute(value, axis, [(i, i ^ stride) for i in range(size)])]
    unnamed x266 -> x67, local copies, waits for them, and re-layouts: 28.9 us -> 12.4 us
    reduce_sum x23 -> x0, other arithmetic: 15 us -> none  [the longest x3 3.94 us: branch_back(): grad_gate = self.by_clip(jnp.sum(grad * branch, axis=1))]
  transfers between devices with their start and end apart: 33 -> 6, of which waited for: 16 -> 1; matrix products, arithmetic and copies ran while one was open for 27% -> 4% of each run, Pallas kernels for 36% -> 74%
where the time goes in v4:
time: 681 us; the launch traced here: 670 us
  Pallas kernels  528 us (78%)
  blocking collectives  55.9 us (8%)
  local copies, waits for them, and re-layouts  31.6 us (5%)
  waiting for transfers between devices  17.3 us (3%)
  between operations  14.6 us (2%)
  other arithmetic  10.4 us (2%)
  starting transfers between devices  8.27 us (1%)
    pallas_call x2, Pallas kernels, attention_back_call(): pl.pallas_call(functools.partial(attention_back_kernel, rows, clips, laye...  210 us
    pallas_call x4, Pallas kernels, forward_call(): pl.pallas_call(kernel, in_specs=specs, out_specs=out_specs, out_shape=out...  177 us
    pallas_call x2, Pallas kernels, mlp_back_call(): pl.pallas_call(functools.partial(mlp_back_kernel, rows, clips, len(others...  74 us
    pallas_call x1, Pallas kernels, head(): pl.pallas_call(functools.partial(head_kernel, ring, clips, pairs), in_spe...  66.8 us
    all_to_all x1, blocking collectives, to_places(): lax.all_to_all(stream.astype(bf16), 'dp', split_axis=1, concat_axis=0, ti...  34.6 us
    all_to_all x1, blocking collectives, to_frames(): lax.all_to_all(stream.astype(bf16), 'dp', split_axis=0, concat_axis=1, ti...  21.3 us
    all_to_all x1, waiting for transfers between devices, to_frames(): lax.all_to_all(stream.astype(bf16), 'dp', split_axis=0, concat_axis=1, ti...  17.1 us
  transfers between devices with their start and end apart: 6, of which 1 were waited for; matrix products, arithmetic and copies ran while one was open for 4% of the time, Pallas kernels for 74%

profile of v4, /device:TPU:0, one launch (start us, length us, event | category | flops | bytes accessed | tf_op | source)
XLA Modules:
  0.0 669.9 jit_solution(14364127431218200529)
XLA Ops:
  7.2 2.0 pad_maximum_fusion
  9.4 0.9 pad_maximum_fusion.1
  11.6 1.4 fusion.3
  15.6 66.8 %shard_map.244 = (bf16[16,72,2304]{2,1,0:T(8,128)(2,1)S(1)}, f32[24,1152]{1,0:T(8,128)S(1)}, bf16[2,128,1152]{2,1,0:T(8,128)(2,1)S(1)}, bf16[2,128,1152]{2,1,0:T(8,128)(2,1)S(1)}) custom-call(bf16[72,2304]{1,0:T(8,128)(2,1)S(1)} %pad_maximum_fusion.2.shard, f32[24,1152]{1,0:T(8,128)S(1)} %reshape.137.small, bf16[2,128,1152]{2,1,0:T(8,128)(2,1)S(1)} %copy-done), custom_call_target="tpu_custom_call" | custom-call | flops 34359738368 | bytes 5308416 | tf_op jit(solution)/shard_map/pallas_call | solution.py:1339
  82.5 2.4 copy-done.1
  87.2 69.0 %shard_map.245 = (f32[256,1152]{1,0:T(8,128)}, bf16[256,1152]{1,0:T(8,128)(2,1)}, f32[256,1152]{1,0:T(8,128)}, f32[2,1,128]{2,1,0:T(1,128)}, bf16[256,1728]{1,0:...) custom-call(bf16[256,1152]{1,0:T(8,128)(2,1)} %bitcast.95, ...), custom_call_target="tpu_custom_call" | custom-call | flops 34359738368 | bytes 33554432 | tf_op jit(solution)/shard_map/pallas_call | solution.py:915
  156.2 34.5 %shard_map.246 = (f32[256,1152]{1,0:T(8,128)}, bf16[256,1152]{1,0:T(8,128)(2,1)}, f32[256,1152]{1,0:T(8,128)}, f32[2,1,128]{2,1,0:T(1,128)}, bf16[256,1152]{1,0:...) custom-call(f32[256,1152]{1,0:T(8,128)} %get-tuple-element.79.refs_0, ...), custom_call_target="tpu_custom_call" | custom-call | flops 34359738368 | bytes 33554432 | tf_op jit(solution)/shard_map/pallas_call | solution.py:915
  190.7 1.7 copy.71
  192.4 34.6 %all_to_all.63 = bf16[2,128,1152]{2,0,1:T(2,128)(2,1)S(1)} all-to-all(bf16[2,128,1152]{2,0,1:T(2,128)(2,1)S(1)} %copy.71), channel_id=1, replica_groups=mesh['dp'=16,'tensor'=2] {'dp'}, dimensions={1} | all-to-all | bytes 1179648 | tf_op jit(solution)/shard_map/all_to_all | solution.py:1214
  228.5 1.7 copy.93
  230.2 4.3 all-to-all-start.1
  234.8 40.2 %shard_map.247 = (f32[256,1152]{1,0:T(8,128)}, bf16[256,1152]{1,0:T(8,128)(2,1)}, f32[256,1152]{1,0:T(8,128)}, f32[2,16,128]{2,1,0:T(8,128)}, bf16[256,1728]{1,0...) custom-call(bf16[256,1152]{1,0:T(8,128)(2,1)} %bitcast.118, ...), custom_call_target="tpu_custom_call" | custom-call | flops 34359738368 | bytes 33554432 | tf_op jit(solution)/shard_map/pallas_call | solution.py:915
  275.0 33.6 %shard_map.248 = (f32[256,1152]{1,0:T(8,128)}, bf16[256,1152]{1,0:T(8,128)(2,1)}, f32[256,1152]{1,0:T(8,128)}, f32[2,16,128]{2,1,0:T(8,128)}, bf16[256,1152]{1,0...) custom-call(f32[256,1152]{1,0:T(8,128)} %get-tuple-element.84.refs_0, ...), custom_call_target="tpu_custom_call" | custom-call | flops 34359738368 | bytes 33554432 | tf_op jit(solution)/shard_map/pallas_call | solution.py:915
  308.6 0.9 copy.75
  309.5 34.7 %shard_map.249 = (f32[256,1152]{1,0:T(8,128)}, f32[6,1152]{1,0:T(8,128)}, bf16[1152,4608]{1,0:T(8,128)(2,1)}) custom-call(bf16[256,1152]{1,0:T(8,128)(2,1)} %bitcast.122, f32[256,1152]{1,0:T(8,128)} %get-tuple-element.85.refs_1_, f32[256,1152]{1,0:T(8,128)} %get-tuple-element.84.refs_0_.refs_2_, f32[12,1152]{1,0:T(8,128)} %get-tuple-element.207.refs_1_.refs_3_, ...), custom_call_target="tpu_custom_call" | custom-call | flops 34359738368 | bytes 33554432 | tf_op jit(solution)/shard_map/pallas_call | solution.py:1033
  344.3 1.0 copy-done.15
  345.3 21.3 %all_to_all.64 = bf16[32,8,1152]{2,1,0:T(8,128)(2,1)S(1)} all-to-all(bf16[32,8,1152]{2,1,0:T(8,128)(2,1)S(1)} %bitcast.120), channel_id=1, replica_groups=mesh['dp'=16,'tensor'=2] {'dp'}, dimensions={0} | all-to-all | bytes 1179648 | tf_op jit(solution)/shard_map/all_to_all | solution.py:1220
  367.5 43.5 %shard_map.250 = (f32[256,1152]{1,0:T(8,128)}, f32[6,1152]{1,0:T(8,128)}, bf16[1152,2304]{1,0:T(8,128)(2,1)}) custom-call(f32[256,1152]{1,0:T(8,128)} %get-tuple-element.95.refs_0_, f32[256,1152]{1,0:T(8,128)} %get-tuple-element.96.refs_1_, bf16[256,1152]{1,0:T(8,128)(2,1)} %bitcast.119, f32[12,1152]{1,0:T(8,128)} %get-tuple-element.207.refs_1_.refs_3_, ...), custom_call_target="tpu_custom_call" | custom-call | flops 34359738368 | bytes 33554432 | tf_op jit(solution)/shard_map/pallas_call | solution.py:623
  411.0 2.2 convert_bitcast_fusion
  413.2 3.6 all-to-all-start.3
  417.4 17.1 %all-to-all-done.3 = bf16[32,8,1152]{2,1,0:T(8,128)(2,1)S(1)} async-done(((bf16[32,8,1152]{2,1,0:T(8,128)(2,1)}), bf16[32,8,1152]{2,1,0:T(8,128)(2,1)S(1)}, u32[]{:S(2)}, u32[]{:S(2)}) %all-to-all-start.3) | async-done | bytes 589856 | tf_op jit(solution)/shard_map/all_to_all | solution.py:1220
  435.4 39.3 %shard_map.251 = (f32[256,1152]{1,0:T(8,128)}, f32[6,1152]{1,0:T(8,128)}, bf16[1152,2304]{1,0:T(8,128)(2,1)}, bf16[1152,2304]{1,0:T(8,128)(2,1)}) custom-call(bf16[256,1152]{1,0:T(8,128)(2,1)} %bitcast.121, f32[256,1152]{1,0:T(8,128)} %get-tuple-element.104.refs_1_, f32[256,1152]{1,0:T(8,128)} %get-tuple-element.79.refs_0_.refs_2_, ...), custom_call_target="tpu_custom_call" | custom-call | flops 34359738368 | bytes 33554432 | tf_op jit(solution)/shard_map/pallas_call | solution.py:1033
  476.2 166.5 %shard_map.252 = (f32[256,1152]{1,0:T(8,128)}, f32[72,2304]{1,0:T(8,128)}, f32[72,2304]{1,0:T(8,128)}, f32[72,2304]{1,0:T(8,128)}, f32[25,1152]{1,0:T(8,128)}) custom-call(f32[256,1152]{1,0:T(8,128)} %get-tuple-element.111.refs_0_, f32[256,1152]{1,0:T(8,128)} %get-tuple-element.112.refs_1_, bf16[256,1152]{1,0:T(8,128)(2,1)} %bitcast.96, ...), custom_call_target="tpu_custom_call" | custom-call | flops 34359738368 | bytes 33554432 | tf_op jit(solution)/shard_map/pallas_call | solution.py:623
  642.7 1.0 fusion.4
  644.7 1.4 copy.94
  646.1 1.4 copy.95
  651.7 1.7 slice_bitcast_fusion.2
  653.4 2.2 fusion.2
  655.7 0.9 slice.126
  656.6 0.9 slice_bitcast_fusion
  657.5 1.0 slice.124
  660.5 1.0 copy.103
  (123 shorter events, 20.6 us)
Async XLA Ops:
  7.2 2.2 copy-start.16
  7.2 2.2 copy-start.17
  7.2 149.0 %all-gather.3.cloned.1.call-start = ((), (), s32[]{:S(2)}) async-start(), calls=%async_computation.6 | async-start | bytes 11280384 | tf_op jit(solution)/shard_map/all_gather | solution.py:1228
  9.3 1.4 copy-start.6
  9.3 265.7 %all-gather.5.cloned.1.call-start = ((), (), s32[]{:S(2)}) async-start(), calls=%async_computation.7 | async-start | bytes 11280384 | tf_op jit(solution)/shard_map/all_gather | solution.py:1228
  10.2 1.3 copy-start.4
  11.6 2.1 copy-start.18
  13.3 1.0 copy-start.19
  13.7 0.9 copy-start.20
  13.9 0.9 copy-start.21
  14.2 1.4 copy-start
  82.5 2.4 copy-start.1
  84.9 0.8 copy-start.2
  227.0 1.5 copy-start.10
  230.2 78.4 %all-to-all-start.1 = ((bf16[2,128,1152]{2,0,1:T(2,128)(2,1)}), bf16[2,128,1152]{2,0,1:T(2,128)(2,1)S(1)}, u32[]{:S(2)}, u32[]{:S(2)}) async-start(bf16[2,128,1152]{2,0,1:T(2,128)(2,1)} %copy.93), calls=%async_computation.1 | async-start | bytes 1179648 | tf_op jit(solution)/shard_map/all_to_all | solution.py:1214
  234.6 240.1 %reduce-scatter.3.cloned.1.call-start = ((), (), s32[]{:S(2)}) async-start(), calls=%async_computation.8 | async-start | bytes 11280384 | tf_op jit(solution)/shard_map/reduce_scatter | solution.py:1434
  344.2 1.1 copy-start.15
  411.0 5.9 copy-start.28
  411.0 5.9 copy-start.29
  411.0 6.0 copy-start.26
  411.0 6.1 copy-start.25
  413.2 21.3 %all-to-all-start.3 = ((bf16[32,8,1152]{2,1,0:T(8,128)(2,1)}), bf16[32,8,1152]{2,1,0:T(8,128)(2,1)S(1)}, u32[]{:S(2)}, u32[]{:S(2)}) async-start(bf16[32,8,1152]{2,1,0:T(8,128)(2,1)} %convert_bitcast_fusion), calls=%async_computation.3 | async-start | bytes 1179648 | tf_op jit(solution)/shard_map/all_to_all | solution.py:1220
  416.8 240.7 %reduce-scatter.5.cloned.1.call-start = ((), (), s32[]{:S(2)}) async-start(), calls=%async_computation.9 | async-start | bytes 5640192 | tf_op jit(solution)/shard_map/reduce_scatter | solution.py:1434
  476.2 167.7 %copy-start.27 = (f32[2,72]{1,0:T(2,128)S(1)}, f32[2,72]{1,0:T(2,128)}, u32[]{:S(2)}) copy-start(f32[2,72]{1,0:T(2,128)} %get-tuple-element.201) | copy-start | bytes 1732
  646.1 1.4 copy-start.12
  647.5 2.6 copy-start.5
  647.8 5.6 copy-start.7
  648.7 6.9 %copy-start.8 = (bf16[72,4608]{1,0:T(8,128)(2,1)S(1)}, bf16[72,4608]{1,0:T(8,128)(2,1)}, u32[]{:S(2)}) copy-start(bf16[72,4608]{1,0:T(8,128)(2,1)} %reduce-scatter.3.cloned.1.call-done) | copy-start | bytes 1990660
  658.5 1.1 copy-start.9
  658.8 1.7 copy-start.11
  659.7 1.8 copy-start.14
  660.5 1.9 copy-start.13
  (4 other events, 3.1 us)
Sparse Core Ops, SparseCore 0:
  10.9 130.5 all-gather.2
  144.4 110.6 all-gather.4
  344.4 125.7 reduce-scatter.2
  474.9 142.1 reduce-scatter.4

commit v5 on v4

--- a/solution.py
+++ b/solution.py
@@ -426,6 +426,42 @@
         self.copy.start()
 
 
+class Exchange:
+    def __init__(self, source, target, sems):
+        self.source, self.target = source, target
+        self.send_sem, self.recv_sem, self.own_sem = sems
+        self.size, self.me = source.shape[0], lax.axis_index("dp")
+
+    @staticmethod
+    def scratch(size):
+        return [pltpu.SemaphoreType.DMA((size - 1,))] * 2 + [pltpu.SemaphoreType.DMA]
+
+    def others(self):
+        return [{"dp": lax.rem(self.me + k, self.size)} for k in range(1, self.size)]
+
+    def start(self):
+        self.own = pltpu.make_async_copy(
+            self.source.at[self.me], self.target.at[self.me], self.own_sem
+        )
+        self.own.start()
+        self.copies = []
+        for k, partner in enumerate(self.others()):
+            copy = pltpu.make_async_remote_copy(
+                src_ref=self.source.at[partner["dp"]], dst_ref=self.target.at[self.me],
+                send_sem=self.send_sem.at[k], recv_sem=self.recv_sem.at[k],
+                device_id=partner, device_id_type=MESH,
+            )
+            copy.start()
+            self.copies.append(copy)
+
+    def finish(self):
+        self.own.wait()
+        for copy in self.copies:
+            copy.wait_recv()
+        for copy in self.copies:
+            copy.wait_send()
+
+
 def spread(value, rows, clips):
     return value.reshape(rows // clips, clips, value.shape[0] // rows, value.shape[1])
 
@@ -451,23 +487,22 @@
     return grad_in, clip_sums(grad_hidden, rows, clips), clip_sums(grad_hidden * normed, rows, clips)
 
 
-def gradient_blocks(target, value, cols):
+def gradient_blocks(target, value):
     ring, rows = target.shape[0], target.shape[3]
     for k in range(4 * ring):
-        target[k // 4, (k // 2) % 2, k % 2, :, cols] = value[k * rows : (k + 1) * rows].astype(bf16)
+        target[k // 4, (k // 2) % 2, k % 2] = value[k * rows : (k + 1) * rows].astype(bf16)
 
 
 def attention_back_kernel(rows, clips, spatial, extra, tailing, pairs, *refs):
     grad, branch, stream, mods, hidden0, hidden1, qkv0, qkv1, att0, att1, weights, *refs = refs
     others, refs = refs[:extra], refs[extra:]
     if tailing:
-        dmod_in, *refs = refs
-    grad_out, *refs = refs
+        dmod_in, grad_out, *refs = refs
     other_outs, refs = refs[:extra], refs[extra:]
     if tailing:
-        own_out, small_out, *refs = refs
+        own_outs, small_out, early_out, refs = refs[:4], refs[4], refs[5], refs[6:]
     else:
-        dmod_out, gw_out, *refs = refs
+        dmod_out, gw_out, landed, *refs = refs
     w, w_sem, db0, db1, part_out, part_in, keep, ga0, ga1, x_sems, *refs = refs
     dqkv, refs = (refs[:3], refs[3:6]), refs[6:]
     inner = att0.shape[1]
@@ -478,12 +513,17 @@
     refs = refs[7 * extra :]
     greeted = [{"tensor": 1 - lax.axis_index("tensor")}]
     if tailing:
-        small, gw, *refs = refs
-        own_job = Scatter(gw, own_out, refs[:7], lambda j: False)
-        total = SmallSum(pairs, small, small_out, refs[7:])
+        small, gw, refs = refs[0], refs[1:5], refs[5:]
+        own_jobs = [
+            Scatter(gw[i], own_outs[i], refs[7 * i : 7 * i + 7], lambda j: False) for i in range(4)
+        ]
+        total = SmallSum(pairs, small, small_out, refs[28:32])
+        early = SmallSum(pairs, dmod_in, early_out, refs[32:])
         greeted = total.partners + [{"dp": jobs[0].after}, {"dp": jobs[0].before}]
-    elif extra:
-        greeted += jobs[0].neighbours()
+    else:
+        low, *refs = refs
+        exchange = Exchange(low, landed, refs)
+        greeted += exchange.others()
     greet(greeted)
     load = pltpu.make_async_copy(weights, w, w_sem)
     load.start()
@@ -493,7 +533,12 @@
     first = Swap(db0, db1, x_sems, 0)
     pipeline = Pipeline()
     pipeline.add(jobs)
-    tick = pipeline.tick
+
+    def tick():
+        pipeline.tick()
+        if tailing:
+            early.tick()
+
     dgate = clip_sums(grad[...].astype(f32) * branch[...], rows, clips)
     load.wait()
     w_proj = w[:, 3 * inner :]
@@ -555,33 +600,38 @@
         value = dot_tn(left, right)
         cols = slice(p * inner, (p + 1) * inner)
         if tailing:
-            gradient_blocks(gw, value, cols)
+            gradient_blocks(gw[p], value)
         else:
             gw_out[:, cols] = value.astype(bf16)
         if p % 2:
             tick()
     if tailing:
-        pipeline.add([own_job])
+        pipeline.add(own_jobs)
     second.copy.wait_recv()
     result, dshift, dscale = norm_back_rows(
         grad[...], keep[...] + part_in[...].astype(f32), stream[...], clip_rows(mods, clips, 1), rows, clips
     )
-    grad_out[...] = result
+    if tailing:
+        grad_out[...] = result
+    else:
+        low[...] = result.reshape(low.shape).astype(bf16)
+        exchange.start()
     dmod = (dshift, dscale, dgate)
     if tailing:
         for k, value in enumerate(dmod):
             small[k * clips : (k + 1) * clips] = value
-        small[3 * clips :] = dmod_in[...]
         more = total.tick()
         while more:
             pipeline.tick()
             more = total.tick()
         pipeline.finish()
         total.finish()
+        early.finish()
     else:
         for k, value in enumerate(dmod):
             dmod_out[k * clips : (k + 1) * clips] = value
         pipeline.finish()
+        exchange.finish()
     for exchange in (first, second):
         exchange.copy.wait_send()
 
@@ -599,7 +649,7 @@
     specs = [vmem] * len(args) + [anywhere] * (1 + len(others))
     args += [weights, *others]
     shape = jax.ShapeDtypeStruct
-    outs = [shape((count, width), f32)]
+    outs = [shape((count, width), f32)] if dmod_in is not None else []
     scratch = [pltpu.VMEM(weights.shape, bf16), pltpu.SemaphoreType.DMA]
     scratch += [pltpu.VMEM((count, width), bf16)] * 4 + [pltpu.VMEM((count, width), f32)]
     scratch += [pltpu.VMEM((count, inner), bf16)] * 2 + [pltpu.SemaphoreType.DMA((2, 2))]
@@ -611,15 +661,18 @@
     if tailing:
         args.append(dmod_in)
         specs.append(vmem)
-        outs.append(shape((share, 4 * inner), f32))
-        total = (3 * clips + dmod_in.shape[0], width)
-        outs.append(shape(total, f32))
+        outs += [shape((share, inner), f32)] * 4
+        total = (3 * clips, width)
+        outs += [shape(total, f32), shape(dmod_in.shape, f32)]
         scratch.append(pltpu.VMEM(total, f32))
-        scratch.append(pltpu.VMEM((ring, 2, 2, share, 4 * inner), bf16))
-        scratch += Scatter.scratch(ring, share, 4 * inner, False)
-        scratch += SmallSum.scratch(len(pairs), total)
+        scratch += [pltpu.VMEM((ring, 2, 2, share, inner), bf16)] * 4
+        for _ in range(4):
+            scratch += Scatter.scratch(ring, share, inner, False)
+        scratch += SmallSum.scratch(len(pairs), total) + SmallSum.scratch(len(pairs), dmod_in.shape)
     else:
-        outs += [shape((3 * clips, width), f32), shape((width, 4 * inner), bf16)]
+        blocks = (4 * ring, count // (4 * ring), width)
+        outs += [shape((3 * clips, width), f32), shape((width, 4 * inner), bf16), shape(blocks, bf16)]
+        scratch += [pltpu.VMEM(blocks, bf16)] + Exchange.scratch(4 * ring)
     return pl.pallas_call(
         functools.partial(attention_back_kernel, rows, clips, layer.spatial, len(others), tailing, pairs),
         in_specs=specs,
@@ -735,7 +788,7 @@
     return jnp.broadcast_to(sums, (frames, 128))
 
 
-def sublayer_end(pieces, stream, mods, span, keep, part_in, swaps, outs):
+def sublayer_end(pieces, stream, mods, span, keep, part_in, swaps, outs, regroup=None):
     stream_out, stream_low, branch_out, squares, rows, clips = outs
     for i, swap_i in enumerate(swaps):
         at = pieces.at(i)
@@ -747,6 +800,14 @@
         total = stream[at, :].astype(f32) + gated
         stream_out[at, :] = total
         stream_low[at, :] = total.astype(bf16)
+        if regroup:
+            size, some = regroup.size, total.shape[0] // regroup.size
+            for d in range(size):
+                regroup.source[d, i * some : (i + 1) * some, :] = total[
+                    d * some : (d + 1) * some
+                ].astype(bf16)
+    if regroup:
+        regroup.start()
     squares[0] = frame_sums(stream_out[...], rows, clips)
     squares[1] = frame_sums(keep[...], rows, clips)
 
@@ -768,7 +829,8 @@
     inner, count = att0.shape[1], stream.shape[0]
     gather = Gather(ring, shard, gathered, refs) if ring else None
     step = gather.step if ring else (lambda: None)
-    greet([{"tensor": 1 - lax.axis_index("tensor")}] + (gather.neighbours() if ring else []))
+    greeted = gather.neighbours() if ring else []
+    greet([{"tensor": 1 - lax.axis_index("tensor")}] + greeted)
     load = pltpu.make_async_copy(weights, w, w_sem)
     load.start()
     step()
@@ -837,11 +899,18 @@
 
 def mlp_kernel(rows, clips, spatial, *refs):
     stream, mods, weights, *refs = refs
+    if not spatial:
+        low, *refs = refs
     stream_out, stream_low, branch_out, squares, hidden0, hidden1, pre0, pre1, act0, act1, *refs = refs
-    w, w_sem, part_out, part_in, keep, x_sems = refs
+    landed, *refs = refs
+    w, w_sem, part_out, part_in, keep, x_sems, *refs = refs
+    if spatial:
+        low, *refs = refs
+    regroup = Exchange(low, landed, refs)
+    greeted = [{"tensor": 1 - lax.axis_index("tensor")}] + regroup.others()
     pieces = Pieces(rows, clips, stream.shape[0], spatial)
     inner = act0.shape[1]
-    greet([{"tensor": 1 - lax.axis_index("tensor")}])
+    greet(greeted)
     load = pltpu.make_async_copy(weights, w, w_sem)
     load.start()
     arrivals, swaps = [], []
@@ -850,6 +919,8 @@
         value = pieces.plus(pieces.times(normed, mods, 4, i, 1.0), mods, 3, i)
         hidden0[pieces.at(i), :] = value.astype(bf16)
         arrivals.append(pieces.swap(hidden0, hidden1, x_sems, i, 0))
+    if not spatial:
+        regroup.start()
     load.wait()
     block = 768 if inner % 768 == 0 else inner
 
@@ -872,13 +943,14 @@
     keep[...] = dot_nt(act0[...], w_down)
     sublayer_end(
         pieces, stream, mods, 5, keep, part_in, swaps,
-        (stream_out, stream_low, branch_out, squares, rows, clips),
+        (stream_out, stream_low, branch_out, squares, rows, clips), regroup if spatial else None,
     )
+    regroup.finish()
     for copy in arrivals + swaps:
         copy.wait_send()
 
 
-def forward_call(layer, attends, stream, mod, weights, hidden=None, shard=None):
+def forward_call(layer, attends, stream, mod, weights, hidden=None, shard=None, ride=None):
     rows, clips, count = layer.rows, layer.clips, layer.rows * layer.tokens
     width = weights.shape[0]
     inner = weights.shape[1] // (4 if attends else 2)
@@ -908,6 +980,15 @@
         outs.append(shape((4 * ring,) + shard.shape, bf16))
         out_specs.append(anywhere)
         scratch += Gather.scratch(ring)
+    size = lax.axis_size("dp")
+    blocks = shape((size, count // size, width), bf16)
+    if ride is not None:
+        args, specs = args + [ride], specs + [vmem]
+    if not attends:
+        outs.append(blocks)
+        out_specs.append(vmem)
+        scratch += [pltpu.VMEM(blocks.shape, bf16)] if layer.spatial else []
+        scratch += Exchange.scratch(size)
     if attends:
         kernel = functools.partial(attention_kernel, rows, clips, layer.spatial, bool(hidden), ring)
     else:
@@ -932,19 +1013,26 @@
     return 0.5 * (1.0 + bend) + 0.5 * value * (1.0 - bend * bend) * root * (1.0 + 3.0 * cubic * square)
 
 
-def mlp_back_kernel(rows, clips, extra, packed, *refs):
+def mlp_back_kernel(rows, clips, extra, packed, rides, *refs):
     grad, branch, stream, mods, hidden0, hidden1, pre0, pre1, act0, act1, weights, *refs = refs
     others, refs = refs[:extra], refs[extra:]
+    if rides:
+        ride, *refs = refs
     grad_out, dmod_out, *refs = refs
     gw_outs, refs = refs[: 2 - packed], refs[2 - packed :]
     other_outs, refs = refs[:extra], refs[extra:]
+    if rides:
+        landed, *refs = refs
     w, w_sem, db0, db1, part_out, part_in, keep, dpre0, dpre1, gw, gw_sem, x_sems, *refs = refs
     inner = act0.shape[1]
     jobs = [
         Scatter(others[i], other_outs[i], refs[7 * i : 7 * i + 7], lambda j: False) for i in range(extra)
     ]
     greeted = [{"tensor": 1 - lax.axis_index("tensor")}]
-    if extra:
+    if rides:
+        exchange = Exchange(ride, landed, refs[7 * extra :])
+        greeted += exchange.others()
+    elif extra:
         greeted += jobs[0].neighbours()
     greet(greeted)
     load = pltpu.make_async_copy(weights, w, w_sem)
@@ -953,6 +1041,8 @@
         (spread(grad[...].astype(f32), rows, clips) * clip_rows(mods, clips, 5)).reshape(grad.shape).astype(bf16)
     )
     first = Swap(db0, db1, x_sems, 0)
+    if rides:
+        exchange.start()
     pipeline = Pipeline()
     pipeline.add(jobs)
     tick = pipeline.tick
@@ -1001,13 +1091,15 @@
     for k, value in enumerate((dshift, dscale, dgate)):
         dmod_out[k * clips : (k + 1) * clips] = value
     pipeline.finish()
+    if rides:
+        exchange.finish()
     for copy in stored[-2:]:
         copy.wait()
     for exchange in (first, second):
         exchange.copy.wait_send()
 
 
-def mlp_back_call(layer, grad, mod, stored, packed, others=()):
+def mlp_back_call(layer, grad, mod, stored, packed, others=(), ride=None):
     stream, branch, hidden, pre, active, weights = stored
     rows, clips, count = layer.rows, layer.clips, layer.rows * layer.tokens
     width, inner, ring = weights.shape[0], active[0].shape[1], lax.axis_size("dp") // 4
@@ -1022,6 +1114,10 @@
     gw = [shape((width, 2 * inner), bf16)] if packed else [shape((width, inner), bf16)] * 2
     outs = [shape((count, width), f32), shape((3 * clips, width), f32)] + gw
     outs += [shape((share, g.shape[-1]), f32) for g in others]
+    rides = ride is not None
+    if rides:
+        args, specs = args + [ride], specs + [vmem]
+        outs.append(shape(ride.shape, bf16))
     block = 768 if inner % 768 == 0 else inner
     scratch = [pltpu.VMEM(weights.shape, bf16), pltpu.SemaphoreType.DMA]
     scratch += [pltpu.VMEM((count, width), bf16)] * 4 + [pltpu.VMEM((count, width), f32)]
@@ -1030,10 +1126,12 @@
     scratch += [pltpu.SemaphoreType.DMA((2, 2))]
     for g in others:
         scratch += Scatter.scratch(ring, share, g.shape[-1], False)
+    if rides:
+        scratch += Exchange.scratch(4 * ring)
     return pl.pallas_call(
-        functools.partial(mlp_back_kernel, rows, clips, len(others), packed),
+        functools.partial(mlp_back_kernel, rows, clips, len(others), packed, rides),
         in_specs=specs,
-        out_specs=[vmem, vmem] + [anywhere] * len(gw) + [vmem] * len(others),
+        out_specs=[vmem, vmem] + [anywhere] * len(gw) + [vmem] * (len(others) + rides),
         out_shape=outs,
         scratch_shapes=scratch,
         cost_estimate=pl.CostEstimate(flops=1 << 35, bytes_accessed=1 << 25, transcendentals=0),
@@ -1480,7 +1578,7 @@
 
     keep = lambda value: value
     mod_s, mod_t = mods.reshape(2, clips, 6, width)
-    fused = lax.axis_size("tensor") == 2 and rows % clips == 0
+    fused = lax.axis_size("tensor") == 2 and rows % clips == 0 and tokens % (8 * dp) == 0
     if fused:
         flat = video_in.reshape(rows * tokens, width)
         mine = [spatial.flat(h) for h in hidden]
@@ -1489,14 +1587,15 @@
         )
         w_attn_t = w_attn_t.reshape(width, -1)
         kept1 = (flat, b1, mine, kept1[:2], kept1[2:])
-        s2, low2, b2, q2, *kept2 = forward_call(spatial, False, s1, mod_s, w_mlp_s)
+        s2, _, b2, q2, *kept2, placed = forward_call(spatial, False, s1, mod_s, w_mlp_s)
         kept2 = (s1, b2, kept2[:2], kept2[2:4], kept2[4:])
-        placed = to_places(spatial.full(low2), bf16).reshape(-1, width)
-        placed, grad_output = tie(placed, grad_output)
+        placed = placed.reshape(-1, width)
+        by_place = grad_output.astype(bf16).reshape(rows, dp, tokens // dp, width)
+        by_place = jnp.moveaxis(by_place, 1, 0).reshape(dp, -1, width)
         s3, _, b3, q3, *kept3 = forward_call(temporal, True, placed, mod_t, w_attn_t)
         kept3 = (placed, b3, kept3[4:], kept3[:2], kept3[2:4])
-        grad = to_places(grad_output, bf16)
-        _, low4, b4, q4, *kept4 = forward_call(temporal, False, s3, mod_t, w_mlp_t)
+        _, low4, b4, q4, *kept4, grad = forward_call(temporal, False, s3, mod_t, w_mlp_t, ride=by_place)
+        grad = grad.reshape(-1, width)
         kept4 = (s3, b4, kept4[:2], kept4[2:4], kept4[4:])
         spots = []
         for layer, values in ((spatial, (q1, q2)), (temporal, (q3, q4))):
@@ -1528,33 +1627,33 @@
         )
     by_span = lambda dmod: jnp.moveaxis(dmod.reshape(3, clips, width), 0, 1)
     if fused:
-        grad, dmod4, gw4 = mlp_back_call(temporal, grad, mod_t, (*kept4[:5], w_mlp_t), True)
+        grad, dmod4, gw4, by_frame = mlp_back_call(
+            temporal, grad, mod_t, (*kept4[:5], w_mlp_t), True, ride=low4.reshape(dp, -1, width)
+        )
+        framed = lambda blocks: jnp.moveaxis(blocks.reshape(dp, rows, -1, width), 0, 1)
+        video_out = framed(by_frame).reshape(video_in.shape)
         own4 = scatter_grads(gw4)
-        video_out = to_frames(temporal.full(low4))
-        grad, video_out = tie(grad, video_out)
-        grad, dmod3, gw3 = attention_back_call(temporal, grad, mod_t, (*kept3[:5], w_attn_t))
-        grad = temporal.full(grad)
+        dmod3, gw3, by_frame = attention_back_call(temporal, grad, mod_t, (*kept3[:5], w_attn_t))
+        grad = framed(by_frame).reshape(-1, width)
     else:
         grad, dmod4, (gw4,) = temporal.mlp_back(grad, mod_t, kept4, False, keep)
         own4 = scatter_grads(gw4)
         grad, dmod3, (gw3,) = temporal.attention_back(grad, mod_t, kept3, False, keep)
         own3 = scatter_grads(gw3)
     if fused:
-        grad, dmod2, up, down = mlp_back_call(
-            spatial, to_frames(grad), mod_s, (*kept2[:5], w_mlp_s), False
+        grad, dmod2, up, down, own3 = mlp_back_call(
+            spatial, grad, mod_s, (*kept2[:5], w_mlp_s), False, (gw3,)
         )
-        own4, gw3 = tie(own4, gw3)
-        own3 = scatter_grads(gw3)
         line = jnp.pad(squares.reshape(1, -1), ((0, 0), (0, width - squares.size)))
         small = jnp.concatenate([dmod2, dmod3, dmod4, line], axis=0)
-        grad, grad_up_s, down_s, own1, late = attention_back_call(
+        grad, grad_up_s, down_s, *own1, late, early = attention_back_call(
             spatial, grad, mod_s, (*kept1[:5], w_attn_s), (up, down), small
         )
         grad = spatial.full(grad)
-        dmod1, dmod2, dmod3, dmod4 = [
-            by_span(late[3 * clips * i : 3 * clips * (i + 1)]) for i in range(4)
-        ]
-        squares = late[12 * clips, : squares.size].reshape(8, FRAMES)
+        own1 = jnp.concatenate(own1, axis=1)
+        dmod1 = by_span(late)
+        dmod2, dmod3, dmod4 = [by_span(early[3 * clips * i : 3 * clips * (i + 1)]) for i in range(3)]
+        squares = early[9 * clips, : squares.size].reshape(8, FRAMES)
     else:
         early = AllSum(
             jnp.concatenate([dmod3.reshape(-1), dmod4.reshape(-1), squares.reshape(-1)]).reshape(-1, 128)

time: 681 us -> 667 us (0.979)
  Pallas kernels: 528 us -> 602 us
  blocking collectives: 55.9 us -> 0 us
  waiting for transfers between devices: 17.3 us -> 0.09 us
  starting transfers between devices: 8.27 us -> 0.12 us
    pallas_call x2, Pallas kernels: 74 us -> 135 us  [mlp_back_call(): pl.pallas_call(functools.partial(mlp_back_kernel, rows, clips, len(others...]
    all_to_all x2 -> x0, blocking collectives: 55.9 us -> none  [the longest x1 34.6 us: to_places(): lax.all_to_all(stream.astype(bf16), 'dp', split_axis=1, concat_axis=0, ti...]
    pallas_call x4, Pallas kernels: 177 us -> 210 us  [forward_call(): pl.pallas_call(kernel, in_specs=specs, out_specs=out_specs, out_shape=out...]
    pallas_call x2, Pallas kernels: 210 us -> 191 us  [attention_back_call(): pl.pallas_call(functools.partial(attention_back_kernel, rows, clips, laye...]
    all_to_all x2 -> x0, waiting for transfers between devices: 17.1 us -> none  [the longest x1 17.1 us: to_frames(): lax.all_to_all(stream.astype(bf16), 'dp', split_axis=0, concat_axis=1, ti...]
    all_to_all x2 -> x0, starting transfers between devices: 7.9 us -> none  [the longest x1 4.31 us: to_places(): lax.all_to_all(stream.astype(bf16), 'dp', split_axis=1, concat_axis=0, ti...]
  transfers between devices with their start and end apart: 6 -> 3, of which waited for: 1 -> 0; matrix products, arithmetic and copies ran while one was open for 4% -> 4% of each run, Pallas kernels for 74% -> 78%
where the time goes in v5:
time: 667 us; the launch traced here: 657 us
  Pallas kernels  602 us (90%)
  local copies, waits for them, and re-layouts  25.8 us (4%)
  between operations  14.5 us (2%)
  other arithmetic  11 us (2%)
    pallas_call x4, Pallas kernels, forward_call(): pl.pallas_call(kernel, in_specs=specs, out_specs=out_specs, out_shape=out...  210 us
    pallas_call x2, Pallas kernels, attention_back_call(): pl.pallas_call(functools.partial(attention_back_kernel, rows, clips, laye...  191 us
    pallas_call x2, Pallas kernels, mlp_back_call(): pl.pallas_call(functools.partial(mlp_back_kernel, rows, clips, len(others...  135 us
    pallas_call x1, Pallas kernels, head(): pl.pallas_call(functools.partial(head_kernel, ring, clips, pairs), in_spe...  66.8 us
  transfers between devices with their start and end apart: 3, of which 0 were waited for; matrix products, arithmetic and copies ran while one was open for 4% of the time, Pallas kernels for 78%

profile of v5, /device:TPU:0, one launch (start us, length us, event | category | flops | bytes accessed | tf_op | source)
XLA Modules:
  0.0 656.9 jit_solution(1842316802289013883)
XLA Ops:
  7.2 2.0 pad_maximum_fusion
  9.4 0.9 pad_maximum_fusion.1
  11.6 1.4 fusion.3
  14.8 0.8 pad_maximum_fusion.3.refs_5_
  15.6 66.8 %shard_map.244 = (bf16[16,72,2304]{2,1,0:T(8,128)(2,1)S(1)}, f32[24,1152]{1,0:T(8,128)S(1)}, bf16[2,128,1152]{2,1,0:T(8,128)(2,1)S(1)}, bf16[2,128,1152]{2,1,0:T(8,128)(2,1)S(1)}) custom-call(bf16[72,2304]{1,0:T(8,128)(2,1)S(1)} %pad_maximum_fusion.2.shard, f32[24,1152]{1,0:T(8,128)S(1)} %reshape.147.small, bf16[2,128,1152]{2,1,0:T(8,128)(2,1)S(1)} %copy-done), custom_call_target="tpu_custom_call" | custom-call | flops 34359738368 | bytes 5308416 | tf_op jit(solution)/shard_map/pallas_call | solution.py:1437
  82.5 2.4 copy-done.1
  87.2 0.9 copy_bitcast_fusion.3.refs_3_
  88.1 67.8 %shard_map.245 = (f32[256,1152]{1,0:T(8,128)}, bf16[256,1152]{1,0:T(8,128)(2,1)}, f32[256,1152]{1,0:T(8,128)}, f32[2,1,128]{2,1,0:T(1,128)}, bf16[256,1728]{1,0:...) custom-call(bf16[256,1152]{1,0:T(8,128)(2,1)} %bitcast.92, ...), custom_call_target="tpu_custom_call" | custom-call | flops 34359738368 | bytes 33554432 | tf_op jit(solution)/shard_map/pallas_call | solution.py:996
  155.9 55.4 %shard_map.246 = (f32[256,1152]{1,0:T(8,128)}, bf16[256,1152]{1,0:T(8,128)(2,1)}, f32[256,1152]{1,0:T(8,128)}, f32[2,1,128]{2,1,0:T(1,128)}, bf16[256,1152]{1,0:...) custom-call(f32[256,1152]{1,0:T(8,128)} %get-tuple-element.80.refs_0, ...), custom_call_target="tpu_custom_call" | custom-call | flops 34359738368 | bytes 33554432 | tf_op jit(solution)/shard_map/pallas_call | solution.py:996
  211.3 37.1 %shard_map.247 = (f32[256,1152]{1,0:T(8,128)}, bf16[256,1152]{1,0:T(8,128)(2,1)}, f32[256,1152]{1,0:T(8,128)}, f32[2,16,128]{2,1,0:T(8,128)}, bf16[256,1728]{1,0...) custom-call(bf16[256,1152]{1,0:T(8,128)(2,1)} %bitcast.142, ...), custom_call_target="tpu_custom_call" | custom-call | flops 34359738368 | bytes 33554432 | tf_op jit(solution)/shard_map/pallas_call | solution.py:996
  248.4 49.3 %shard_map.248 = (f32[256,1152]{1,0:T(8,128)}, bf16[256,1152]{1,0:T(8,128)(2,1)}, f32[256,1152]{1,0:T(8,128)}, f32[2,16,128]{2,1,0:T(8,128)}, bf16[256,1152]{1,0...) custom-call(f32[256,1152]{1,0:T(8,128)} %get-tuple-element.83.refs_0, ...), custom_call_target="tpu_custom_call" | custom-call | flops 34359738368 | bytes 33554432 | tf_op jit(solution)/shard_map/pallas_call | solution.py:996
  297.7 42.0 %shard_map.249 = (f32[256,1152]{1,0:T(8,128)}, f32[6,1152]{1,0:T(8,128)}, bf16[1152,4608]{1,0:T(8,128)(2,1)}, bf16[16,16,1152]{2,1,0:T(8,128)(2,1)}) custom-call(bf16[256,1152]{1,0:T(8,128)(2,1)} %bitcast.145, f32[256,1152]{1,0:T(8,128)} %get-tuple-element.85.refs_1_, f32[256,1152]{1,0:T(8,128)} %get-tuple-element.83.refs_0_.refs_2_, ...), custom_call_target="tpu_custom_call" | custom-call | flops 34359738368 | bytes 33554432 | tf_op jit(solution)/shard_map/pallas_call | solution.py:1131
  340.9 65.2 %shard_map.250 = (f32[6,1152]{1,0:T(8,128)}, bf16[1152,2304]{1,0:T(8,128)(2,1)}, bf16[16,16,1152]{2,1,0:T(8,128)(2,1)}) custom-call(f32[256,1152]{1,0:T(8,128)} %get-tuple-element.94.refs_0_, f32[256,1152]{1,0:T(8,128)} %get-tuple-element.95.refs_1_, bf16[256,1152]{1,0:T(8,128)(2,1)} %bitcast.143, f32[12,1152]{1,0:T(8,128)} %get-tuple-element.193.refs_1_.refs_3_, ...), custom_call_target="tpu_custom_call" | custom-call | flops 34359738368 | bytes 33554432 | tf_op jit(solution)/shard_map/pallas_call | solution.py:676
  406.0 1.9 copy.56
  407.9 92.6 %shard_map.251 = (f32[256,1152]{1,0:T(8,128)}, f32[6,1152]{1,0:T(8,128)}, bf16[1152,2304]{1,0:T(8,128)(2,1)}, bf16[1152,2304]{1,0:T(8,128)(2,1)}, f32[72,2304]{1,0:T(8,128)}) custom-call(bf16[256,1152]{1,0:T(8,128)(2,1)} %bitcast.110, f32[256,1152]{1,0:T(8,128)} %get-tuple-element.103.refs_1_, f32[256,1152]{1,0:T(8,128)} %get-tuple-element.80.refs_0_.refs_2_, ...), custom_call_target="tpu_custom_call" | custom-call | flops 34359738368 | bytes 33554432 | tf_op jit(solution)/shard_map/pallas_call | solution.py:1131
  500.6 1.4 select_maximum_fusion.refs_13_
  502.1 125.6 %shard_map.252 = (f32[256,1152]{1,0:T(8,128)}, f32[72,2304]{1,0:T(8,128)}, f32[72,2304]{1,0:T(8,128)}, f32[72,576]{1,0:T(8,128)}, f32[72,576]{1,0:T(8,128)}, /*i...) custom-call(f32[256,1152]{1,0:T(8,128)} %get-tuple-element.111.refs_0_, ...), custom_call_target="tpu_custom_call" | custom-call | flops 34359738368 | bytes 33554432 | tf_op jit(solution)/shard_map/pallas_call | solution.py:676
  627.7 1.0 fusion.4
  629.5 1.2 concatenate.35
  631.1 0.8 copy.60
  632.8 1.4 copy.71
  634.2 1.4 copy.72
  637.3 0.8 copy.62
  638.2 0.9 convolution_bitcast_fusion.3
  640.6 2.2 fusion.2
  642.8 0.9 copy_bitcast_fusion.2
  643.6 1.3 convert_element_type.19
  644.9 0.9 slice_bitcast_fusion
  645.8 0.9 slice.112
  646.7 1.0 copy.79
  648.5 0.8 copy.81
  649.3 0.8 copy.82
  (106 shorter events, 12.5 us)
Async XLA Ops:
  7.2 2.2 copy-start.15
  7.2 2.2 copy-start.16
  7.2 148.6 %all-gather.3.cloned.1.call-start = ((), (), s32[]{:S(2)}) async-start(), calls=%async_computation.1 | async-start | bytes 11280384 | tf_op jit(solution)/shard_map/all_gather | solution.py:1326
  9.3 1.4 copy-start.6
  9.3 239.1 %all-gather.5.cloned.1.call-start = ((), (), s32[]{:S(2)}) async-start(), calls=%async_computation.2 | async-start | bytes 11280384 | tf_op jit(solution)/shard_map/all_gather | solution.py:1326
  10.2 1.3 copy-start.4
  10.3 633.4 %reduce-scatter.2.cloned.1.call-start = ((), (), s32[]{:S(2)}) async-start(), calls=%async_computation.3 | async-start | bytes 11280384 | tf_op jit(solution)/shard_map/reduce_scatter | solution.py:1532
  11.6 2.1 copy-start.17
  13.3 1.0 copy-start.18
  13.7 0.9 copy-start.20
  13.9 0.9 copy-start.21
  14.2 1.4 copy-start
  15.6 71.5 %copy-start.9 = (f32[2,128,1152]{2,1,0:T(8,128)S(1)}, f32[2,128,1152]{2,1,0:T(8,128)}, u32[]{:S(2)}) copy-start(f32[2,128,1152]{2,1,0:T(8,128)} %param.25) | copy-start | bytes 3538948
  82.5 2.4 copy-start.1
  84.9 0.8 copy-start.2
  85.7 0.8 copy-start.3
  339.7 0.7 copy-start.27
  339.7 0.7 copy-start.28
  339.7 0.8 copy-start.25
  339.7 0.9 copy-start.24
  407.9 92.7 %copy-start.22 = (f32[6,1152]{1,0:T(8,128)S(1)}, f32[6,1152]{1,0:T(8,128)}, u32[]{:S(2)}) copy-start(f32[6,1152]{1,0:T(8,128)} %get-tuple-element.121) | copy-start | bytes 82948
  407.9 92.7 %copy-start.23 = (f32[6,1152]{1,0:T(8,128)S(1)}, f32[6,1152]{1,0:T(8,128)}, u32[]{:S(2)}) copy-start(f32[6,1152]{1,0:T(8,128)} %get-tuple-element.120) | copy-start | bytes 82948
  630.8 1.2 copy-start.26
  634.2 2.8 copy-start.11
  637.0 1.2 copy-start.5
  637.3 3.3 copy-start.7
  638.2 4.6 copy-start.14
  643.6 2.2 copy-start.8
  644.9 1.8 copy-start.10
  646.7 1.1 copy-start.19
  646.7 1.8 copy-start.13
  647.8 1.5 copy-start.12
Sparse Core Ops, SparseCore 0:
  10.9 129.2 all-gather.2
  143.1 97.0 all-gather.4
  339.9 158.4 reduce-scatter.1

commit v6 on v5

--- a/solution.py
+++ b/solution.py
@@ -1026,7 +1026,7 @@
     w, w_sem, db0, db1, part_out, part_in, keep, dpre0, dpre1, gw, gw_sem, x_sems, *refs = refs
     inner = act0.shape[1]
     jobs = [
-        Scatter(others[i], other_outs[i], refs[7 * i : 7 * i + 7], lambda j: False) for i in range(extra)
+        Scatter(others[i], other_outs[i], refs[7 * i : 7 * i + 7], lambda j: j % 6 == 5) for i in range(extra)
     ]
     greeted = [{"tensor": 1 - lax.axis_index("tensor")}]
     if rides:
@@ -1125,7 +1125,7 @@
     scratch += [pltpu.VMEM((2, width, block), bf16), pltpu.SemaphoreType.DMA((2,))]
     scratch += [pltpu.SemaphoreType.DMA((2, 2))]
     for g in others:
-        scratch += Scatter.scratch(ring, share, g.shape[-1], False)
+        scratch += Scatter.scratch(ring, share, g.shape[-1])
     if rides:
         scratch += Exchange.scratch(4 * ring)
     return pl.pallas_call(

time: 667 us -> 670 us (level)
  no operation moved by 1% of the time
where the time goes in v6:
time: 670 us; the launch traced here: 657 us
  Pallas kernels  602 us (90%)
  local copies, waits for them, and re-layouts  25.8 us (4%)
  between operations  14.5 us (2%)
  other arithmetic  11 us (2%)
    pallas_call x4, Pallas kernels, forward_call(): pl.pallas_call(kernel, in_specs=specs, out_specs=out_specs, out_shape=out...  210 us
    pallas_call x2, Pallas kernels, attention_back_call(): pl.pallas_call(functools.partial(attention_back_kernel, rows, clips, laye...  189 us
    pallas_call x2, Pallas kernels, mlp_back_call(): pl.pallas_call(functools.partial(mlp_back_kernel, rows, clips, len(others...  136 us
    pallas_call x1, Pallas kernels, head(): pl.pallas_call(functools.partial(head_kernel, ring, clips, pairs), in_spe...  66.8 us
  transfers between devices with their start and end apart: 3, of which 0 were waited for; matrix products, arithmetic and copies ran while one was open for 4% of the time, Pallas kernels for 78%

profile of v6, /device:TPU:0, one launch (start us, length us, event | category | flops | bytes accessed | tf_op | source)
XLA Modules:
  0.0 657.2 jit_solution(3900541173426250024)
XLA Ops:
  7.2 2.0 pad_maximum_fusion
  9.4 0.9 pad_maximum_fusion.1
  11.6 1.4 fusion.3
  14.8 0.8 pad_maximum_fusion.3.refs_5_
  15.6 66.8 %shard_map.244 = (bf16[16,72,2304]{2,1,0:T(8,128)(2,1)S(1)}, f32[24,1152]{1,0:T(8,128)S(1)}, bf16[2,128,1152]{2,1,0:T(8,128)(2,1)S(1)}, bf16[2,128,1152]{2,1,0:T(8,128)(2,1)S(1)}) custom-call(bf16[72,2304]{1,0:T(8,128)(2,1)S(1)} %pad_maximum_fusion.2.shard, f32[24,1152]{1,0:T(8,128)S(1)} %reshape.147.small, bf16[2,128,1152]{2,1,0:T(8,128)(2,1)S(1)} %copy-done), custom_call_target="tpu_custom_call" | custom-call | flops 34359738368 | bytes 5308416 | tf_op jit(solution)/shard_map/pallas_call | solution.py:1437
  82.5 2.4 copy-done.1
  87.2 0.9 copy_bitcast_fusion.3.refs_3_
  88.1 67.8 %shard_map.245 = (f32[256,1152]{1,0:T(8,128)}, bf16[256,1152]{1,0:T(8,128)(2,1)}, f32[256,1152]{1,0:T(8,128)}, f32[2,1,128]{2,1,0:T(1,128)}, bf16[256,1728]{1,0:...) custom-call(bf16[256,1152]{1,0:T(8,128)(2,1)} %bitcast.92, ...), custom_call_target="tpu_custom_call" | custom-call | flops 34359738368 | bytes 33554432 | tf_op jit(solution)/shard_map/pallas_call | solution.py:996
  155.9 55.4 %shard_map.246 = (f32[256,1152]{1,0:T(8,128)}, bf16[256,1152]{1,0:T(8,128)(2,1)}, f32[256,1152]{1,0:T(8,128)}, f32[2,1,128]{2,1,0:T(1,128)}, bf16[256,1152]{1,0:...) custom-call(f32[256,1152]{1,0:T(8,128)} %get-tuple-element.80.refs_0, ...), custom_call_target="tpu_custom_call" | custom-call | flops 34359738368 | bytes 33554432 | tf_op jit(solution)/shard_map/pallas_call | solution.py:996
  211.3 37.1 %shard_map.247 = (f32[256,1152]{1,0:T(8,128)}, bf16[256,1152]{1,0:T(8,128)(2,1)}, f32[256,1152]{1,0:T(8,128)}, f32[2,16,128]{2,1,0:T(8,128)}, bf16[256,1728]{1,0...) custom-call(bf16[256,1152]{1,0:T(8,128)(2,1)} %bitcast.142, ...), custom_call_target="tpu_custom_call" | custom-call | flops 34359738368 | bytes 33554432 | tf_op jit(solution)/shard_map/pallas_call | solution.py:996
  248.4 49.3 %shard_map.248 = (f32[256,1152]{1,0:T(8,128)}, bf16[256,1152]{1,0:T(8,128)(2,1)}, f32[256,1152]{1,0:T(8,128)}, f32[2,16,128]{2,1,0:T(8,128)}, bf16[256,1152]{1,0...) custom-call(f32[256,1152]{1,0:T(8,128)} %get-tuple-element.83.refs_0, ...), custom_call_target="tpu_custom_call" | custom-call | flops 34359738368 | bytes 33554432 | tf_op jit(solution)/shard_map/pallas_call | solution.py:996
  297.7 42.0 %shard_map.249 = (f32[256,1152]{1,0:T(8,128)}, f32[6,1152]{1,0:T(8,128)}, bf16[1152,4608]{1,0:T(8,128)(2,1)}, bf16[16,16,1152]{2,1,0:T(8,128)(2,1)}) custom-call(bf16[256,1152]{1,0:T(8,128)(2,1)} %bitcast.145, f32[256,1152]{1,0:T(8,128)} %get-tuple-element.85.refs_1_, f32[256,1152]{1,0:T(8,128)} %get-tuple-element.83.refs_0_.refs_2_, ...), custom_call_target="tpu_custom_call" | custom-call | flops 34359738368 | bytes 33554432 | tf_op jit(solution)/shard_map/pallas_call | solution.py:1131
  340.9 65.2 %shard_map.250 = (f32[6,1152]{1,0:T(8,128)}, bf16[1152,2304]{1,0:T(8,128)(2,1)}, bf16[16,16,1152]{2,1,0:T(8,128)(2,1)}) custom-call(f32[256,1152]{1,0:T(8,128)} %get-tuple-element.94.refs_0_, f32[256,1152]{1,0:T(8,128)} %get-tuple-element.95.refs_1_, bf16[256,1152]{1,0:T(8,128)(2,1)} %bitcast.143, f32[12,1152]{1,0:T(8,128)} %get-tuple-element.193.refs_1_.refs_3_, ...), custom_call_target="tpu_custom_call" | custom-call | flops 34359738368 | bytes 33554432 | tf_op jit(solution)/shard_map/pallas_call | solution.py:676
  406.0 1.9 copy.56
  407.9 94.4 %shard_map.251 = (f32[256,1152]{1,0:T(8,128)}, f32[6,1152]{1,0:T(8,128)}, bf16[1152,2304]{1,0:T(8,128)(2,1)}, bf16[1152,2304]{1,0:T(8,128)(2,1)}, f32[72,2304]{1,0:T(8,128)}) custom-call(bf16[256,1152]{1,0:T(8,128)(2,1)} %bitcast.110, f32[256,1152]{1,0:T(8,128)} %get-tuple-element.103.refs_1_, f32[256,1152]{1,0:T(8,128)} %get-tuple-element.80.refs_0_.refs_2_, ...), custom_call_target="tpu_custom_call" | custom-call | flops 34359738368 | bytes 33554432 | tf_op jit(solution)/shard_map/pallas_call | solution.py:1131
  502.4 1.4 select_maximum_fusion.refs_13_
  503.8 124.1 %shard_map.252 = (f32[256,1152]{1,0:T(8,128)}, f32[72,2304]{1,0:T(8,128)}, f32[72,2304]{1,0:T(8,128)}, f32[72,576]{1,0:T(8,128)}, f32[72,576]{1,0:T(8,128)}, /*i...) custom-call(f32[256,1152]{1,0:T(8,128)} %get-tuple-element.111.refs_0_, ...), custom_call_target="tpu_custom_call" | custom-call | flops 34359738368 | bytes 33554432 | tf_op jit(solution)/shard_map/pallas_call | solution.py:676
  628.0 1.0 fusion.4
  629.8 1.2 concatenate.35
  631.3 0.8 copy.60
  633.0 1.4 copy.71
  634.5 1.4 copy.72
  637.6 0.8 copy.62
  638.5 0.9 convolution_bitcast_fusion.3
  640.9 2.2 fusion.2
  643.0 0.9 copy_bitcast_fusion.2
  643.9 1.3 convert_element_type.19
  645.2 0.9 slice_bitcast_fusion
  646.1 0.9 slice.112
  647.0 1.0 copy.79
  648.7 0.8 copy.81
  649.6 0.8 copy.82
  (106 shorter events, 12.5 us)
Async XLA Ops:
  7.2 2.2 copy-start.15
  7.2 2.2 copy-start.16
  7.2 148.6 %all-gather.3.cloned.1.call-start = ((), (), s32[]{:S(2)}) async-start(), calls=%async_computation.1 | async-start | bytes 11280384 | tf_op jit(solution)/shard_map/all_gather | solution.py:1326
  9.3 1.4 copy-start.6
  9.3 239.1 %all-gather.5.cloned.1.call-start = ((), (), s32[]{:S(2)}) async-start(), calls=%async_computation.2 | async-start | bytes 11280384 | tf_op jit(solution)/shard_map/all_gather | solution.py:1326
  10.2 1.3 copy-start.4
  10.3 633.6 %reduce-scatter.2.cloned.1.call-start = ((), (), s32[]{:S(2)}) async-start(), calls=%async_computation.3 | async-start | bytes 11280384 | tf_op jit(solution)/shard_map/reduce_scatter | solution.py:1532
  11.6 2.1 copy-start.17
  13.3 1.0 copy-start.18
  13.7 0.9 copy-start.20
  13.9 0.9 copy-start.21
  14.2 1.4 copy-start
  15.6 71.5 %copy-start.9 = (f32[2,128,1152]{2,1,0:T(8,128)S(1)}, f32[2,128,1152]{2,1,0:T(8,128)}, u32[]{:S(2)}) copy-start(f32[2,128,1152]{2,1,0:T(8,128)} %param.25) | copy-start | bytes 3538948
  82.5 2.4 copy-start.1
  84.9 0.8 copy-start.2
  85.7 0.8 copy-start.3
  339.7 0.7 copy-start.27
  339.7 0.7 copy-start.28
  339.7 0.8 copy-start.25
  339.7 0.9 copy-start.24
  407.9 94.4 %copy-start.22 = (f32[6,1152]{1,0:T(8,128)S(1)}, f32[6,1152]{1,0:T(8,128)}, u32[]{:S(2)}) copy-start(f32[6,1152]{1,0:T(8,128)} %get-tuple-element.121) | copy-start | bytes 82948
  407.9 94.4 %copy-start.23 = (f32[6,1152]{1,0:T(8,128)S(1)}, f32[6,1152]{1,0:T(8,128)}, u32[]{:S(2)}) copy-start(f32[6,1152]{1,0:T(8,128)} %get-tuple-element.120) | copy-start | bytes 82948
  631.0 1.2 copy-start.26
  634.4 2.8 copy-start.11
  637.3 1.2 copy-start.5
  637.6 3.3 copy-start.7
  638.5 4.6 copy-start.14
  643.9 2.2 copy-start.8
  645.2 1.8 copy-start.10
  647.0 1.1 copy-start.19
  647.0 1.8 copy-start.13
  648.1 1.5 copy-start.12
Sparse Core Ops, SparseCore 0:
  10.9 129.2 all-gather.2
  143.1 97.0 all-gather.4
  339.9 162.8 reduce-scatter.1
